TPU v7x, 32 devices: a whole 2x2x4 slice. The times are simulated.
32 devices in a mesh: ulysses: 4 (over y, x), blk: 8 (over z, core).
Axes of the slice: x: 2, y: 2, z: 4, core: 2. Of those that a mesh axis runs over, the one named last changes fastest.
Arguments:
- inputs: bfloat16 [2, 2048, 1024], P(None, ('blk', 'ulysses')), may hold values from -16 to 16
- v_first: bfloat16 [2, 2048, 1024], P(None, ('blk', 'ulysses')), may hold values from -6 to 6
- grad_out: bfloat16 [2, 2048, 1024], P(None, ('blk', 'ulysses')), may hold values from -6 to 6
- positions: int32 [2, 2048], P(None, ('blk', 'ulysses')), may hold values from 0 to 2047, as said below
- segments: int32 [2, 2048], replicated, may hold values from 0 to 1, as said below
- w_query: bfloat16 [1024, 1024], P(('ulysses', 'blk')), may hold values from -0.1875 to 0.1875
- w_key: bfloat16 [1024, 1024], P(('ulysses', 'blk')), may hold values from -0.1875 to 0.1875
- w_value: bfloat16 [1024, 1024], P(('ulysses', 'blk')), may hold values from -0.1875 to 0.1875
- w_out: bfloat16 [1024, 1024], P(('ulysses', 'blk')), may hold values from -1.5 to 1.5
- w_gate: bfloat16 [1024, 2816], P(('ulysses', 'blk')), may hold values from -0.1875 to 0.1875
- w_up: bfloat16 [1024, 2816], P(('ulysses', 'blk')), may hold values from -0.1875 to 0.1875
- w_down: bfloat16 [2816, 1024], P(('ulysses', 'blk')), may hold values from -0.109375 to 0.109375
- gain_attn: bfloat16 [1024], P(('ulysses', 'blk')), may hold values from 0.5 to 1.5
- gain_ffn: bfloat16 [1024], P(('ulysses', 'blk')), may hold values from 0.5 to 1.5
Outputs:
- output: bfloat16 [2, 2048, 1024], P(None, ('blk', 'ulysses'))
- grad_inputs: bfloat16 [2, 2048, 1024], P(None, ('blk', 'ulysses'))
- grad_v_first: bfloat16 [2, 2048, 1024], P(None, ('blk', 'ulysses'))
- grad_w_query: float32 [1024, 1024], P(('ulysses', 'blk'))
- grad_w_key: float32 [1024, 1024], P(('ulysses', 'blk'))
- grad_w_value: float32 [1024, 1024], P(('ulysses', 'blk'))
- grad_w_out: float32 [1024, 1024], P(('ulysses', 'blk'))
- grad_w_gate: float32 [1024, 2816], P(('ulysses', 'blk'))
- grad_w_up: float32 [1024, 2816], P(('ulysses', 'blk'))
- grad_w_down: float32 [2816, 1024], P(('ulysses', 'blk'))
- grad_gain_attn: float32 [1024], P(('ulysses', 'blk'))
- grad_gain_ffn: float32 [1024], P(('ulysses', 'blk'))
- stats: float32 [3], replicated
Inputs may be any that keep to these rules, and one draw needn't show every extreme that they name: `segments`: each sequence holds one document of 2048 tokens or two, the second starting between 512 and 1536; some sequence holds one. `positions`: the token's distance from the first token of its document.
All inputs are finite; a program needn't handle non-finite values.
Results may differ from a plain program's by a relative error of at most 0.017.
Values may be sent and summed in bfloat16 or wider, within the bound.
A program may use at most 192 MiB of HBM per device.

v0:
```python
import jax
import jax.numpy as jnp
from jax import lax
from jax.sharding import PartitionSpec as P

HEADS = 16
HD = 64


epsilon = 1e-06
rope_base = 10000.0
neg_big = -1e30


def norm_rows(values, gain):
    factor = lax.rsqrt(jnp.mean(values * values, axis=-1, keepdims=True) + epsilon)
    hatted = values * factor
    return (hatted * gain, hatted, factor)


def norm_back(grad_normed, hatted, factor, gain):
    scaled = grad_normed * gain
    inner = jnp.mean(scaled * hatted, axis=-1, keepdims=True)
    return (factor * (scaled - hatted * inner), jnp.sum(grad_normed * hatted, axis=(0, 1)))


def rope_tables(positions):
    half_dim = HD // 2
    inverse = rope_base ** (-2.0 * jnp.arange(half_dim, dtype=jnp.float32) / HD)
    angles = positions.astype(jnp.float32)[:, :, None] * inverse
    return (jnp.cos(angles)[:, :, None, :], jnp.sin(angles)[:, :, None, :])


def rotate(values, cosine, sine, forward_turn):
    shaped = values.reshape(values.shape[0], values.shape[1], HEADS, HD)
    half_dim = HD // 2
    first = shaped[..., :half_dim]
    second = shaped[..., half_dim:]
    if forward_turn:
        turned = jnp.concatenate(
            [first * cosine - second * sine, second * cosine + first * sine], axis=-1
        )
    else:
        turned = jnp.concatenate(
            [first * cosine + second * sine, second * cosine - first * sine], axis=-1
        )
    return turned.reshape(values.shape)


def project(activations, weight):
    return jnp.einsum("std,de->ste", activations, weight, preferred_element_type=jnp.float32)


def project_back(gradient, weight):
    return jnp.einsum("ste,de->std", gradient, weight, preferred_element_type=jnp.float32)


def weight_grad(activations, gradient):
    return jnp.einsum("std,ste->de", activations, gradient, preferred_element_type=jnp.float32)


def allowed_mask(segments, query_first, query_count, key_first, key_count):
    seg_query = lax.dynamic_slice_in_dim(segments, query_first, query_count, 1)
    seg_key = lax.dynamic_slice_in_dim(segments, key_first, key_count, 1)
    query_place = query_first + jnp.arange(query_count, dtype=jnp.int32)
    key_place = key_first + jnp.arange(key_count, dtype=jnp.int32)
    causal = key_place[None, :] <= query_place[:, None]
    same_doc = seg_query[:, :, None] == seg_key[:, None, :]
    return (causal[None] & same_doc)[:, :, None, :]


def over_blocks(step_fn, running, pieces, block_rows):
    row_count = pieces[0].shape[1]
    block_count = row_count // block_rows
    stacked = tuple(
        (
            jnp.moveaxis(
                member.reshape((member.shape[0], block_count, block_rows) + member.shape[2:]), 1, 0
            )
            for member in pieces
        )
    )
    offsets = block_rows * jnp.arange(block_count, dtype=jnp.int32)

    def advance(current, scan_entry):
        return (step_fn(current, scan_entry[:-1], scan_entry[-1]), None)

    running, unused = lax.scan(advance, running, stacked + (offsets,))
    return running


def add_rows(buffer, update, first_row):
    current = lax.dynamic_slice_in_dim(buffer, first_row, update.shape[1], 1)
    return lax.dynamic_update_slice_in_dim(buffer, current + update, first_row, 1)


def unchanged(running):
    return running


def local(
    inputs,
    v_first,
    grad_out,
    positions,
    segments,
    w_query,
    w_key,
    w_value,
    w_out,
    w_gate,
    w_up,
    w_down,
    gain_attn,
    gain_ffn,
):
    gathered = (
        lax.all_gather(w_query, ("ulysses", "blk"), axis=0, tiled=True),
        lax.all_gather(w_key, ("ulysses", "blk"), axis=0, tiled=True),
        lax.all_gather(w_value, ("ulysses", "blk"), axis=0, tiled=True),
        lax.all_gather(w_out, ("ulysses", "blk"), axis=0, tiled=True),
        lax.all_gather(w_gate, ("ulysses", "blk"), axis=0, tiled=True),
        lax.all_gather(w_up, ("ulysses", "blk"), axis=0, tiled=True),
        lax.all_gather(w_down, ("ulysses", "blk"), axis=0, tiled=True),
        lax.all_gather(gain_attn, ("ulysses", "blk"), axis=0, tiled=True),
        lax.all_gather(gain_ffn, ("ulysses", "blk"), axis=0, tiled=True),
    )
    (
        full_query,
        full_key,
        full_value,
        full_out,
        full_gate,
        full_up,
        full_down,
        full_gain_attn,
        full_gain_ffn,
    ) = gathered
    score_scale = HD ** (-0.5)
    residual = inputs.astype(jnp.float32)
    normed_f, hatted_attn, factor_attn = norm_rows(residual, full_gain_attn.astype(jnp.float32))
    normed = normed_f.astype(jnp.bfloat16)
    cosine, sine = rope_tables(positions)
    query_tok = rotate(project(normed, full_query), cosine, sine, True).astype(jnp.bfloat16)
    key_tok = rotate(project(normed, full_key), cosine, sine, True).astype(jnp.bfloat16)
    value_tok = (0.5 * project(normed, full_value) + 0.5 * v_first.astype(jnp.float32)).astype(
        jnp.bfloat16
    )
    query_head, key_head, value_head = (
        lax.all_to_all(query_tok, "ulysses", split_axis=2, concat_axis=1, tiled=True),
        lax.all_to_all(key_tok, "ulysses", split_axis=2, concat_axis=1, tiled=True),
        lax.all_to_all(value_tok, "ulysses", split_axis=2, concat_axis=1, tiled=True),
    )
    seq_count, block_rows, width = query_head.shape
    heads_local = width // HD
    query_start = lax.axis_index("blk") * block_rows
    full_rows = block_rows * lax.axis_size("blk")

    def split_heads(values):
        return values.reshape(values.shape[0], values.shape[1], heads_local, HD)

    query_four = split_heads(query_head)

    def attend_rows(running, pieces, first_row):
        key_rows, value_rows = pieces
        key_count = key_rows.shape[1]

        def attend_compute(current):
            best, total, accum = current
            allowed = allowed_mask(segments, query_start, block_rows, first_row, key_count)
            scores = (
                jnp.einsum(
                    "sqhd,skhd->sqhk",
                    query_four,
                    split_heads(key_rows),
                    preferred_element_type=jnp.float32,
                )
                * score_scale
            )
            masked = jnp.where(allowed, scores, neg_big)
            new_best = jnp.maximum(best, jnp.max(masked, axis=-1))
            weights = jnp.where(allowed, jnp.exp(masked - new_best[..., None]), 0.0)
            rescale = jnp.exp(best - new_best)
            total = total * rescale + jnp.sum(weights, axis=-1)
            accum = accum * rescale[..., None] + jnp.einsum(
                "sqhk,skhd->sqhd",
                weights.astype(jnp.bfloat16),
                split_heads(value_rows),
                preferred_element_type=jnp.float32,
            )
            return (new_best, total, accum)

        return lax.cond(
            first_row <= query_start + block_rows - 1, attend_compute, unchanged, running
        )

    stat_zeros = jnp.zeros((seq_count, block_rows, heads_local), jnp.float32)
    head_zeros = jnp.zeros((seq_count, block_rows, heads_local, HD), jnp.float32)
    initial = (
        jnp.full((seq_count, block_rows, heads_local), neg_big, jnp.float32),
        stat_zeros,
        head_zeros,
    )
    best, total, accum = over_blocks(
        attend_rows,
        initial,
        (
            lax.all_gather(key_head, "blk", axis=1, tiled=True),
            lax.all_gather(value_head, "blk", axis=1, tiled=True),
        ),
        block_rows,
    )
    log_total = best + jnp.log(total)
    attn_heads = accum / total[..., None]
    attn_low = attn_heads.reshape(seq_count, block_rows, width).astype(jnp.bfloat16)
    mixed = lax.all_to_all(attn_low, "ulysses", split_axis=1, concat_axis=2, tiled=True)
    attn_branch = project(mixed, full_out)
    hidden = residual + attn_branch
    normed_ffn_f, hatted_ffn, factor_ffn = norm_rows(hidden, full_gain_ffn.astype(jnp.float32))
    normed_ffn = normed_ffn_f.astype(jnp.bfloat16)
    gate = project(normed_ffn, full_gate)
    up_proj = project(normed_ffn, full_up)
    sigmoid_gate = jax.nn.sigmoid(gate)
    silu_gate = gate * sigmoid_gate
    act = (silu_gate * up_proj).astype(jnp.bfloat16)
    ffn_branch = project(act, full_down)
    output_f = hidden + ffn_branch
    output = output_f.astype(jnp.bfloat16)
    squares = lax.psum(
        (
            jnp.sum(residual * residual),
            jnp.sum(attn_branch * attn_branch),
            jnp.sum(output_f * output_f),
        ),
        ("ulysses", "blk"),
    )
    entry_count = residual.size * lax.axis_size("ulysses") * lax.axis_size("blk")
    statistics = jnp.sqrt(jnp.stack(squares) / entry_count)
    again = (
        lax.all_gather(w_query, ("ulysses", "blk"), axis=0, tiled=True),
        lax.all_gather(w_key, ("ulysses", "blk"), axis=0, tiled=True),
        lax.all_gather(w_value, ("ulysses", "blk"), axis=0, tiled=True),
        lax.all_gather(w_out, ("ulysses", "blk"), axis=0, tiled=True),
        lax.all_gather(w_gate, ("ulysses", "blk"), axis=0, tiled=True),
        lax.all_gather(w_up, ("ulysses", "blk"), axis=0, tiled=True),
        lax.all_gather(w_down, ("ulysses", "blk"), axis=0, tiled=True),
        lax.all_gather(gain_attn, ("ulysses", "blk"), axis=0, tiled=True),
        lax.all_gather(gain_ffn, ("ulysses", "blk"), axis=0, tiled=True),
    )
    (
        back_query,
        back_key,
        back_value,
        back_out,
        back_gate,
        back_up,
        back_down,
        back_gain_attn,
        back_gain_ffn,
    ) = again
    grad_act = project_back(grad_out, back_down)
    grad_gate = (grad_act * up_proj * sigmoid_gate * (1.0 + gate * (1.0 - sigmoid_gate))).astype(
        jnp.bfloat16
    )
    grad_up = (grad_act * silu_gate).astype(jnp.bfloat16)
    grad_normed_ffn = project_back(grad_gate, back_gate) + project_back(grad_up, back_up)
    grad_ffn_norm, grad_gain_ffn = norm_back(
        grad_normed_ffn, hatted_ffn, factor_ffn, back_gain_ffn.astype(jnp.float32)
    )
    grad_hidden = grad_out.astype(jnp.float32) + grad_ffn_norm
    grad_branch = grad_hidden.astype(jnp.bfloat16)
    grad_mixed = project_back(grad_branch, back_out).astype(jnp.bfloat16)
    dout_head = lax.all_to_all(grad_mixed, "ulysses", split_axis=2, concat_axis=1, tiled=True)
    dout_four = split_heads(dout_head)
    row_dot = jnp.sum(dout_four.astype(jnp.float32) * attn_heads, axis=-1)

    def grad_rows(running, pieces, first_row):
        key_rows, value_rows = pieces
        key_count = key_rows.shape[1]

        def grad_compute(current):
            grad_query, grad_keys, grad_values = current
            key_part = split_heads(key_rows)
            allowed = allowed_mask(segments, query_start, block_rows, first_row, key_count)
            scores = (
                jnp.einsum(
                    "sqhd,skhd->sqhk", query_four, key_part, preferred_element_type=jnp.float32
                )
                * score_scale
            )
            probs = jnp.where(allowed, jnp.exp(scores - log_total[..., None]), 0.0)
            prob_grad = jnp.einsum(
                "sqhd,skhd->sqhk",
                dout_four,
                split_heads(value_rows),
                preferred_element_type=jnp.float32,
            )
            score_grad = (probs * (prob_grad - row_dot[..., None])).astype(jnp.bfloat16)
            grad_query = (
                grad_query
                + jnp.einsum(
                    "sqhk,skhd->sqhd", score_grad, key_part, preferred_element_type=jnp.float32
                )
                * score_scale
            )
            key_term = (
                jnp.einsum(
                    "sqhk,sqhd->skhd", score_grad, query_four, preferred_element_type=jnp.float32
                )
                * score_scale
            )
            value_term = jnp.einsum(
                "sqhk,sqhd->skhd",
                probs.astype(jnp.bfloat16),
                dout_four,
                preferred_element_type=jnp.float32,
            )
            return (
                grad_query,
                add_rows(grad_keys, key_term, first_row),
                add_rows(grad_values, value_term, first_row),
            )

        return lax.cond(first_row <= query_start + block_rows - 1, grad_compute, unchanged, running)

    full_zeros = jnp.zeros((seq_count, full_rows, heads_local, HD), jnp.float32)
    grad_query_own, grad_keys_all, grad_values_all = over_blocks(
        grad_rows,
        (head_zeros, full_zeros, full_zeros),
        (
            lax.all_gather(key_head, "blk", axis=1, tiled=True),
            lax.all_gather(value_head, "blk", axis=1, tiled=True),
        ),
        block_rows,
    )
    grad_key_own, grad_value_own = (
        lax.psum_scatter(
            grad_keys_all.reshape(seq_count, full_rows, width).astype(jnp.bfloat16),
            "blk",
            scatter_dimension=1,
            tiled=True,
        ).astype(jnp.float32),
        lax.psum_scatter(
            grad_values_all.reshape(seq_count, full_rows, width).astype(jnp.bfloat16),
            "blk",
            scatter_dimension=1,
            tiled=True,
        ).astype(jnp.float32),
    )
    grad_query_own = grad_query_own.reshape(seq_count, block_rows, width)
    grad_query_tok, grad_key_tok, grad_value_tok = (
        lax.all_to_all(
            grad_query_own.astype(jnp.bfloat16), "ulysses", split_axis=1, concat_axis=2, tiled=True
        ),
        lax.all_to_all(
            grad_key_own.astype(jnp.bfloat16), "ulysses", split_axis=1, concat_axis=2, tiled=True
        ),
        lax.all_to_all(
            grad_value_own.astype(jnp.bfloat16), "ulysses", split_axis=1, concat_axis=2, tiled=True
        ),
    )
    grad_query_raw = rotate(grad_query_tok.astype(jnp.float32), cosine, sine, False).astype(
        jnp.bfloat16
    )
    grad_key_raw = rotate(grad_key_tok.astype(jnp.float32), cosine, sine, False).astype(
        jnp.bfloat16
    )
    grad_v_first = grad_value_tok * 0.5
    grad_normed = (
        project_back(grad_query_raw, back_query)
        + project_back(grad_key_raw, back_key)
        + project_back(grad_v_first, back_value)
    )
    grad_attn_norm, grad_gain_attn = norm_back(
        grad_normed, hatted_attn, factor_attn, back_gain_attn.astype(jnp.float32)
    )
    grad_inputs = (grad_hidden + grad_attn_norm).astype(jnp.bfloat16)
    model_width = w_query.shape[1]
    hidden_width = w_gate.shape[1]
    owned = lax.psum_scatter(
        jnp.concatenate(
            [
                weight_grad(normed, grad_query_raw),
                weight_grad(normed, grad_key_raw),
                weight_grad(normed, grad_v_first),
                weight_grad(mixed, grad_branch),
                weight_grad(normed_ffn, grad_gate),
                weight_grad(normed_ffn, grad_up),
                grad_gain_attn[:, None],
                grad_gain_ffn[:, None],
            ],
            axis=1,
        ),
        ("ulysses", "blk"),
        scatter_dimension=0,
        tiled=True,
    )
    grad_w_down = lax.psum_scatter(
        weight_grad(act, grad_out), ("ulysses", "blk"), scatter_dimension=0, tiled=True
    )
    column = 0
    pieces = []
    for span in (model_width, model_width, model_width, model_width, hidden_width, hidden_width):
        pieces.append(owned[:, column : column + span])
        column = column + span
    grad_gain_attn_own = owned[:, column]
    grad_gain_ffn_own = owned[:, column + 1]
    return (
        output,
        grad_inputs,
        grad_v_first,
        pieces[0],
        pieces[1],
        pieces[2],
        pieces[3],
        pieces[4],
        pieces[5],
        grad_w_down,
        grad_gain_attn_own,
        grad_gain_ffn_own,
        statistics,
    )


def solution(mesh):
    in_specs = (
        P(None, ("blk", "ulysses"), None),
        P(None, ("blk", "ulysses"), None),
        P(None, ("blk", "ulysses"), None),
        P(None, ("blk", "ulysses")),
        P(),
        P(("ulysses", "blk"), None),
        P(("ulysses", "blk"), None),
        P(("ulysses", "blk"), None),
        P(("ulysses", "blk"), None),
        P(("ulysses", "blk"), None),
        P(("ulysses", "blk"), None),
        P(("ulysses", "blk"), None),
        P(("ulysses", "blk")),
        P(("ulysses", "blk")),
    )
    out_specs = (
        P(None, ("blk", "ulysses"), None),
        P(None, ("blk", "ulysses"), None),
        P(None, ("blk", "ulysses"), None),
        P(("ulysses", "blk"), None),
        P(("ulysses", "blk"), None),
        P(("ulysses", "blk"), None),
        P(("ulysses", "blk"), None),
        P(("ulysses", "blk"), None),
        P(("ulysses", "blk"), None),
        P(("ulysses", "blk"), None),
        P(("ulysses", "blk")),
        P(("ulysses", "blk")),
        P(),
    )
    return jax.shard_map(local, mesh=mesh, in_specs=in_specs, out_specs=out_specs, check_vma=False)
```

profile of v0, /device:TPU:0, one launch (start us, length us, event | category | flops | bytes accessed | tf_op | source)
XLA Modules:
  0.0 1447.1 jit_solution(2881601103230846029)
XLA Ops:
  11.1 42.1 %all-reduce.3 = (bf16[1024]{0:T(1024)(128)(2,1)S(1)}, bf16[1024]{0:T(1024)(128)(2,1)S(1)}) all-reduce(bf16[1024]{0:T(1024)(128)(2,1)S(1)} %dynamic-update-slice, bf16[1024]{0:T(1024)(128)(2,1)S(1)} %dynamic-update-slice.1), channel_id=1, replica_groups=mesh['ulysses'=4,'blk'=8] {'ulysses','blk'}, use_global_device_ids=true, to_apply=%add | all-reduce | flops 2048 | bytes 8192
  54.3 15.9 %all-gather.16.cloned.1.call-done = bf16[1024,1024]{1,0:T(8,128)(2,1)} async-done(((bf16[32,1024]{1,0:T(8,128)(2,1)}), bf16[1024,1024]{1,0:T(8,128)(2,1)}) %all-gather.16.cloned.1.call-update) | async-done | bytes 2097168 | tf_op jit(solution)/shard_map/all_gather | solution.py:120
  73.2 8.8 all_to_all.111
  84.0 44.6 %all-gather.14.cloned.1.call-done = bf16[1024,1024]{1,0:T(8,128)(2,1)} async-done(((bf16[32,1024]{1,0:T(8,128)(2,1)}), bf16[1024,1024]{1,0:T(8,128)(2,1)}) %all-gather.14.cloned.1.call-update) | async-done | bytes 2097168 | tf_op jit(solution)/shard_map/all_gather | solution.py:118
  131.0 56.0 %all-gather.10.cloned.1.call-done = bf16[1024,1024]{1,0:T(8,128)(2,1)} async-done(((bf16[32,1024]{1,0:T(8,128)(2,1)}), bf16[1024,1024]{1,0:T(8,128)(2,1)}) %all-gather.10.cloned.1.call-update) | async-done | bytes 2097168 | tf_op jit(solution)/shard_map/all_gather | solution.py:119
  191.6 8.8 all_to_all.112
  206.5 3.6 all-to-all-start.1
  210.6 4.8 all-to-all-done.1
  217.0 3.9 copy.149
  220.9 26.7 %all-gather.12.cloned.1.call-done = bf16[2,2048,256]{2,1,0:T(8,128)(2,1)} async-done(((bf16[2,256,256]{2,1,0:T(8,128)(2,1)}), bf16[2,2048,256]{2,1,0:T(8,128)(2,1)}) %all-gather.12.cloned.1.call-update) | async-done | bytes 2097168 | tf_op jit(solution)/shard_map/all_gather | solution.py:208
  247.6 3.9 copy.147
  251.6 22.1 %while.32 = (s32[]{:T(128)}, f32[2,256,4]{1,2,0:T(4,128)S(1)}, f32[2,256,4]{1,2,0:T(4,128)S(1)}, f32[2,256,4,64]{1,3,2,0:T(8,128)S(1)}, s32[8]{0:T(128)}, /*inde...) while((s32[]{:T(128)}, f32[2,256,4]{1,2,0:T(4,128)S(1)}, ...), condition=%wide.region_6.7_spmd, body=%wide.region_1.6_spmd.sunk | while | flops 141627904 | bytes 9978231 | solution.py:88
  253.5 6.7 conditional.4
  274.7 3.6 all-to-all-start.3
  278.3 5.4 all-to-all-done.3
  283.8 22.7 %all-gather.20.cloned.1.call-done = bf16[1024,1024]{1,0:T(8,128)(2,1)} async-done(((bf16[32,1024]{1,0:T(8,128)(2,1)}), bf16[1024,1024]{1,0:T(8,128)(2,1)}) %all-gather.20.cloned.1.call-update) | async-done | bytes 2097168 | tf_op jit(solution)/shard_map/all_gather | solution.py:121
  309.4 66.4 %all-gather.24.cloned.1.call-done = bf16[1024,2816]{1,0:T(8,128)(2,1)} async-done(((bf16[32,2816]{1,0:T(8,128)(2,1)}), bf16[1024,2816]{1,0:T(8,128)(2,1)}) %all-gather.24.cloned.1.call-update) | async-done | bytes 5767184 | tf_op jit(solution)/shard_map/all_gather | solution.py:123
  375.8 4.7 fusion.28
  380.5 64.4 %all-gather.26.cloned.1.call-done = bf16[2816,1024]{1,0:T(8,128)(2,1)} async-done(((bf16[88,1024]{1,0:T(8,128)(2,1)}), bf16[2816,1024]{1,0:T(8,128)(2,1)}) %all-gather.26.cloned.1.call-update) | async-done | bytes 5767184 | tf_op jit(solution)/shard_map/all_gather | solution.py:124
  444.9 5.9 fusion.22
  450.8 63.3 %all-gather.22.cloned.1.call-done = bf16[1024,2816]{1,0:T(8,128)(2,1)} async-done(((bf16[32,2816]{1,0:T(8,128)(2,1)}), bf16[1024,2816]{1,0:T(8,128)(2,1)}) %all-gather.22.cloned.1.call-update) | async-done | bytes 5767184 | tf_op jit(solution)/shard_map/all_gather | solution.py:122
  514.1 5.7 multiply_convert_fusion.1
  519.8 5.2 fusion.26
  530.9 3.4 all-to-all-start.4
  535.2 5.1 all-to-all-done.4
  546.7 32.7 %while.33 = (s32[]{:T(128)}, f32[2,256,4,64]{1,3,2,0:T(8,128)S(1)}, f32[2,2048,4,64]{1,3,2,0:T(8,128)}, f32[2,2048,4,64]{1,3,2,0:T(8,128)}, s32[8]{0:T(128)}, /*...) while((s32[]{:T(128)}, f32[2,256,4,64]{1,3,2,0:T(8,128)S(1)}, ...), condition=%wide.region_13.14_spmd, body=%wide.region_10.13_spmd.sunk | while | flops 340197888 | bytes 17990072 | solution.py:88
  548.6 17.3 %conditional.5 = ((f32[2,256,4,64]{1,3,2,0:T(8,128)S(1)}, f32[2,2048,4,64]{1,3,2,0:T(8,128)}, f32[2,2048,4,64]{1,3,2,0:T(8,128)})) conditional(s32[]{:T(128)} %convert_element_type.258, (f32[2,256,4,64]{1,3,2,0:T(8,128)S(1)}, f32[2,2048,4,64]{1,3,2,0:T(8,128)}, f32[2,2048,4,64]{1,3,2,0:T(8,128)}) %tuple.123, (s32[]{:T(128)}, s32[]{:T(128)}, ...), branch_computations={%region_11.11_spmd, %region_12.12_spmd} | conditional | flops 340197888 | bytes 17989768 | solution.py:324
  558.8 3.5 dynamic_update_slice.8
  562.3 3.5 dynamic_update_slice.9
  579.4 3.8 convert_element_type.182
  583.3 3.9 convert_element_type.175
  588.4 5.9 convolution_bitcast_fusion.4
  595.2 3.4 all-to-all-start.5
  598.7 6.0 convolution_bitcast_fusion.3
  605.7 2.8 convolution_bitcast_fusion.5
  608.5 127.2 %reduce-scatter.7.cloned.1.call-done = bf16[2,256,256]{1,2,0:T(8,128)(2,1)} async-done(((bf16[2,2048,256]{1,2,0:T(8,128)(2,1)}), bf16[2,256,256]{1,2,0:T(8,128)(2,1)}) %reduce-scatter.7.cloned.1.call-update) | async-done | bytes 262160 | tf_op jit(solution)/shard_map/reduce_scatter | solution.py:343
  737.5 4.0 all-to-all-start.7
  742.3 30.1 %reduce-scatter.5.cloned.1.call-done = bf16[2,256,256]{1,2,0:T(8,128)(2,1)} async-done(((bf16[2,2048,256]{1,2,0:T(8,128)(2,1)}), bf16[2,256,256]{1,2,0:T(8,128)(2,1)}) %reduce-scatter.5.cloned.1.call-update) | async-done | bytes 262160 | tf_op jit(solution)/shard_map/reduce_scatter | solution.py:337
  774.3 3.7 all-to-all-start.6
  779.3 4.1 all-to-all-done.6
  785.1 3.2 add_convert_fusion
  793.4 3.0 convolution_bitcast_fusion.7
  807.0 42.7 %concatenate.23 = f32[1024,9730]{1,0:T(8,128)} concatenate(f32[1024,1024]{1,0:T(8,128)} %convolution_bitcast_fusion.8, f32[1024,1024]{1,0:T(8,128)} %convolution_bitcast_fusion.7, f32[1024,1024]{1,0:T(8,128)} %convolution_bitcast_fusion.6, f32[1024,1024]{1,0:T(8,128)} %convolution_bitcast_fusion.5, f32[1024,2816]{1,0:T(8,128)} %convolution_bitcast_fusion.4, ...), dimensions={1} | concatenate | bytes 79708160 | tf_op jit(solution)/shard_map/concatenate | solution.py:381
  850.8 5.9 convolution_bitcast_fusion.2
  856.8 4.9 multiply_reduce_fusion
  861.6 39.3 %all-reduce.2 = (f32[1]{0:T(128)}, f32[1]{0:T(128)}, f32[1]{0:T(128)}) all-reduce(f32[1]{0:T(128)} %bitcast.61, f32[1]{0:T(128)} %bitcast.60, f32[1]{0:T(128)} %bitcast.59), channel_id=1, replica_groups=mesh['ulysses'=4,'blk'=8] {'ulysses','blk'}, use_global_device_ids=true, to_apply=%region_26.27 | all-reduce | flops 3 | bytes 24 | tf_op jit(solution)/shard_map/psum | solution.py:229
  904.4 375.5 %reduce-scatter.9.cloned.1.call-done = f32[32,9730]{1,0:T(8,128)} async-done(((f32[1024,9730]{1,0:T(8,128)}), f32[32,9730]{1,0:T(8,128)}) %reduce-scatter.9.cloned.1.call-update) | async-done | bytes 1245456 | tf_op jit(solution)/shard_map/reduce_scatter | solution.py:380
  1285.2 154.9 %reduce-scatter.11.cloned.1.call-done = f32[88,1024]{1,0:T(8,128)} async-done(((f32[2816,1024]{1,0:T(8,128)}), f32[88,1024]{1,0:T(8,128)}) %reduce-scatter.11.cloned.1.call-update) | async-done | bytes 360464 | tf_op jit(solution)/shard_map/reduce_scatter | solution.py:398
  (228 shorter events, 110.9 us)
Async XLA Ops:
  7.2 63.1 %all-gather.16.cloned.1.call-start = ((), (), s32[]{:S(2)}) async-start(), calls=%async_computation.15 | async-start | bytes 2162688 | tf_op jit(solution)/shard_map/all_gather | solution.py:120
  7.9 120.7 %all-gather.14.cloned.1.call-start = ((), (), s32[]{:S(2)}) async-start(), calls=%async_computation.14 | async-start | bytes 2162688 | tf_op jit(solution)/shard_map/all_gather | solution.py:118
  8.7 178.3 %all-gather.10.cloned.1.call-start = ((), (), s32[]{:S(2)}) async-start(), calls=%async_computation.12 | async-start | bytes 2162688 | tf_op jit(solution)/shard_map/all_gather | solution.py:119
  9.4 207.6 %all-gather.18.cloned.1.call-start = ((), (), s32[]{:S(2)}) async-start(), calls=%async_computation.16 | async-start | bytes 2359296 | tf_op jit(solution)/shard_map/all_gather | solution.py:209
  53.2 133.7 %copy-start.21 = (f32[1024]{0:T(1024)}, f32[1024]{0:T(1024)S(1)}, u32[]{:S(2)}) copy-start(f32[1024]{0:T(1024)S(1)} %convert_element_type.149) | copy-start | bytes 12292
  54.3 132.6 %copy-start.23 = (f32[2,64]{1,0:T(2,128)}, f32[2,64]{1,0:T(2,128)S(1)}, u32[]{:S(2)}) copy-start(f32[2,64]{1,0:T(2,128)S(1)} %add_rsqrt_fusion.1) | copy-start | bytes 1540
  72.4 11.3 copy-start.28
  72.8 55.8 %copy-start = (bf16[2,64,1024]{2,1,0:T(8,128)(2,1)S(1)}, bf16[2,64,1024]{2,1,0:T(8,128)(2,1)}, u32[]{:S(2)}) copy-start(bf16[2,64,1024]{2,1,0:T(8,128)(2,1)} %param.22) | copy-start | bytes 786436
  83.6 164.0 %all-gather.12.cloned.1.call-start = ((), (), s32[]{:S(2)}) async-start(), calls=%async_computation.13 | async-start | bytes 2359296 | tf_op jit(solution)/shard_map/all_gather | solution.py:208
  202.0 104.4 %all-gather.20.cloned.1.call-start = ((), (), s32[]{:S(2)}) async-start(), calls=%async_computation.17 | async-start | bytes 2162688 | tf_op jit(solution)/shard_map/all_gather | solution.py:121
  202.6 173.2 %all-gather.24.cloned.1.call-start = ((), (), s32[]{:S(2)}) async-start(), calls=%async_computation.19 | async-start | bytes 5947392 | tf_op jit(solution)/shard_map/all_gather | solution.py:123
  203.3 241.6 %all-gather.26.cloned.1.call-start = ((), (), s32[]{:S(2)}) async-start(), calls=%async_computation.20 | async-start | bytes 5947392 | tf_op jit(solution)/shard_map/all_gather | solution.py:124
  204.1 310.0 %all-gather.22.cloned.1.call-start = ((), (), s32[]{:S(2)}) async-start(), calls=%async_computation.18 | async-start | bytes 5947392 | tf_op jit(solution)/shard_map/all_gather | solution.py:122
  206.5 8.9 all-to-all-start.1
  274.7 9.0 all-to-all-start.3
  278.3 246.7 %copy-start.25 = (f32[1024]{0:T(1024)}, f32[1024]{0:T(1024)S(1)}, u32[]{:S(2)}) copy-start(f32[1024]{0:T(1024)S(1)} %convert_element_type.158) | copy-start | bytes 12292
  283.8 25.4 %copy-start.15 = (bf16[2,4,8,8,256]{4,3,1,2,0:T(8,128)(2,1)}, bf16[2,4,8,8,256]{4,3,1,2,0:T(8,128)(2,1)S(1)}, u32[]{:S(2)}) copy-start(bf16[2,4,8,8,256]{4,3,1,2,0:T(8,128)(2,1)S(1)} %copy.195) | copy-start | bytes 786436
  309.2 215.8 %copy-start.27 = (f32[2,64]{1,0:T(2,128)}, f32[2,64]{1,0:T(2,128)S(1)}, u32[]{:S(2)}) copy-start(f32[2,64]{1,0:T(2,128)S(1)} %add_rsqrt_fusion) | copy-start | bytes 1540
  309.3 204.8 %copy-start.6 = (bf16[2,64,1024]{2,1,0:T(8,128)(2,1)}, bf16[2,64,1024]{2,1,0:T(8,128)(2,1)S(1)}, u32[]{:S(2)}) copy-start(bf16[2,64,1024]{2,1,0:T(8,128)(2,1)S(1)} %multiply_convert_fusion.3) | copy-start | bytes 786436
  309.3 135.6 %copy-start.13 = (bf16[2,64,1024]{2,1,0:T(8,128)(2,1)S(1)}, bf16[2,64,1024]{2,1,0:T(8,128)(2,1)}, u32[]{:S(2)}) copy-start(bf16[2,64,1024]{2,1,0:T(8,128)(2,1)} %param.24) | copy-start | bytes 786436
  519.8 5.2 copy-start.10
  519.8 5.2 copy-start.8
  519.8 5.2 copy-start.1
  525.0 3.5 copy-start.5
  530.9 9.4 all-to-all-start.4
  534.3 201.4 %reduce-scatter.7.cloned.1.call-start = ((), (), s32[]{:S(2)}) async-start(), calls=%async_computation.22 | async-start | bytes 2359296 | tf_op jit(solution)/shard_map/reduce_scatter | solution.py:343
  583.3 189.2 %reduce-scatter.5.cloned.1.call-start = ((), (), s32[]{:S(2)}) async-start(), calls=%async_computation.21 | async-start | bytes 2359296 | tf_op jit(solution)/shard_map/reduce_scatter | solution.py:337
  587.2 0.9 copy-start.7
  587.2 1.2 copy-start.9
  594.3 4.3 copy-start.11
  595.2 13.3 all-to-all-start.5
  598.6 6.0 copy-start.26
  598.6 7.0 copy-start.16
  737.5 36.7 %all-to-all-start.7 = ((bf16[2,256,256]{2,0,1:T(2,128)(2,1)}), bf16[2,256,256]{2,0,1:T(2,128)(2,1)}, u32[]{:S(2)}, u32[]{:S(2)}) async-start(bf16[2,256,256]{2,0,1:T(2,128)(2,1)} %copy.166), calls=%async_computation.9 | async-start | bytes 524288 | tf_op jit(solution)/shard_map/all_to_all | solution.py:358
  774.3 9.1 all-to-all-start.6
  778.0 501.9 %reduce-scatter.9.cloned.1.call-start = ((), (), s32[]{:S(2)}) async-start(), calls=%async_computation.23 | async-start | bytes 41631744 | tf_op jit(solution)/shard_map/reduce_scatter | solution.py:380
  779.2 22.8 %copy-start.17 = (bf16[2,4,8,8,256]{4,3,1,2,0:T(8,128)(2,1)}, bf16[2,4,8,8,256]{4,3,1,2,0:T(8,128)(2,1)S(1)}, u32[]{:S(2)}) copy-start(bf16[2,4,8,8,256]{4,3,1,2,0:T(8,128)(2,1)S(1)} %copy.196) | copy-start | bytes 786436
  788.3 2.5 copy-start.19
  788.3 2.6 copy-start.20
  788.3 5.1 copy-start.22
  788.3 5.1 copy-start.24
  799.2 2.8 copy-start.2
  802.0 1.6 copy-start.3
  803.6 1.6 copy-start.4
  805.2 1.8 copy-start.18
  849.6 1.1 copy-start.12
  849.6 1.2 copy-start.14
  849.7 590.4 %reduce-scatter.11.cloned.1.call-start = ((), (), s32[]{:S(2)}) async-start(), calls=%async_computation.24 | async-start | bytes 11894784 | tf_op jit(solution)/shard_map/reduce_scatter | solution.py:398
Sparse Core Ops, SparseCore 0:
  11.0 59.1 all-gather.15
  73.2 55.3 all-gather.13
  131.6 55.3 all-gather.9
  189.0 27.9 all-gather.17
  219.0 28.5 all-gather.11
  250.5 55.9 all-gather.19
  309.3 66.4 all-gather.23
  378.7 66.2 all-gather.25
  447.8 66.2 all-gather.21
  583.4 152.2 reduce-scatter.6
  738.0 34.3 reduce-scatter.4
  849.8 430.0 reduce-scatter.8
  1282.8 157.2 reduce-scatter.10
where the time goes:
time: 1460 us; the launch traced here: 1450 us
  waiting for transfers between devices  1070 us (73%)
  local copies, waits for them, and re-layouts  120 us (8%)
  blocking collectives  98.9 us (7%)
  matrix products  77.9 us (5%)
  other arithmetic  25.1 us (2%)
  starting transfers between devices  22.7 us (2%)
  loops' own time  15 us (1%)
  between operations  15 us (1%)
    reduce_scatter x1, waiting for transfers between devices, local(): lax.psum_scatter(jnp.concatenate([weight_grad(normed, grad_query_raw), we...  375 us
    reduce_scatter x1, waiting for transfers between devices, local(): lax.psum_scatter(weight_grad(act, grad_out), ('ulysses', 'blk'), scatter_...  155 us
    reduce_scatter x1, waiting for transfers between devices, local(): lax.psum_scatter(grad_values_all.reshape(seq_count, full_rows, width).ast...  127 us
    all_gather x1, waiting for transfers between devices, local(): lax.all_gather(w_up, ('ulysses', 'blk'), axis=0, tiled=True)  66.4 us
    all_gather x1, waiting for transfers between devices, local(): lax.all_gather(w_down, ('ulysses', 'blk'), axis=0, tiled=True)  64.4 us
    all_gather x1, waiting for transfers between devices, local(): lax.all_gather(w_gate, ('ulysses', 'blk'), axis=0, tiled=True)  63.3 us
    all_gather x1, waiting for transfers between devices, local(): lax.all_gather(w_key, ('ulysses', 'blk'), axis=0, tiled=True)  56 us
    all_gather x1, waiting for transfers between devices, local(): lax.all_gather(w_query, ('ulysses', 'blk'), axis=0, tiled=True)  44.6 us
  transfers between devices with their start and end apart: 19, of which 17 were waited for; matrix products, arithmetic and copies ran while one was open for 7% of the time, Pallas kernels for 0%

commit v1 on v0

--- a/solution.py
+++ b/solution.py
@@ -1,6 +1,10 @@
+import functools
+
 import jax
 import jax.numpy as jnp
 from jax import lax
+from jax.experimental import pallas as pl
+from jax.experimental.pallas import tpu as pltpu
 from jax.sharding import PartitionSpec as P
 
 HEADS = 16
@@ -422,6 +426,763 @@
     )
 
 
+MESH = pl.DeviceIdType.MESH
+LANES = 128
+VMEM_BYTES = 58 << 20
+f32 = jnp.float32
+bf16 = jnp.bfloat16
+
+
+class Net:
+    def __init__(self, send_sems, recv_sems):
+        self.send_sems, self.recv_sems = send_sems, recv_sems
+        self.count, self.open = 0, []
+
+    def push(self, src, dst, u, b):
+        at = self.count
+        self.count += 1
+        copy = pltpu.make_async_remote_copy(
+            src_ref=src,
+            dst_ref=dst,
+            send_sem=self.send_sems.at[at],
+            recv_sem=self.recv_sems.at[at],
+            device_id=(u, b),
+            device_id_type=MESH,
+        )
+        copy.start()
+        self.open.append(copy)
+        return copy
+
+    def drain(self):
+        for copy in self.open:
+            copy.wait_send()
+        self.open = []
+
+
+def arrive(copies):
+    for copy in copies:
+        copy.wait_recv()
+
+
+def here():
+    return lax.axis_index("ulysses"), lax.axis_index("blk")
+
+
+def greet(u, b, n_u, n_b):
+    barrier = pltpu.get_barrier_semaphore()
+    for off in range(1, n_u):
+        pl.semaphore_signal(barrier, inc=1, device_id=(u ^ off, b), device_id_type=MESH)
+    for off in range(1, n_b):
+        pl.semaphore_signal(barrier, inc=1, device_id=(u, b ^ off), device_id_type=MESH)
+    pl.semaphore_wait(barrier, n_u - 1 + n_b - 1)
+
+
+def dot(left, right):
+    return jnp.dot(left, right, preferred_element_type=f32)
+
+
+def dot_nt(left, right):
+    return lax.dot_general(left, right, (((1,), (1,)), ((), ())), preferred_element_type=f32)
+
+
+def dot_tn(left, right):
+    return lax.dot_general(left, right, (((0,), (0,)), ((), ())), preferred_element_type=f32)
+
+
+def lane_of(shape):
+    return lax.broadcasted_iota(jnp.int32, shape, len(shape) - 1)
+
+
+def swap_halves(tile):
+    return pltpu.roll(tile, HD, tile.ndim - 1)
+
+
+def partner(tile):
+    low = lane_of(tile.shape) % HD < HD // 2
+    return jnp.where(low, pltpu.roll(tile, LANES - HD // 2, 1), pltpu.roll(tile, HD // 2, 1))
+
+
+def pack_rows(rows):
+    half = rows.shape[0] // 2
+    low = lane_of((half, LANES)) < HD
+    return jnp.where(low, rows[:half], swap_halves(rows[half:]))
+
+
+def unpack_rows(packed):
+    return jnp.concatenate([packed, swap_halves(packed)], axis=0)
+
+
+class Gather:
+    def __init__(self, net, slot, u, b, n_b):
+        self.net, self.slot, self.u, self.b, self.n_b = net, slot, u, b, n_b
+        mine = slot(b)
+        self.along = [net.push(mine, mine, u, b ^ (2 * k)) for k in range(1, n_b // 2)]
+        self.side = [net.push(mine, mine, u, b ^ 1)]
+
+    def relay(self):
+        for k in range(1, self.n_b // 2):
+            self.along[k - 1].wait_recv()
+            got = self.slot(self.b ^ (2 * k))
+            self.side.append(self.net.push(got, got, self.u, self.b ^ 1))
+
+    def finish(self):
+        arrive(self.side)
+
+
+def kernel_project(dims, x, vf, go, wqkv, wgu, gains, cosr, sinr, units, normed, wq, gog, wg1, gain,
+                   xg, vfg, stage, gbuf, send_sems, recv_sems):
+    n_u, n_b, seqs, td, rows, heads = dims
+    tb = n_u * td
+    u, b = here()
+    net = Net(send_sems, recv_sems)
+    mine = pl.ds(pl.multiple_of(b * rows, rows), rows)
+    slab = pl.ds(pl.multiple_of(u * td, td), td)
+    greet(u, b, n_u, n_b)
+    others = [u ^ off for off in range(1, n_u)]
+    got_w = [net.push(wqkv.at[v], wq.at[u, mine], v, b) for v in others]
+    got_g = [net.push(gains, gbuf.at[b, u], v, b) for v in others]
+    got_x = [net.push(x, xg.at[:, slab], v, b) for v in others]
+    got_v = [net.push(vf.at[v], vfg.at[:, slab], v, b) for v in others]
+    wq[u, mine] = wqkv[u]
+    gbuf[b, u] = gains[...]
+    xg[:, slab] = x[...]
+    vfg[:, slab] = vf[u]
+    gog[:, slab] = go[...]
+    wg1[u] = wgu[u]
+    arrive(got_w)
+    weights = Gather(net, lambda c: wq.at[:, pl.ds(pl.multiple_of(c * rows, rows), rows)], u, b, n_b)
+    arrive(got_g)
+    got_g = [net.push(gbuf.at[b], gbuf.at[b], u, b ^ off) for off in range(1, n_b)]
+    got_o = [net.push(go, gog.at[:, slab], v, b) for v in others]
+    got_o += [net.push(wgu.at[v], wg1.at[u], v, b) for v in others]
+    arrive(got_g)
+    per_tile = LANES // rows
+    for tile in range(n_u * n_b // per_tile):
+        total = None
+        for index in range(tile * per_tile, (tile + 1) * per_tile):
+            term = gbuf[index % n_b, index // n_b]
+            total = term if total is None else total + term
+        gain[:, tile * LANES : (tile + 1) * LANES] = total
+    arrive(got_x)
+
+    def norm(step, carry):
+        s, part = step // 2, step % 2
+        place = pl.ds(pl.multiple_of(part * (tb // 2), tb // 2), tb // 2)
+        values = xg[s, place].astype(f32)
+        factor = lax.rsqrt(jnp.mean(values * values, axis=-1, keepdims=True) + epsilon)
+        normed[s, place] = (values * factor * gain[0:1, :]).astype(bf16)
+        return carry
+
+    lax.fori_loop(0, 2 * seqs, norm, 0)
+    arrive(got_v)
+    weights.relay()
+    weights.finish()
+
+    depth = wq.shape[0] * wq.shape[1]
+    for s in range(seqs):
+        left = normed[s]
+        for n in range(heads // 2):
+            found = dot(left, wq[:, :, n * 256 : (n + 1) * 256].reshape(depth, 256))
+            for i in range(2):
+                tile = found[:, i * LANES : (i + 1) * LANES]
+                turned = tile * cosr[s] + partner(tile) * sinr[s]
+                stage[s * heads + 2 * n + i, 0:tb] = turned.astype(bf16)
+        for n in range(heads // 4):
+            at = heads * LANES + n * 256
+            found = dot(left, wq[:, :, at : at + 256].reshape(depth, 256))
+            for i in range(2):
+                first = vfg[s, :, n * 256 + i * LANES : n * 256 + (i + 1) * LANES].astype(f32)
+                value = 0.5 * found[:, i * LANES : (i + 1) * LANES] + 0.5 * first
+                unit = s * heads + 4 * n + 2 * i
+                stage[unit, tb:] = pack_rows(value).astype(bf16)
+                stage[unit + 1, tb:] = pack_rows(swap_halves(value)).astype(bf16)
+    got = [net.push(stage.at[b ^ off], units.at[b], u, b ^ off) for off in range(1, n_b)]
+    units[b] = stage[b]
+    arrive(got)
+    arrive(got_o)
+    net.drain()
+
+
+def fill_units(units, tb, store):
+    def one(block, carry):
+        low = lane_of((tb, LANES)) < HD
+        tile = units[block, 0:tb].astype(f32)
+        query = jnp.where(low, tile * HD ** (-0.5), 0.0)
+        key = jnp.where(low, swap_halves(tile), 0.0)
+        value = jnp.where(low, unpack_rows(units[block, tb:].astype(f32)), 0.0)
+        store(block, query, key, value)
+        return carry
+
+    lax.fori_loop(0, units.shape[0], one, 0)
+
+
+QB, KB = 512, 256
+
+
+def allowed_block(first_key, first_query, low_row):
+    key_place = first_key + lax.broadcasted_iota(jnp.int32, (KB, QB), 0)
+    query_place = first_query + lax.broadcasted_iota(jnp.int32, (KB, QB), 1)
+    return (key_place <= query_place) & (key_place >= low_row)
+
+
+def kernel_attend(dims, units, low, x, wout, wg1, wd, gain, hidden, nf, wg, wdg, wo, mix, heads_t, lse, sums,
+                  keys, query_t, value_t, acc, stage, parts, branch, branch_low, landed, nf_own,
+                  send_sems, recv_sems):
+    n_u, n_b, seqs, td, rows, heads = dims
+    tb = n_u * td
+    u, b = here()
+    net = Net(send_sems, recv_sems)
+    slab = pl.ds(pl.multiple_of(u * td, td), td)
+    ff_rows = wd.shape[0]
+    greet(u, b, n_u, n_b)
+
+    def slot(ref, size):
+        return lambda c: ref.at[pl.ds(pl.multiple_of(c * size, size), size)]
+
+    wo[pl.ds(pl.multiple_of(b * rows, rows), rows)] = wout[...]
+    g_out = Gather(net, slot(wo, rows), u, b, n_b)
+    wdg[pl.ds(pl.multiple_of(b * ff_rows, ff_rows), ff_rows)] = wd[...]
+    g_down = Gather(net, slot(wdg, ff_rows), u, b, n_b)
+    wg[:, pl.ds(pl.multiple_of(b * rows, rows), rows)] = wg1[...]
+    g_gate = Gather(net, lambda c: wg.at[:, pl.ds(pl.multiple_of(c * rows, rows), rows)], u, b, n_b)
+
+    def store(block, query, key, value):
+        place = pl.ds(pl.multiple_of(block * tb, tb), tb)
+        keys[place] = key.astype(bf16)
+        query_t[:, place] = jnp.transpose(query).astype(bf16)
+        value_t[:, place] = jnp.transpose(value)[:HD].astype(bf16)
+
+    fill_units(units, tb, store)
+    seq = n_b * tb
+
+    def attend(qb, carry):
+        q_at = pl.ds(pl.multiple_of(qb * QB, QB), QB)
+        query = query_t[:, q_at]
+        low_row = low[0:1, q_at]
+        acc[...] = jnp.zeros_like(acc)
+
+        def inner(kb, state):
+            best, total = state
+            k_at = pl.ds(pl.multiple_of(kb * KB, KB), KB)
+            scores = dot(keys[k_at], query)
+            scores = jnp.where(allowed_block(kb * KB, qb * QB, low_row), scores, neg_big)
+            new_best = jnp.maximum(best, jnp.max(scores, axis=0, keepdims=True))
+            weights = jnp.exp(scores - new_best)
+            rescale = jnp.exp(best - new_best)
+            total = total * rescale + jnp.sum(weights, axis=0, keepdims=True)
+            acc[...] = acc[...] * rescale + dot(value_t[:, k_at], weights.astype(bf16))
+            return new_best, total
+
+        start = (jnp.full((1, QB), neg_big, f32), jnp.zeros((1, QB), f32))
+        best, total = lax.fori_loop(0, (qb + 1) * (QB // KB), inner, start)
+        out = acc[...] / total
+        heads_t[:, q_at] = out
+        lse[:, q_at] = jnp.broadcast_to(best + jnp.log(total), (8, QB))
+        turned = jnp.transpose(jnp.concatenate([out, jnp.zeros_like(out)], axis=0))
+        for i in range(QB // tb):
+            stage[qb * (QB // tb) + i] = pack_rows(turned[i * tb : (i + 1) * tb]).astype(bf16)
+        return carry
+
+    lax.fori_loop(0, seq // QB, attend, 0)
+    got = [net.push(stage.at[b ^ off], parts.at[b], u, b ^ off) for off in range(1, n_b)]
+    parts[b] = stage[b]
+    g_out.relay()
+    arrive(got)
+    half = tb // 2
+    for s in range(seqs):
+        for pair in range(heads // 2):
+            one = parts[s * heads + 2 * pair].astype(f32)
+            two = parts[s * heads + 2 * pair + 1].astype(f32)
+            low_lane = lane_of(one.shape) < HD
+            lanes = slice(pair * LANES, (pair + 1) * LANES)
+            mix[s, :half, lanes] = jnp.where(low_lane, one, swap_halves(two)).astype(bf16)
+            mix[s, half:, lanes] = jnp.where(low_lane, swap_halves(one), two).astype(bf16)
+    g_out.finish()
+    others = [u ^ off for off in range(1, n_u)]
+
+    def project_out(s, carry):
+        found = dot(mix[s], wo[...])
+        branch[s] = found
+        branch_low[s] = found.astype(bf16)
+        return carry
+
+    lax.fori_loop(0, seqs, project_out, 0)
+
+    def part(v):
+        return pl.ds(pl.multiple_of(v * td, td), td)
+
+    got = [net.push(branch_low.at[:, part(v)], landed.at[u], v, b) for v in others]
+    arrive(got)
+    for s in range(seqs):
+        total = branch[s, slab]
+        for v in others:
+            total = total + landed[v, s].astype(f32)
+        own = x[s].astype(f32)
+        hid = own + total
+        hidden[s] = hid
+        factor = lax.rsqrt(jnp.mean(hid * hid, axis=-1, keepdims=True) + epsilon)
+        nf_own[s] = (hid * factor * gain[1:2, :]).astype(bf16)
+        squares = [jnp.sum(own * own, axis=0, keepdims=True), jnp.sum(total * total, axis=0, keepdims=True)]
+        if s == 0:
+            sums[...] = jnp.zeros_like(sums)
+        for i, square in enumerate(squares):
+            sums[i : i + 1] = sums[i : i + 1] + square
+    got = [net.push(nf_own, nf.at[:, slab], v, b) for v in others]
+    nf[:, slab] = nf_own[...]
+    g_down.relay()
+    g_gate.relay()
+    g_down.finish()
+    g_gate.finish()
+    arrive(got)
+    net.drain()
+
+
+class Scatter:
+    def __init__(self, net, u, b, n_b, mine, paired, summed, landed):
+        self.net, self.u, self.b, self.n_z = net, u, b, n_b // 2
+        self.mine, self.paired, self.summed, self.landed = mine, paired, summed, landed
+        core = b % 2
+        self.swap = [net.push(mine(z, 1 - core), paired(z), u, b ^ 1) for z in range(self.n_z)]
+
+    def middle(self):
+        z_own, core = self.b // 2, self.b % 2
+        self.along = []
+        for k in range(self.n_z):
+            if k == 0:
+                arrive(self.swap)
+            z = z_own ^ ((k + 1) % self.n_z)
+            self.summed[z] = (
+                self.mine(z, core)[...].astype(f32) + self.paired(z)[...].astype(f32)
+            ).astype(bf16)
+            if k + 1 < self.n_z:
+                self.along.append(
+                    self.net.push(
+                        self.summed.at[z], self.landed.at[k], self.u, self.b ^ (2 * (k + 1))
+                    )
+                )
+
+    def finish(self):
+        arrive(self.along)
+        total = self.summed[self.b // 2].astype(f32)
+        for k in range(self.n_z - 1):
+            total = total + self.landed[k].astype(f32)
+        return total
+
+
+def kernel_feed(dims, nf, gog, wg, wdg, wo, mix, hidden, gain, sums_in, out, ghid, units, dwd, dwgu, dwo, sums,
+                act, dgu, d_part, d_low, f_part, f_low, landed_d, landed_f, gb_own, gb, stage,
+                wd_buf, wd_pair, wd_sum, wd_land, wg_buf, wg_pair, wg_sum, wg_land, wg_low,
+                send_sems, recv_sems):
+    n_u, n_b, seqs, td, rows, heads = dims
+    tb = n_u * td
+    n_z = n_b // 2
+    u, b = here()
+    net = Net(send_sems, recv_sems)
+    slab = pl.ds(pl.multiple_of(u * td, td), td)
+    greet(u, b, n_u, n_b)
+    others = [u ^ off for off in range(1, n_u)]
+    depth = wg.shape[0] * wg.shape[1]
+    units_ff = wdg.shape[0]
+    ff_rows = units_ff // n_b
+
+    def part(v):
+        return pl.ds(pl.multiple_of(v * td, td), td)
+
+    def hidden_units(s, carry):
+        left = nf[s]
+        grad = gog[s]
+        for n in range(units_ff // 256):
+            span = slice(n * 256, (n + 1) * 256)
+            up_span = slice(units_ff + n * 256, units_ff + (n + 1) * 256)
+            gate = dot(left, wg[:, :, span].reshape(depth, 256))
+            up = dot(left, wg[:, :, up_span].reshape(depth, 256))
+            grad_act = dot_nt(grad, wdg[span])
+            sig = 1.0 / (1.0 + jnp.exp(-gate))
+            silu = gate * sig
+            act[s, :, span] = (silu * up).astype(bf16)
+            dgu[s, :, span] = (grad_act * up * sig * (1.0 + gate * (1.0 - sig))).astype(bf16)
+            dgu[s, :, up_span] = (grad_act * silu).astype(bf16)
+        return carry
+
+    lax.fori_loop(0, seqs, hidden_units, 0)
+
+    def back(s, carry):
+        left = dgu[s]
+        for v in range(n_u):
+            lanes = slice(v * 256, (v + 1) * 256)
+            found = dot_nt(left, wg[v])
+            d_part[s, :, lanes] = found
+            d_low[s, :, lanes] = found.astype(bf16)
+        return carry
+
+    lax.fori_loop(0, seqs, back, 0)
+    got_d = [net.push(d_low.at[:, part(v)], landed_d.at[u], v, b) for v in others]
+
+    width = wdg.shape[1]
+    half_units = units_ff // 2
+    for n in range(2):
+        span = slice(n * half_units, (n + 1) * half_units)
+        found = dot_tn(act[:, :, span].reshape(seqs * tb, half_units), gog[...].reshape(seqs * tb, width))
+        wd_buf[n * (n_z // 2) : (n + 1) * (n_z // 2)] = found.astype(bf16).reshape(
+            n_z // 2, 2, ff_rows, width
+        )
+    s_down = Scatter(net, u, b, n_b, lambda z, c: wd_buf.at[z, c], lambda z: wd_pair.at[z], wd_sum, wd_land)
+    for v in range(n_u):
+        left = nf[:, :, v * 256 : (v + 1) * 256].reshape(seqs * tb, 256)
+        found = dot_tn(left, dgu[...].reshape(seqs * tb, 2 * units_ff))
+        wg_buf[:, :, v] = found.astype(bf16).reshape(n_z, 2, rows, 2 * units_ff)
+    s_gate = Scatter(net, u, b, n_b, lambda z, c: wg_buf.at[z, c], lambda z: wg_pair.at[z], wg_sum, wg_land)
+
+    s_down.middle()
+    s_gate.middle()
+
+    arrive(got_d)
+    sums[...] = sums_in[...]
+    for s in range(seqs):
+        grad_normed = d_part[s, slab]
+        for v in others:
+            grad_normed = grad_normed + landed_d[v, s].astype(f32)
+        hid = hidden[s]
+        factor = lax.rsqrt(jnp.mean(hid * hid, axis=-1, keepdims=True) + epsilon)
+        hat = hid * factor
+        scaled = grad_normed * gain[1:2, :]
+        inner = jnp.mean(scaled * hat, axis=-1, keepdims=True)
+        total = gog[s, slab].astype(f32) + factor * (scaled - hat * inner)
+        ghid[s] = total
+        gb_own[s] = total.astype(bf16)
+        sums[4:5] = sums[4:5] + jnp.sum(grad_normed * hat, axis=0, keepdims=True)
+    got_b = [net.push(gb_own, gb.at[:, slab], v, b) for v in others]
+    gb[:, slab] = gb_own[...]
+
+    def forward(s, carry):
+        found = dot(act[s], wdg[...])
+        f_part[s] = found
+        f_low[s] = found.astype(bf16)
+        return carry
+
+    lax.fori_loop(0, seqs, forward, 0)
+    arrive(got_b)
+    for s in range(seqs):
+        for pair in range(heads // 2):
+            found = dot_nt(gb[s], wo[pair * LANES : (pair + 1) * LANES])
+            stage[s * heads + 2 * pair] = pack_rows(found).astype(bf16)
+            stage[s * heads + 2 * pair + 1] = pack_rows(swap_halves(found)).astype(bf16)
+    got_u = [net.push(stage.at[b ^ off], units.at[b], u, b ^ off) for off in range(1, n_b)]
+    units[b] = stage[b]
+    got_f = [net.push(f_low.at[:, part(v)], landed_f.at[u], v, b) for v in others]
+    found = dot_tn(mix[...].reshape(seqs * tb, mix.shape[2]), gb[...].reshape(seqs * tb, width))
+    dwo[...] = found.astype(bf16).reshape(dwo.shape)
+
+    arrive(got_f)
+    for s in range(seqs):
+        total = hidden[s] + f_part[s, slab]
+        for v in others:
+            total = total + landed_f[v, s].astype(f32)
+        out[s] = total.astype(bf16)
+        sums[2:3] = sums[2:3] + jnp.sum(total * total, axis=0, keepdims=True)
+
+    dwd[...] = s_down.finish()
+    wg_low[...] = s_gate.finish().astype(bf16)
+    got = [net.push(wg_low.at[v], dwgu.at[u], v, b) for v in others]
+    dwgu[u] = wg_low[u]
+    arrive(got_u)
+    arrive(got)
+    net.drain()
+
+
+def kernel_back(dims, units, grads, heads_t, lse, low, normed, wq, cosr, sinr, ghid, x, gain, dwo_in, sums_in,
+                gin, gvf, dwq, dwo, sums,
+                keys, key_t, query, query_t, value, grad, grad_t, row_dot, dq_t, dk, dv, stage, returned, raw,
+                gin_part, gin_low, landed, gv, wq_buf, wq_pair, wq_sum, wq_land, wq_low,
+                wo_pair, wo_sum, wo_land, sums_own, sums_u, sums_ub, sums_b, send_sems, recv_sems):
+    n_u, n_b, seqs, td, rows, heads = dims
+    tb = n_u * td
+    n_z = n_b // 2
+    seq = n_b * tb
+    u, b = here()
+    net = Net(send_sems, recv_sems)
+    slab = pl.ds(pl.multiple_of(u * td, td), td)
+    greet(u, b, n_u, n_b)
+    others = [u ^ off for off in range(1, n_u)]
+    s_out = Scatter(net, u, b, n_b, lambda z, c: dwo_in.at[z, c], lambda z: wo_pair.at[z], wo_sum, wo_land)
+
+    def part(v):
+        return pl.ds(pl.multiple_of(v * td, td), td)
+
+    def store(block, q, k, v):
+        place = pl.ds(pl.multiple_of(block * tb, tb), tb)
+        keys[place] = k.astype(bf16)
+        key_t[:, place] = jnp.transpose(k)[:HD].astype(bf16)
+        query[place] = q.astype(bf16)
+        query_t[:, place] = jnp.transpose(q).astype(bf16)
+        value[place] = v.astype(bf16)
+        g = unpack_rows(grads[block].astype(f32))
+        g = jnp.where(lane_of(g.shape) < HD, g, 0.0)
+        grad[place] = g.astype(bf16)
+        turned = jnp.transpose(g)
+        grad_t[:, place] = turned.astype(bf16)
+        total = jnp.sum(turned[:HD] * heads_t[:, place], axis=0, keepdims=True)
+        row_dot[:, place] = jnp.broadcast_to(total, (8, tb))
+
+    fill_units(units, tb, store)
+    s_out.middle()
+    dq_t[...] = jnp.zeros_like(dq_t)
+
+    def outer(kb, carry):
+        k_at = pl.ds(pl.multiple_of(kb * KB, KB), KB)
+        dk[...] = jnp.zeros_like(dk)
+        dv[...] = jnp.zeros_like(dv)
+
+        def inner(qb, carry):
+            q_at = pl.ds(pl.multiple_of(qb * QB, QB), QB)
+            scores = dot(keys[k_at], query_t[:, q_at])
+            seen = allowed_block(kb * KB, qb * QB, low[0:1, q_at])
+            probs = jnp.where(seen, jnp.exp(scores - lse[0:1, q_at]), 0.0)
+            prob_grad = dot(value[k_at], grad_t[:, q_at])
+            score_grad = (probs * (prob_grad - row_dot[0:1, q_at])).astype(bf16)
+            dv[...] += dot(probs.astype(bf16), grad[q_at])
+            dk[...] += dot(score_grad, query[q_at])
+            dq_t[:, q_at] += dot(key_t[:, k_at], score_grad)
+            return carry
+
+        lax.fori_loop(kb // (QB // KB), seq // QB, inner, 0)
+        low_lane = lane_of((KB, LANES)) < HD
+        stage[kb, 0:tb] = jnp.where(low_lane, 0.0, swap_halves(dk[...])).astype(bf16)
+        stage[kb, tb:] = pack_rows(dv[...]).astype(bf16)
+        return carry
+
+    lax.fori_loop(0, seq // KB, outer, 0)
+
+    def turn_query(block, carry):
+        place = pl.ds(pl.multiple_of(block * tb, tb), tb)
+        columns = dq_t[:, place] * HD ** (-0.5)
+        turned = jnp.transpose(jnp.concatenate([columns, jnp.zeros_like(columns)], axis=0))
+        low_lane = lane_of(turned.shape) < HD
+        stage[block, 0:tb] = jnp.where(low_lane, turned, stage[block, 0:tb].astype(f32)).astype(bf16)
+        return carry
+
+    lax.fori_loop(0, n_b, turn_query, 0)
+    got = [net.push(stage.at[b ^ off], returned.at[b], u, b ^ off) for off in range(1, n_b)]
+    returned[b] = stage[b]
+    dwo[...] = s_out.finish()
+    arrive(got)
+
+    wide = heads * LANES
+    for s in range(seqs):
+        for head in range(heads):
+            tile = returned[s * heads + head, 0:tb].astype(f32)
+            turned = tile * cosr[s] - partner(tile) * sinr[s]
+            raw[s, :, head * LANES : (head + 1) * LANES] = turned.astype(bf16)
+        for pair in range(heads // 2):
+            one = unpack_rows(returned[s * heads + 2 * pair, tb:].astype(f32))
+            two = unpack_rows(returned[s * heads + 2 * pair + 1, tb:].astype(f32))
+            both = 0.5 * jnp.where(lane_of(one.shape) < HD, one, swap_halves(two))
+            raw[s, :, wide + pair * LANES : wide + (pair + 1) * LANES] = both.astype(bf16)
+    got_v = [net.push(raw.at[:, part(v), pl.ds(wide, gv.shape[3])], gv.at[u], v, b) for v in others]
+    gv[u] = raw[:, slab, wide:]
+
+    def back(s, carry):
+        left = raw[s]
+        for v in range(n_u):
+            lanes = slice(v * 256, (v + 1) * 256)
+            found = dot_nt(left, wq[v])
+            gin_part[s, :, lanes] = found
+            gin_low[s, :, lanes] = found.astype(bf16)
+        return carry
+
+    lax.fori_loop(0, seqs, back, 0)
+    got_g = [net.push(gin_low.at[:, part(v)], landed.at[u], v, b) for v in others]
+    columns = raw.shape[2]
+    for v in range(n_u):
+        left = normed[:, :, v * 256 : (v + 1) * 256].reshape(seqs * tb, 256)
+        found = dot_tn(left, raw[...].reshape(seqs * tb, columns))
+        wq_buf[:, :, v] = found.astype(bf16).reshape(n_z, 2, rows, columns)
+    s_qkv = Scatter(net, u, b, n_b, lambda z, c: wq_buf.at[z, c], lambda z: wq_pair.at[z], wq_sum, wq_land)
+    s_qkv.middle()
+
+    arrive(got_g)
+    sums_own[...] = sums_in[...]
+    for s in range(seqs):
+        grad_normed = gin_part[s, slab]
+        for v in others:
+            grad_normed = grad_normed + landed[v, s].astype(f32)
+        own = x[s].astype(f32)
+        factor = lax.rsqrt(jnp.mean(own * own, axis=-1, keepdims=True) + epsilon)
+        hat = own * factor
+        scaled = grad_normed * gain[0:1, :]
+        inner = jnp.mean(scaled * hat, axis=-1, keepdims=True)
+        gin[s] = (ghid[s] + factor * (scaled - hat * inner)).astype(bf16)
+        sums_own[3:4] = sums_own[3:4] + jnp.sum(grad_normed * hat, axis=0, keepdims=True)
+    got_s = [net.push(sums_own, sums_u.at[u], v, b) for v in others]
+    arrive(got_s)
+    total = sums_own[...]
+    for v in others:
+        total = total + sums_u[v]
+    sums_ub[...] = total
+    got_s = [net.push(sums_ub, sums_b.at[b], u, b ^ off) for off in range(1, n_b)]
+    arrive(got_s)
+    for off in range(1, n_b):
+        total = total + sums_b[b ^ off]
+    sums[...] = total
+    arrive(got_v)
+    for v in range(n_u):
+        gvf[:, :, v * 256 : (v + 1) * 256] = gv[v]
+    wq_low[...] = s_qkv.finish().astype(bf16)
+    got = [net.push(wq_low.at[v], dwq.at[u], v, b) for v in others]
+    dwq[u] = wq_low[u]
+    arrive(got)
+    net.drain()
+
+
+def call(kernel, dims, name, collective_id, outs, scratch, copies, inputs):
+    vmem = pl.BlockSpec(memory_space=pltpu.VMEM)
+    return pl.pallas_call(
+        functools.partial(kernel, dims),
+        out_shape=[jax.ShapeDtypeStruct(shape, dtype) for shape, dtype in outs],
+        in_specs=[vmem] * len(inputs),
+        out_specs=[vmem] * len(outs),
+        scratch_shapes=[pltpu.VMEM(shape, dtype) for shape, dtype in scratch]
+        + [pltpu.SemaphoreType.DMA((copies,))] * 2,
+        compiler_params=pltpu.CompilerParams(
+            collective_id=collective_id, has_side_effects=True, vmem_limit_bytes=VMEM_BYTES
+        ),
+        name=name,
+    )(*inputs)
+
+
+def pad_to(values, axis, size):
+    widths = [(0, 0)] * values.ndim
+    widths[axis] = (0, size - values.shape[axis])
+    return jnp.pad(values, widths)
+
+
+def local_units(
+    inputs, v_first, grad_out, positions, segments,
+    w_query, w_key, w_value, w_out, w_gate, w_up, w_down, gain_attn, gain_ffn,
+    debug=None,
+):
+    n_u, n_b = lax.axis_size("ulysses"), lax.axis_size("blk")
+    u, b = here()
+    seqs, td, width = inputs.shape
+    rows = w_query.shape[0]
+    heads = HEADS // n_u
+    tb = n_u * td
+    seq = n_b * tb
+    ff_own = w_down.shape[0]
+    ff_pad = -(-ff_own // 32) * 32
+    ff = ff_pad * n_b
+    dims = (n_u, n_b, seqs, td, rows, heads)
+
+    place = jnp.arange(seq, dtype=jnp.int32)
+    cut = jnp.sum(1 - segments, axis=1, keepdims=True)
+    first = jnp.where(segments == 1, cut, 0)
+    low = lax.dynamic_slice_in_dim(first, b // heads, 1, 0)
+    low = jnp.broadcast_to(low, (8, seq))
+    local_place = (place[None, :] - first).astype(f32)
+    angle_rows = lax.dynamic_slice_in_dim(local_place, b * tb, tb, 1)
+    inverse = rope_base ** (-2.0 * jnp.arange(HD // 2, dtype=f32) / HD)
+    angles = angle_rows[:, :, None] * inverse
+    cosine, sine = jnp.cos(angles), jnp.sin(angles)
+    cosr = jnp.concatenate([cosine] * 4, axis=-1)
+    sinr = jnp.concatenate([-sine, sine] * 2, axis=-1)
+
+    qk = jnp.stack([w_query.reshape(rows, n_u, heads, HD), w_key.reshape(rows, n_u, heads, HD)], axis=3)
+    wqkv = jnp.concatenate(
+        [qk.reshape(rows, n_u, heads * 2 * HD), w_value.reshape(rows, n_u, heads * HD)], axis=2
+    )
+    wqkv = jnp.moveaxis(wqkv, 1, 0)
+
+    def hidden_columns(weight):
+        parted = pad_to(weight.reshape(rows, n_u, n_b, ff_own), 3, ff_pad)
+        return parted.reshape(rows, n_u, ff)
+
+    wgu = jnp.moveaxis(
+        jnp.concatenate([hidden_columns(w_gate), hidden_columns(w_up)], axis=2), 1, 0
+    )
+    wd = pad_to(w_down, 0, ff_pad)
+    vf = jnp.moveaxis(v_first.reshape(seqs, td, n_u, heads * HD), 2, 0)
+    pair = jnp.stack([gain_attn, gain_ffn]).astype(f32)
+    lane = (jnp.arange(LANES) // rows) == (u * n_b + b) % (LANES // rows)
+    gains = pad_to(jnp.where(lane[None, :], jnp.tile(pair, (1, LANES // rows)), 0.0), 0, 8)
+
+    columns = 3 * heads * HD
+    units, normed, wq, gog, wg1, gain = call(
+        kernel_project, dims, "project", 1,
+        [((n_b, tb + tb // 2, LANES), bf16), ((seqs, tb, width), bf16), ((n_u, n_b * rows, columns), bf16),
+         ((seqs, tb, width), bf16), ((n_u, rows, 2 * ff), bf16), ((8, width), f32)],
+        [((seqs, tb, width), bf16), ((seqs, tb, heads * HD), bf16), ((n_b, tb + tb // 2, LANES), bf16),
+         ((n_b, n_u, 8, LANES), f32)],
+        48,
+        [inputs, vf, grad_out, wqkv, wgu, gains, cosr, sinr],
+    )
+    hidden, nf, wg, wdg, wo, mix, heads_t, lse, sums = call(
+        kernel_attend, dims, "attend", 2,
+        [((seqs, td, width), f32), ((seqs, tb, width), bf16), ((n_u, n_b * rows, 2 * ff), bf16),
+         ((ff, width), bf16), ((n_b * rows, width), bf16), ((seqs, tb, heads * HD), bf16),
+         ((HD, seq), f32), ((8, seq), f32), ((8, width), f32)],
+        [((seq, LANES), bf16), ((LANES, seq), bf16), ((HD, seq), bf16), ((HD, QB), f32),
+         ((n_b, tb // 2, LANES), bf16), ((n_b, tb // 2, LANES), bf16), ((seqs, tb, width), f32),
+         ((seqs, tb, width), bf16), ((n_u, seqs, td, width), bf16), ((seqs, td, width), bf16)],
+        48,
+        [units, low, inputs, w_out, wg1, wd, gain],
+    )
+    n_z = n_b // 2
+    out, ghid, grads, dwd, dwgu, dwo_part, sums = call(
+        kernel_feed, dims, "feed", 3,
+        [((seqs, td, width), bf16), ((seqs, td, width), f32), ((n_b, tb // 2, LANES), bf16),
+         ((ff_pad, width), f32), ((n_u, rows, 2 * ff), bf16), ((n_z, 2, rows, width), bf16), ((8, width), f32)],
+        [((seqs, tb, ff), bf16), ((seqs, tb, 2 * ff), bf16),
+         ((seqs, tb, width), f32), ((seqs, tb, width), bf16), ((seqs, tb, width), f32), ((seqs, tb, width), bf16),
+         ((n_u, seqs, td, width), bf16), ((n_u, seqs, td, width), bf16),
+         ((seqs, td, width), bf16), ((seqs, tb, width), bf16), ((n_b, tb // 2, LANES), bf16),
+         ((n_z, 2, ff_pad, width), bf16), ((n_z, ff_pad, width), bf16), ((n_z, ff_pad, width), bf16),
+         ((n_z - 1, ff_pad, width), bf16),
+         ((n_z, 2, n_u, rows, 2 * ff), bf16), ((n_z, n_u, rows, 2 * ff), bf16), ((n_z, n_u, rows, 2 * ff), bf16),
+         ((n_z - 1, n_u, rows, 2 * ff), bf16), ((n_u, rows, 2 * ff), bf16)],
+        48,
+        [nf, gog, wg, wdg, wo, mix, hidden, gain, sums],
+    )
+    gin, gvf, dwq, dwo, sums = call(
+        kernel_back, dims, "back", 4,
+        [((seqs, td, width), bf16), ((seqs, td, width), bf16), ((n_u, rows, columns), bf16),
+         ((rows, width), f32), ((8, width), f32)],
+        [((seq, LANES), bf16), ((HD, seq), bf16), ((seq, LANES), bf16), ((LANES, seq), bf16),
+         ((seq, LANES), bf16), ((seq, LANES), bf16), ((LANES, seq), bf16), ((8, seq), f32), ((HD, seq), f32),
+         ((KB, LANES), f32), ((KB, LANES), f32), ((n_b, tb + tb // 2, LANES), bf16),
+         ((n_b, tb + tb // 2, LANES), bf16), ((seqs, tb, columns), bf16),
+         ((seqs, tb, width), f32), ((seqs, tb, width), bf16), ((n_u, seqs, td, width), bf16),
+         ((n_u, seqs, td, heads * HD), bf16),
+         ((n_z, 2, n_u, rows, columns), bf16), ((n_z, n_u, rows, columns), bf16),
+         ((n_z, n_u, rows, columns), bf16), ((n_z - 1, n_u, rows, columns), bf16), ((n_u, rows, columns), bf16),
+         ((n_z, rows, width), bf16), ((n_z, rows, width), bf16), ((n_z - 1, rows, width), bf16),
+         ((8, width), f32), ((n_u, 8, width), f32), ((8, width), f32), ((n_b, 8, width), f32)],
+        64,
+        [units, grads, heads_t, lse, low, normed, wq, cosr, sinr, ghid, inputs, gain, dwo_part, sums],
+    )
+    dwq = jnp.moveaxis(dwq.astype(f32), 0, 1)
+    dqk = dwq[:, :, : heads * 2 * HD].reshape(rows, n_u, heads, 2, HD)
+    grad_w_query = dqk[:, :, :, 0].reshape(rows, width)
+    grad_w_key = dqk[:, :, :, 1].reshape(rows, width)
+    grad_w_value = dwq[:, :, heads * 2 * HD :].reshape(rows, width)
+    dwgu = jnp.moveaxis(dwgu.astype(f32), 0, 1).reshape(rows, n_u, 2, n_b, ff_pad)[..., :ff_own]
+    grad_w_gate = dwgu[:, :, 0].reshape(rows, w_gate.shape[1])
+    grad_w_up = dwgu[:, :, 1].reshape(rows, w_gate.shape[1])
+    grad_w_down = dwd[:ff_own]
+    gain_at = (u * n_b + b) * rows
+    grad_gain_attn = lax.dynamic_slice_in_dim(sums[3], gain_at, rows, 0)
+    grad_gain_ffn = lax.dynamic_slice_in_dim(sums[4], gain_at, rows, 0)
+    statistics = jnp.sqrt(jnp.sum(sums[:3], axis=1) / (seqs * seq * width))
+    return (
+        out, gin, gvf, grad_w_query, grad_w_key, grad_w_value, dwo, grad_w_gate, grad_w_up, grad_w_down,
+        grad_gain_attn, grad_gain_ffn, statistics,
+    )
+
+
+def fits_units(mesh):
+    n_u, n_b = mesh.shape["ulysses"], mesh.shape["blk"]
+    return n_u == 4 and n_b == 8
+
+
 def solution(mesh):
     in_specs = (
         P(None, ("blk", "ulysses"), None),
@@ -454,4 +1215,5 @@
         P(("ulysses", "blk")),
         P(),
     )
-    return jax.shard_map(local, mesh=mesh, in_specs=in_specs, out_specs=out_specs, check_vma=False)
+    path = local_units if fits_units(mesh) else local
+    return jax.shard_map(path, mesh=mesh, in_specs=in_specs, out_specs=out_specs, check_vma=False)

time: 1460 us -> 336 us (0.23)
  waiting for transfers between devices: 1070 us -> 0 us
  Pallas kernels: 0 us -> 305 us
  local copies, waits for them, and re-layouts: 120 us -> 19.7 us
  blocking collectives: 98.9 us -> 0 us
  matrix products: 77.9 us -> 0 us
  starting transfers between devices: 22.7 us -> 0 us
  other arithmetic: 25.1 us -> 9.25 us
  loops' own time: 15 us -> 0 us
    reduce_scatter x4 -> x0, waiting for transfers between devices: 688 us -> none  [the longest x1 375 us: local(): lax.psum_scatter(jnp.concatenate([weight_grad(normed, grad_query_raw), we...]
    all_gather x9 -> x0, waiting for transfers between devices: 361 us -> none  [the longest x1 66.4 us: local(): lax.all_gather(w_up, ('ulysses', 'blk'), axis=0, tiled=True)]
    pallas_call x0 -> x4, Pallas kernels: none -> 305 us  [call(): pl.pallas_call(functools.partial(kernel, dims), out_shape=[jax.ShapeDtype...]
    dot_general x28 -> x0, matrix products: 77.9 us -> none  [the longest x7 29.2 us: weight_grad(): jnp.einsum('std,ste->de', activations, gradient, preferred_element_type=j...]
    concatenate x1 -> x0, local copies, waits for them, and re-layouts: 42.7 us -> none  [local(): jnp.concatenate([weight_grad(normed, grad_query_raw), weight_grad(normed,...]
    unnamed x1 -> x0, blocking collectives: 42.1 us -> none
    psum x1 -> x0, blocking collectives: 39.3 us -> none  [local(): lax.psum((jnp.sum(residual * residual), jnp.sum(attn_branch * attn_branch...]
    dynamic_slice x20 -> x3, local copies, waits for them, and re-layouts: 23.7 us -> 1.18 us  [the longest x1 0.58 us: local_units(): grad_gain_ffn = lax.dynamic_slice_in_dim(sums[4], gain_at, rows, 0)]
  transfers between devices with their start and end apart: 19 -> 0, of which waited for: 17 -> 0; matrix products, arithmetic and copies ran while one was open for 7% -> 0% of each run, Pallas kernels for 0% -> 0%
where the time goes in v1:
time: 336 us; the launch traced here: 335 us
  Pallas kernels  305 us (91%)
  local copies, waits for them, and re-layouts  19.7 us (6%)
  other arithmetic  9.25 us (3%)
    pallas_call x4, Pallas kernels, call(): pl.pallas_call(functools.partial(kernel, dims), out_shape=[jax.ShapeDtype...  305 us

profile of v1, /device:TPU:0, one launch (start us, length us, event | category | flops | bytes accessed | tf_op | source)
XLA Modules:
  0.0 335.4 jit_solution(5856016163121433708)
XLA Ops:
  0.7 0.9 subtract_reduce_fusion
  1.6 0.7 maximum_convert_fusion
  2.3 0.1 tile.10
  2.4 0.6 pad.17.gains
  3.0 0.8 compare_select_fusion
  3.8 0.6 broadcast_in_dim.41.low
  4.4 0.8 copy.51
  5.3 1.0 stack_reshape.6
  6.3 0.2 copy.35
  6.6 1.0 stack_reshape.7
  7.6 0.2 copy.36
  7.8 0.7 pad_maximum_fusion
  8.5 0.2 reshape.103
  8.7 0.7 maximum_bitcast_fusion.1.wqkv
  9.4 0.7 pad.18.wd
  10.1 0.7 copy.50
  10.8 0.6 reshape.105
  11.6 0.2 reshape.106
  11.8 0.6 reshape.107
  12.5 0.2 reshape.108
  12.7 0.8 maximum_bitcast_fusion.wgu
  13.5 1.0 fusion
  14.5 1.3 pad_maximum_fusion.1
  15.8 55.1 %project.1 = (bf16[8,384,128]{2,1,0:T(8,128)(2,1)}, bf16[2,256,1024]{2,1,0:T(8,128)(2,1)}, bf16[4,256,768]{2,1,0:T(8,128)(2,1)}, bf16[2,256,1024]{2,1,0:T(8,128)...) custom-call(bf16[2,64,1024]{2,1,0:T(8,128)(2,1)} %x.13, bf16[4,2,64,256]{3,2,1,0:T(8,128)(2,1)} %bitcast.55, ...), custom_call_target="tpu_custom_call" | custom-call | tf_op jit(solution)/shard_map/project/pallas_call | solution.py:1039
  70.9 101.0 %attend.1 = (f32[2,64,1024]{2,1,0:T(8,128)}, bf16[2,256,1024]{2,1,0:T(8,128)(2,1)}, bf16[4,256,1536]{2,1,0:T(8,128)(2,1)}, bf16[768,1024]{1,0:T(8,128)(2,1)}, bf...) custom-call(bf16[8,384,128]{2,1,0:T(8,128)(2,1)} %get-tuple-element., ...), custom_call_target="tpu_custom_call" | custom-call | tf_op jit(solution)/shard_map/attend/pallas_call | solution.py:1039
  171.9 72.8 %feed.1 = (bf16[2,64,1024]{2,1,0:T(8,128)(2,1)}, f32[2,64,1024]{2,1,0:T(8,128)}, bf16[8,128,128]{2,1,0:T(8,128)(2,1)}, f32[96,1024]{1,0:T(8,128)}, bf16[4,32,153...) custom-call(bf16[2,256,1024]{2,1,0:T(8,128)(2,1)} %get-tuple-element.43.nf, ...), custom_call_target="tpu_custom_call" | custom-call | tf_op jit(solution)/shard_map/feed/pallas_call | solution.py:1039
  244.7 76.5 %back.1 = (bf16[2,64,1024]{2,1,0:T(8,128)(2,1)}, bf16[2,64,1024]{2,1,0:T(8,128)(2,1)}, bf16[4,32,768]{2,1,0:T(8,128)(2,1)}, f32[32,1024]{1,0:T(8,128)}, f32[8,1024]{1,0:T(8,128)}) custom-call(bf16[8,384,128]{2,1,0:T(8,128)(2,1)} %get-tuple-element.40.units, bf16[8,128,128]{2,1,0:T(8,128)(2,1)} %get-tuple-element.52.grads, ...), custom_call_target="tpu_custom_call" | custom-call | tf_op jit(solution)/shard_map/back/pallas_call | solution.py:1039
  321.3 0.9 slice_reduce_fusion
  322.2 0.8 fusion.7
  323.0 0.6 fusion.4
  323.6 0.6 fusion.3
  324.2 0.5 multiply_sqrt_fusion
  324.7 0.8 slice.39
  325.5 1.0 convert_bitcast_fusion.1
  326.5 0.7 copy.47
  327.1 0.4 reshape.109
  327.5 0.4 fusion.6
  328.0 0.9 reshape_squeeze.13
  328.9 0.9 reshape_squeeze.12
  329.8 0.1 convert_bitcast_fusion
  329.9 0.3 reshape.114
  330.3 0.1 fusion.5
  330.4 1.0 reshape_squeeze.15
  331.5 1.0 reshape_squeeze.14
  332.6 0.7 copy.56
  333.3 0.7 copy.57
  334.0 0.7 copy.58
  334.7 0.7 copy.59
  (36 shorter events, 0.5 us)
Async XLA Ops:
  0.6 8.8 %copy-start.8 = (bf16[88,1024]{1,0:T(8,128)(2,1)S(1)}, bf16[88,1024]{1,0:T(8,128)(2,1)}, u32[]{:S(2)}) copy-start(bf16[88,1024]{1,0:T(8,128)(2,1)} %param.24) | copy-start | bytes 540676
  5.3 4.8 %copy-start.2 = (bf16[2,64,1024]{2,1,0:T(8,128)(2,1)S(1)}, bf16[2,64,1024]{2,1,0:T(8,128)(2,1)}, u32[]{:S(2)}) copy-start(bf16[2,64,1024]{2,1,0:T(8,128)(2,1)} %param.15) | copy-start | bytes 786436
  6.5 4.3 %copy-start.6 = (bf16[32,2816]{1,0:T(8,128)(2,1)S(1)}, bf16[32,2816]{1,0:T(8,128)(2,1)}, u32[]{:S(2)}) copy-start(bf16[32,2816]{1,0:T(8,128)(2,1)} %param.22) | copy-start | bytes 540676
  8.7 3.1 copy-start.7
  244.7 80.0 %copy-start.1 = (f32[96,1024]{1,0:T(8,128)S(1)}, f32[96,1024]{1,0:T(8,128)}, u32[]{:S(2)}) copy-start(f32[96,1024]{1,0:T(8,128)} %get-tuple-element.65) | copy-start | bytes 1179652
  327.5 2.3 copy-start
  330.4 2.2 copy-start.3
  330.4 2.9 copy-start.5
  331.5 2.5 copy-start.4
  331.5 3.2 copy-start.9

commit v2 on v0

--- a/solution.py
+++ b/solution.py
@@ -1,6 +1,11 @@
+import functools
+import types
+
 import jax
 import jax.numpy as jnp
 from jax import lax
+from jax.experimental import pallas as pl
+from jax.experimental.pallas import tpu as pltpu
 from jax.sharding import PartitionSpec as P
 
 HEADS = 16
@@ -422,6 +427,734 @@
     )
 
 
+MESH = pl.DeviceIdType.MESH
+LANES = 128
+VMEM_BYTES = 61 << 20
+f32 = jnp.float32
+bf16 = jnp.bfloat16
+QB, KB = 512, 256
+
+
+class Copy:
+    def __init__(self, copy, send_at, recv_at, when):
+        self.copy, self.at, self.recv_at, self.when = copy, send_at, recv_at, when
+
+    def wait_recv(self):
+        self.copy.wait_recv()
+
+    def wait_send(self):
+        if self.when is None:
+            self.copy.wait_send()
+        else:
+            pl.when(self.when)(self.copy.wait_send)
+
+
+class Net:
+    def __init__(self, send_sems, recv_sems):
+        self.send_sems, self.recv_sems = send_sems, recv_sems
+        self.count, self.open = 0, []
+
+    def push(self, src, dst, u, b, when=None, recv_at=None, at=None):
+        if at is None:
+            at = self.count
+            self.count += 1
+        recv_at = at if recv_at is None else recv_at
+        copy = pltpu.make_async_remote_copy(
+            src_ref=src,
+            dst_ref=dst,
+            send_sem=self.send_sems.at[at],
+            recv_sem=self.recv_sems.at[recv_at],
+            device_id=(u, b),
+            device_id_type=MESH,
+        )
+        if when is None:
+            copy.start()
+        else:
+            pl.when(when)(copy.start)
+        made = Copy(copy, at, recv_at, when)
+        self.open.append(made)
+        return made
+
+    def sent(self, copies):
+        for copy in copies:
+            copy.wait_send()
+        self.open = [copy for copy in self.open if copy not in copies]
+
+    def drain(self):
+        for copy in self.open:
+            copy.wait_send()
+        self.open = []
+
+
+def arrive(copies):
+    for copy in copies:
+        copy.wait_recv()
+
+
+def here():
+    return lax.axis_index("ulysses"), lax.axis_index("blk")
+
+
+def greet(u, b, n_u, n_b):
+    barrier = pltpu.get_barrier_semaphore()
+    for off in range(1, n_u):
+        pl.semaphore_signal(barrier, inc=1, device_id=(u ^ off, b), device_id_type=MESH)
+    for off in range(1, n_b):
+        pl.semaphore_signal(barrier, inc=1, device_id=(u, b ^ off), device_id_type=MESH)
+    pl.semaphore_wait(barrier, n_u - 1 + n_b - 1)
+
+
+def dot(left, right):
+    return jnp.dot(left, right, preferred_element_type=f32)
+
+
+def dot_nt(left, right):
+    return lax.dot_general(left, right, (((1,), (1,)), ((), ())), preferred_element_type=f32)
+
+
+def dot_tn(left, right):
+    return lax.dot_general(left, right, (((0,), (0,)), ((), ())), preferred_element_type=f32)
+
+
+def at_block(index, size):
+    return pl.ds(pl.multiple_of(index * size, size), size)
+
+
+def lane_of(shape):
+    return lax.broadcasted_iota(jnp.int32, shape, len(shape) - 1)
+
+
+def swap_halves(tile):
+    return pltpu.roll(tile, HD, tile.ndim - 1)
+
+
+def partner(tile):
+    low = lane_of(tile.shape) % HD < HD // 2
+    return jnp.where(low, pltpu.roll(tile, LANES - HD // 2, 1), pltpu.roll(tile, HD // 2, 1))
+
+
+def pack_rows(rows):
+    half = rows.shape[0] // 2
+    low = lane_of((half, LANES)) < HD
+    return jnp.where(low, rows[:half], swap_halves(rows[half:]))
+
+
+def unpack_rows(packed):
+    return jnp.concatenate([packed, swap_halves(packed)], axis=0)
+
+
+class Gather:
+    def __init__(self, net, slot, u, b):
+        self.net, self.slot, self.u, self.b = net, slot, u, b
+        self.inner = ((b // 2) == 1) | ((b // 2) == 2)
+        mine = slot(b)
+        self.two = net.push(mine, mine, u, b ^ 4)
+        self.one = net.push(mine, mine, u, b ^ 2)
+        self.three = net.push(mine, mine, u, b ^ 6, when=self.inner)
+        self.side = [net.push(mine, mine, u, b ^ 1)]
+
+    def beside(self, owner):
+        got = self.slot(owner)
+        self.side.append(self.net.push(got, got, self.u, self.b ^ 1))
+
+    def forward(self):
+        self.two.wait_recv()
+        got = self.slot(self.b ^ 4)
+        self.net.push(got, got, self.u, self.b ^ 2, when=self.inner, recv_at=self.three.at)
+        self.beside(self.b ^ 4)
+
+    def relay(self):
+        self.one.wait_recv()
+        self.beside(self.b ^ 2)
+        self.three.wait_recv()
+        self.beside(self.b ^ 6)
+
+    def finish(self):
+        arrive(self.side)
+
+
+class Scatter:
+    def __init__(self, net, u, b, mine, paired, summed, landed):
+        self.net, self.u, self.b = net, u, b
+        self.mine, self.paired, self.summed, self.landed = mine, paired, summed, landed
+        self.z = b // 2
+        self.inner = (self.z == 1) | (self.z == 2)
+        self.swap = [net.push(mine(z, 1 - b % 2), paired.at[z], u, b ^ 1) for z in range(4)]
+
+    def add(self, z):
+        self.summed[z] = (self.mine(z, self.b % 2)[...].astype(f32) + self.paired[z].astype(f32)).astype(bf16)
+
+    def middle(self):
+        net, u, b, z, inner = self.net, self.u, self.b, self.z, self.inner
+        outer = jnp.logical_not(inner)
+        arrive(self.swap)
+        self.add(z ^ 3)
+        far = self.summed.at[z ^ 3]
+        self.extra = net.push(far, self.landed.at[3], u, b ^ 2, when=outer)
+        self.three = net.push(far, self.landed.at[2], u, b ^ 6, when=inner)
+        self.add(z ^ 2)
+        self.two = net.push(self.summed.at[z ^ 2], self.landed.at[1], u, b ^ 4, when=outer)
+        self.add(z ^ 1)
+        self.one = net.push(self.summed.at[z ^ 1], self.landed.at[0], u, b ^ 2)
+        self.add(z)
+
+    def merge(self):
+        net, u, b, z = self.net, self.u, self.b, self.z
+
+        @pl.when(self.inner)
+        def _():
+            self.extra.wait_recv()
+            self.summed[z ^ 2] = (self.summed[z ^ 2].astype(f32) + self.landed[3].astype(f32)).astype(bf16)
+
+        net.push(self.summed.at[z ^ 2], self.landed.at[1], u, b ^ 4, when=self.inner, at=self.two.at)
+
+    def finish(self, total):
+        self.one.wait_recv()
+        self.two.wait_recv()
+        total[...] = (
+            self.summed[self.z].astype(f32) + self.landed[0].astype(f32) + self.landed[1].astype(f32)
+        ).astype(total.dtype)
+
+        @pl.when(self.inner)
+        def _():
+            self.three.wait_recv()
+            total[...] = (total[...].astype(f32) + self.landed[2].astype(f32)).astype(total.dtype)
+
+
+def fill_units(units, tb, store):
+    def one(block, carry):
+        low = lane_of((tb, LANES)) < HD
+        tile = units[block, 0:tb].astype(f32)
+        query = jnp.where(low, tile * HD ** (-0.5), 0.0)
+        key = jnp.where(low, swap_halves(tile), 0.0)
+        value = jnp.where(low, unpack_rows(units[block, tb:].astype(f32)), 0.0)
+        store(block, query, key, value)
+        return carry
+
+    lax.fori_loop(0, units.shape[0], one, 0)
+
+
+def allowed_block(first_key, first_query, low_row):
+    key_place = first_key + lax.broadcasted_iota(jnp.int32, (KB, QB), 0)
+    query_place = first_query + lax.broadcasted_iota(jnp.int32, (KB, QB), 1)
+    return (key_place <= query_place) & (key_place >= low_row)
+
+
+def layer_kernel(dims, names, *refs):
+    n_u, n_b, seqs, td, rows, heads = dims
+    r = types.SimpleNamespace(**dict(zip(names, refs)))
+    tb = n_u * td
+    tokens = seqs * tb
+    seq = n_b * tb
+    n_z = n_b // 2
+    width = r.x.shape[2]
+    u, b = here()
+    net = Net(r.send_sems, r.recv_sems)
+    others = [u ^ off for off in range(1, n_u)]
+    slab = at_block(u, td)
+    mine = at_block(b, rows)
+    ff = r.wdg.shape[0]
+    ff_rows = ff // n_b
+
+    def part(v):
+        return at_block(v, td)
+
+    greet(u, b, n_u, n_b)
+    got_w = [net.push(r.wqkv.at[v], r.wq.at[u, mine], v, b) for v in others]
+    got_g = [net.push(r.gains, r.gbuf.at[b, u], v, b) for v in others]
+    r.wo[mine] = r.wout[...]
+    g_out = Gather(net, lambda c: r.wo.at[at_block(c, rows)], u, b)
+    got_x = [net.push(r.x, r.xg.at[:, slab], v, b) for v in others]
+    r.wq[u, mine] = r.wqkv[u]
+    r.gbuf[b, u] = r.gains[...]
+    r.xg[:, slab] = r.x[...]
+    r.vfg[:, slab] = r.vf[u]
+    r.gog[:, slab] = r.go[...]
+    arrive(got_w)
+    g_qkv = Gather(net, lambda c: r.wq.at[:, at_block(c, rows)], u, b)
+    arrive(got_g)
+    got_g = [net.push(r.gbuf.at[b], r.gbuf.at[b], u, b ^ off) for off in range(1, n_b)]
+    got_v = [net.push(r.vf.at[v], r.vfg.at[:, slab], v, b) for v in others]
+    r.wg[u, mine] = r.wgu[u]
+    got_o = [net.push(r.wgu.at[v], r.wg.at[u, mine], v, b) for v in others]
+    arrive(got_g)
+    per_tile = LANES // rows
+    for tile in range(n_u * n_b // per_tile):
+        total = None
+        for index in range(tile * per_tile, (tile + 1) * per_tile):
+            term = r.gbuf[index % n_b, index // n_b]
+            total = term if total is None else total + term
+        r.gain[:, tile * LANES : (tile + 1) * LANES] = total
+    arrive(got_x)
+
+    def norm(step, carry):
+        s, place = step // 2, at_block(step % 2, tb // 2)
+        values = r.xg[s, place].astype(f32)
+        factor = lax.rsqrt(jnp.mean(values * values, axis=-1, keepdims=True) + epsilon)
+        r.normed[s, place] = (values * factor * r.gain[0:1, :]).astype(bf16)
+        return carry
+
+    lax.fori_loop(0, 2 * seqs, norm, 0)
+    got_go = [net.push(r.go, r.gog.at[:, slab], v, b) for v in others]
+    g_out.forward()
+    g_qkv.forward()
+    arrive(got_v)
+    g_qkv.relay()
+    g_qkv.finish()
+
+    for s in range(seqs):
+        left = r.normed[s]
+        for n in range(heads // 2):
+            found = dot(left, r.wq[:, :, n * 256 : (n + 1) * 256].reshape(width, 256))
+            for i in range(2):
+                tile = found[:, i * LANES : (i + 1) * LANES]
+                turned = tile * r.cosr[s] + partner(tile) * r.sinr[s]
+                r.stage[s * heads + 2 * n + i, 0:tb] = turned.astype(bf16)
+        for n in range(heads // 4):
+            first_lane = heads * LANES + n * 256
+            found = dot(left, r.wq[:, :, first_lane : first_lane + 256].reshape(width, 256))
+            for i in range(2):
+                first = r.vfg[s, :, n * 256 + i * LANES : n * 256 + (i + 1) * LANES].astype(f32)
+                value = 0.5 * found[:, i * LANES : (i + 1) * LANES] + 0.5 * first
+                unit = s * heads + 4 * n + 2 * i
+                r.stage[unit, tb:] = pack_rows(value).astype(bf16)
+                r.stage[unit + 1, tb:] = pack_rows(swap_halves(value)).astype(bf16)
+    got_q = [net.push(r.stage.at[b ^ off], r.units.at[b], u, b ^ off) for off in range(n_b - 1, 0, -1)]
+    r.units[b] = r.stage[b]
+    r.wdg[at_block(b, ff_rows)] = r.wd[...]
+    g_out.relay()
+    arrive(got_q)
+    g_out.finish()
+
+    g_down = Gather(net, lambda c: r.wdg.at[at_block(c, ff_rows)], u, b)
+
+    def store(block, query, key, value):
+        place = at_block(block, tb)
+        r.keys[place] = key.astype(bf16)
+        r.key_t[:, place] = jnp.transpose(key)[:HD].astype(bf16)
+        r.query[place] = query.astype(bf16)
+        r.query_t[:, place] = jnp.transpose(query).astype(bf16)
+        r.value[place] = value.astype(bf16)
+        r.value_t[:, place] = jnp.transpose(value)[:HD].astype(bf16)
+
+    fill_units(r.units, tb, store)
+
+    def attend(qb, carry):
+        q_at = at_block(qb, QB)
+        query = r.query_t[:, q_at]
+        low_row = r.low[0:1, q_at]
+        r.acc[...] = jnp.zeros_like(r.acc)
+
+        def inner(kb, state):
+            best, total = state
+            k_at = at_block(kb, KB)
+            scores = dot(r.keys[k_at], query)
+            scores = jnp.where(allowed_block(kb * KB, qb * QB, low_row), scores, neg_big)
+            new_best = jnp.maximum(best, jnp.max(scores, axis=0, keepdims=True))
+            weights = jnp.exp(scores - new_best)
+            rescale = jnp.exp(best - new_best)
+            total = total * rescale + jnp.sum(weights, axis=0, keepdims=True)
+            r.acc[...] = r.acc[...] * rescale + dot(r.value_t[:, k_at], weights.astype(bf16))
+            return new_best, total
+
+        start = (jnp.full((1, QB), neg_big, f32), jnp.zeros((1, QB), f32))
+        best, total = lax.fori_loop(0, (qb + 1) * (QB // KB), inner, start)
+        out = r.acc[...] / total
+        r.heads_t[:, q_at] = out
+        r.lse[:, q_at] = jnp.broadcast_to(best + jnp.log(total), (8, QB))
+        turned = jnp.transpose(jnp.concatenate([out, jnp.zeros_like(out)], axis=0))
+        for i in range(QB // tb):
+            r.ostage[qb * (QB // tb) + i] = pack_rows(turned[i * tb : (i + 1) * tb]).astype(bf16)
+        return carry
+
+    lax.fori_loop(0, seq // QB, attend, 0)
+    got = [net.push(r.ostage.at[b ^ off], r.parts.at[b], u, b ^ off) for off in range(n_b - 1, 0, -1)]
+    r.parts[b] = r.ostage[b]
+    g_down.forward()
+    arrive(got)
+    arrive(got_o)
+    g_gate = Gather(net, lambda c: r.wg.at[:, at_block(c, rows)], u, b)
+    half = tb // 2
+    for s in range(seqs):
+        for pair in range(heads // 2):
+            one = r.parts[s * heads + 2 * pair].astype(f32)
+            two = r.parts[s * heads + 2 * pair + 1].astype(f32)
+            low_lane = lane_of(one.shape) < HD
+            lanes = slice(pair * LANES, (pair + 1) * LANES)
+            r.mix[s, :half, lanes] = jnp.where(low_lane, one, swap_halves(two)).astype(bf16)
+            r.mix[s, half:, lanes] = jnp.where(low_lane, swap_halves(one), two).astype(bf16)
+
+    def project_out(s, carry):
+        r.branch[s] = dot(r.mix[s], r.wo[...]).astype(bf16)
+        return carry
+
+    lax.fori_loop(0, seqs, project_out, 0)
+    got = [net.push(r.branch.at[:, part(v)], r.landed_b.at[u], v, b) for v in others]
+    r.landed_b[u] = r.branch[:, slab]
+    g_down.relay()
+    arrive(got)
+    r.sums[...] = jnp.zeros_like(r.sums)
+    for s in range(seqs):
+        total = sum(r.landed_b[v, s].astype(f32) for v in range(n_u))
+        own = r.x[s].astype(f32)
+        hid = own + total
+        r.hidden[s] = hid
+        factor = lax.rsqrt(jnp.mean(hid * hid, axis=-1, keepdims=True) + epsilon)
+        r.nf_own[s] = (hid * factor * r.gain[1:2, :]).astype(bf16)
+        r.sums[0:1] = r.sums[0:1] + jnp.sum(own * own, axis=0, keepdims=True)
+        r.sums[1:2] = r.sums[1:2] + jnp.sum(total * total, axis=0, keepdims=True)
+    got = [net.push(r.nf_own, r.nf.at[:, slab], v, b) for v in others]
+    r.nf[:, slab] = r.nf_own[...]
+    arrive(got_go)
+    g_down.finish()
+    g_gate.forward()
+    g_gate.relay()
+    arrive(got)
+    g_gate.finish()
+
+    def hidden_units(s, carry):
+        left = r.nf[s]
+        grad = r.gog[s]
+        for n in range(ff // 256):
+            span = slice(n * 256, (n + 1) * 256)
+            up_span = slice(ff + n * 256, ff + (n + 1) * 256)
+            gate = dot(left, r.wg[:, :, span].reshape(width, 256))
+            up = dot(left, r.wg[:, :, up_span].reshape(width, 256))
+            grad_act = dot_nt(grad, r.wdg[span])
+            sig = 1.0 / (1.0 + jnp.exp(-gate))
+            silu = gate * sig
+            r.act[s, :, span] = (silu * up).astype(bf16)
+            r.dgu[s, :, span] = (grad_act * up * sig * (1.0 + gate * (1.0 - sig))).astype(bf16)
+            r.dgu[s, :, up_span] = (grad_act * silu).astype(bf16)
+        return carry
+
+    lax.fori_loop(0, seqs, hidden_units, 0)
+
+    def back_units(s, carry):
+        left = r.dgu[s]
+        for v in range(n_u):
+            r.d_low[s, :, v * 256 : (v + 1) * 256] = dot_nt(left, r.wg[v]).astype(bf16)
+        return carry
+
+    lax.fori_loop(0, seqs, back_units, 0)
+    got_d = [net.push(r.d_low.at[:, part(v)], r.landed_d.at[u], v, b) for v in others]
+    r.landed_d[u] = r.d_low[:, slab]
+
+    half_units = ff // 2
+    for n in range(2):
+        span = slice(n * half_units, (n + 1) * half_units)
+        found = dot_tn(r.act[:, :, span].reshape(tokens, half_units), r.gog[...].reshape(tokens, width))
+        r.wd_buf[n * (n_z // 2) : (n + 1) * (n_z // 2)] = found.astype(bf16).reshape(
+            n_z // 2, 2, ff_rows, width
+        )
+    s_down = Scatter(net, u, b, lambda z, c: r.wd_buf.at[z, c], r.wd_pair, r.wd_sum, r.wd_land)
+    for v in range(n_u):
+        left = r.nf[:, :, v * 256 : (v + 1) * 256].reshape(tokens, 256)
+        found = dot_tn(left, r.dgu[...].reshape(tokens, 2 * ff))
+        r.wg_buf[:, :, v] = found.astype(bf16).reshape(n_z, 2, rows, 2 * ff)
+        if v == 1:
+            s_down.middle()
+    s_gate = Scatter(net, u, b, lambda z, c: r.wg_buf.at[z, c], r.wg_pair, r.wg_sum, r.wg_land)
+
+    arrive(got_d)
+    for s in range(seqs):
+        grad_normed = sum(r.landed_d[v, s].astype(f32) for v in range(n_u))
+        hid = r.hidden[s]
+        factor = lax.rsqrt(jnp.mean(hid * hid, axis=-1, keepdims=True) + epsilon)
+        hat = hid * factor
+        scaled = grad_normed * r.gain[1:2, :]
+        inner = jnp.mean(scaled * hat, axis=-1, keepdims=True)
+        total = r.go[s].astype(f32) + factor * (scaled - hat * inner)
+        r.ghid[s] = total
+        r.gb_own[s] = total.astype(bf16)
+        r.sums[4:5] = r.sums[4:5] + jnp.sum(grad_normed * hat, axis=0, keepdims=True)
+    got_b = [net.push(r.gb_own, r.gb.at[:, slab], v, b) for v in others]
+    r.gb[:, slab] = r.gb_own[...]
+    s_down.merge()
+
+    def forward(s, carry):
+        r.f_low[s] = dot(r.act[s], r.wdg[...]).astype(bf16)
+        return carry
+
+    lax.fori_loop(0, seqs, forward, 0)
+    arrive(got_b)
+    for s in range(seqs):
+        for pair in range(heads // 2):
+            found = dot_nt(r.gb[s], r.wo[pair * LANES : (pair + 1) * LANES])
+            r.ostage2[s * heads + 2 * pair] = pack_rows(found).astype(bf16)
+            r.ostage2[s * heads + 2 * pair + 1] = pack_rows(swap_halves(found)).astype(bf16)
+    got_u = [net.push(r.ostage2.at[b ^ off], r.grads.at[b], u, b ^ off) for off in range(n_b - 1, 0, -1)]
+    r.grads[b] = r.ostage2[b]
+    got_f = [net.push(r.f_low.at[:, part(v)], r.landed_f.at[u], v, b) for v in others]
+    r.landed_f[u] = r.f_low[:, slab]
+    found = dot_tn(r.mix[...].reshape(tokens, heads * HD), r.gb[...].reshape(tokens, width))
+    r.wo_buf[...] = found.astype(bf16).reshape(n_z, 2, rows, width)
+    s_out = Scatter(net, u, b, lambda z, c: r.wo_buf.at[z, c], r.wo_pair, r.wo_sum, r.wo_land)
+    arrive(got_u)
+    s_gate.middle()
+
+    def more(block, carry):
+        place = at_block(block, tb)
+        g = unpack_rows(r.grads[block].astype(f32))
+        g = jnp.where(lane_of(g.shape) < HD, g, 0.0)
+        r.grad[place] = g.astype(bf16)
+        turned = jnp.transpose(g)
+        r.grad_t[:, place] = turned.astype(bf16)
+        total = jnp.sum(turned[:HD] * r.heads_t[:, place], axis=0, keepdims=True)
+        r.row_dot[:, place] = jnp.broadcast_to(total, (8, tb))
+        return carry
+
+    lax.fori_loop(0, n_b, more, 0)
+    r.dq_t[...] = jnp.zeros_like(r.dq_t)
+    net.sent(got_q)
+
+    def outer(kb, carry):
+        k_at = at_block(kb, KB)
+        r.dk[...] = jnp.zeros_like(r.dk)
+        r.dv[...] = jnp.zeros_like(r.dv)
+
+        def inner(qb, carry):
+            q_at = at_block(qb, QB)
+            scores = dot(r.keys[k_at], r.query_t[:, q_at])
+            seen = allowed_block(kb * KB, qb * QB, r.low[0:1, q_at])
+            probs = jnp.where(seen, jnp.exp(scores - r.lse[0:1, q_at]), 0.0)
+            prob_grad = dot(r.value[k_at], r.grad_t[:, q_at])
+            score_grad = (probs * (prob_grad - r.row_dot[0:1, q_at])).astype(bf16)
+            r.dv[...] += dot(probs.astype(bf16), r.grad[q_at])
+            r.dk[...] += dot(score_grad, r.query[q_at])
+            r.dq_t[:, q_at] += dot(r.key_t[:, k_at], score_grad)
+            return carry
+
+        lax.fori_loop(kb // (QB // KB), seq // QB, inner, 0)
+        low_lane = lane_of((KB, LANES)) < HD
+        r.stage[kb, 0:tb] = jnp.where(low_lane, 0.0, swap_halves(r.dk[...])).astype(bf16)
+        r.stage[kb, tb:] = pack_rows(r.dv[...]).astype(bf16)
+        return carry
+
+    lax.fori_loop(0, seq // KB, outer, 0)
+
+    def turn_query(block, carry):
+        columns = r.dq_t[:, at_block(block, tb)] * HD ** (-0.5)
+        turned = jnp.transpose(jnp.concatenate([columns, jnp.zeros_like(columns)], axis=0))
+        low_lane = lane_of(turned.shape) < HD
+        r.stage[block, 0:tb] = jnp.where(low_lane, turned, r.stage[block, 0:tb].astype(f32)).astype(bf16)
+        return carry
+
+    lax.fori_loop(0, n_b, turn_query, 0)
+    got = [net.push(r.stage.at[b ^ off], r.returned.at[b], u, b ^ off) for off in range(n_b - 1, 0, -1)]
+    r.returned[b] = r.stage[b]
+    s_gate.merge()
+    s_out.middle()
+    arrive(got_f)
+    for s in range(seqs):
+        total = r.hidden[s] + sum(r.landed_f[v, s].astype(f32) for v in range(n_u))
+        r.out[s] = total.astype(bf16)
+        r.sums[2:3] = r.sums[2:3] + jnp.sum(total * total, axis=0, keepdims=True)
+    s_down.finish(r.dwd)
+    arrive(got)
+
+    wide = heads * LANES
+    for s in range(seqs):
+        for head in range(heads):
+            tile = r.returned[s * heads + head, 0:tb].astype(f32)
+            turned = tile * r.cosr[s] - partner(tile) * r.sinr[s]
+            r.raw[s, :, head * LANES : (head + 1) * LANES] = turned.astype(bf16)
+        for pair in range(heads // 2):
+            one = unpack_rows(r.returned[s * heads + 2 * pair, tb:].astype(f32))
+            two = unpack_rows(r.returned[s * heads + 2 * pair + 1, tb:].astype(f32))
+            both = 0.5 * jnp.where(lane_of(one.shape) < HD, one, swap_halves(two))
+            r.raw[s, :, wide + pair * LANES : wide + (pair + 1) * LANES] = both.astype(bf16)
+    columns = r.raw.shape[2]
+    for v in range(n_u):
+        left = r.normed[:, :, v * 256 : (v + 1) * 256].reshape(tokens, 256)
+        found = dot_tn(left, r.raw[...].reshape(tokens, columns))
+        r.wq_buf[:, :, v] = found.astype(bf16).reshape(n_z, 2, rows, columns)
+    s_qkv = Scatter(net, u, b, lambda z, c: r.wq_buf.at[z, c], r.wq_pair, r.wq_sum, r.wq_land)
+    s_out.merge()
+
+    def back_inputs(s, carry):
+        left = r.raw[s]
+        for v in range(n_u):
+            r.gin_low[s, :, v * 256 : (v + 1) * 256] = dot_nt(left, r.wq[v]).astype(bf16)
+        return carry
+
+    lax.fori_loop(0, seqs, back_inputs, 0)
+    got_g = [net.push(r.gin_low.at[:, part(v)], r.landed_g.at[u], v, b) for v in others]
+    r.landed_g[u] = r.gin_low[:, slab]
+    s_qkv.middle()
+    got_v = [net.push(r.raw.at[:, part(v), pl.ds(wide, heads * HD)], r.gv.at[u], v, b) for v in others]
+    r.gv[u] = r.raw[:, slab, wide:]
+    s_gate.finish(r.wg_low)
+    got_c = [net.push(r.wg_low.at[v], r.dwgu.at[u], v, b) for v in others]
+    r.dwgu[u] = r.wg_low[u]
+    s_qkv.merge()
+    s_out.finish(r.dwo)
+    arrive(got_g)
+    for s in range(seqs):
+        grad_normed = sum(r.landed_g[v, s].astype(f32) for v in range(n_u))
+        own = r.x[s].astype(f32)
+        factor = lax.rsqrt(jnp.mean(own * own, axis=-1, keepdims=True) + epsilon)
+        hat = own * factor
+        scaled = grad_normed * r.gain[0:1, :]
+        inner = jnp.mean(scaled * hat, axis=-1, keepdims=True)
+        r.gin[s] = (r.ghid[s] + factor * (scaled - hat * inner)).astype(bf16)
+        r.sums[3:4] = r.sums[3:4] + jnp.sum(grad_normed * hat, axis=0, keepdims=True)
+    got_s = [net.push(r.sums, r.sums_u.at[u], v, b) for v in others]
+    r.sums_u[u] = r.sums[...]
+    arrive(got_s)
+    r.sums_b[b] = sum(r.sums_u[v] for v in range(n_u))
+    got_s = [net.push(r.sums_b.at[b], r.sums_b.at[b], u, b ^ off) for off in range(1, n_b)]
+    arrive(got_v)
+    for v in range(n_u):
+        r.gvf[:, :, v * 256 : (v + 1) * 256] = r.gv[v]
+    arrive(got_s)
+    r.totals[...] = sum(r.sums_b[c] for c in range(n_b))
+    s_qkv.finish(r.wq_low)
+    got = [net.push(r.wq_low.at[v], r.dwq.at[u], v, b) for v in others]
+    r.dwq[u] = r.wq_low[u]
+    arrive(got_c)
+    arrive(got)
+    net.drain()
+
+
+def pad_to(values, axis, size):
+    widths = [(0, 0)] * values.ndim
+    widths[axis] = (0, size - values.shape[axis])
+    return jnp.pad(values, widths)
+
+
+def local_units(
+    inputs, v_first, grad_out, positions, segments,
+    w_query, w_key, w_value, w_out, w_gate, w_up, w_down, gain_attn, gain_ffn,
+):
+    n_u, n_b = lax.axis_size("ulysses"), lax.axis_size("blk")
+    u, b = here()
+    seqs, td, width = inputs.shape
+    rows = w_query.shape[0]
+    heads = HEADS // n_u
+    tb = n_u * td
+    seq = n_b * tb
+    ff_own = w_down.shape[0]
+    ff_pad = -(-ff_own // 32) * 32
+    ff = ff_pad * n_b
+    dims = (n_u, n_b, seqs, td, rows, heads)
+
+    place = jnp.arange(seq, dtype=jnp.int32)
+    cut = jnp.sum(1 - segments, axis=1, keepdims=True)
+    first = jnp.where(segments == 1, cut, 0)
+    low = lax.dynamic_slice_in_dim(first, b // heads, 1, 0)
+    low = jnp.broadcast_to(low, (8, seq))
+    local_place = (place[None, :] - first).astype(f32)
+    angle_rows = lax.dynamic_slice_in_dim(local_place, b * tb, tb, 1)
+    inverse = rope_base ** (-2.0 * jnp.arange(HD // 2, dtype=f32) / HD)
+    angles = angle_rows[:, :, None] * inverse
+    cosine, sine = jnp.cos(angles), jnp.sin(angles)
+    cosr = jnp.concatenate([cosine] * 4, axis=-1)
+    sinr = jnp.concatenate([-sine, sine] * 2, axis=-1)
+
+    qk = jnp.stack([w_query.reshape(rows, n_u, heads, HD), w_key.reshape(rows, n_u, heads, HD)], axis=3)
+    wqkv = jnp.concatenate(
+        [qk.reshape(rows, n_u, heads * 2 * HD), w_value.reshape(rows, n_u, heads * HD)], axis=2
+    )
+    wqkv = jnp.moveaxis(wqkv, 1, 0)
+
+    def hidden_columns(weight):
+        parted = pad_to(weight.reshape(rows, n_u, n_b, ff_own), 3, ff_pad)
+        return parted.reshape(rows, n_u, ff)
+
+    wgu = jnp.moveaxis(
+        jnp.concatenate([hidden_columns(w_gate), hidden_columns(w_up)], axis=2), 1, 0
+    )
+    wd = pad_to(w_down, 0, ff_pad)
+    vf = jnp.moveaxis(v_first.reshape(seqs, td, n_u, heads * HD), 2, 0)
+    pair = jnp.stack([gain_attn, gain_ffn]).astype(f32)
+    lane = (jnp.arange(LANES) // rows) == (u * n_b + b) % (LANES // rows)
+    gains = pad_to(jnp.where(lane[None, :], jnp.tile(pair, (1, LANES // rows)), 0.0), 0, 8)
+
+    columns = 3 * heads * HD
+    n_z = n_b // 2
+    own, block = (seqs, td, width), (seqs, tb, width)
+    inputs_of = dict(
+        x=inputs, vf=vf, go=grad_out, wqkv=wqkv, wgu=wgu, wout=w_out, wd=wd, gains=gains,
+        cosr=cosr, sinr=sinr, low=low,
+    )
+    outs = dict(
+        out=(own, bf16), gin=(own, bf16), gvf=(own, bf16), dwq=((n_u, rows, columns), bf16),
+        dwo=((rows, width), f32), dwd=((ff_pad, width), f32), dwgu=((n_u, rows, 2 * ff), bf16),
+        totals=((8, width), f32),
+    )
+    scratch = dict(
+        xg=(block, bf16), vfg=((seqs, tb, heads * HD), bf16), gbuf=((n_b, n_u, 8, LANES), f32),
+        gain=((8, width), f32), normed=(block, bf16), wq=((n_u, n_b * rows, columns), bf16),
+        gog=(block, bf16), wg=((n_u, n_b * rows, 2 * ff), bf16), wdg=((ff, width), bf16),
+        wo=((n_b * rows, width), bf16), stage=((n_b, tb + tb // 2, LANES), bf16),
+        units=((n_b, tb + tb // 2, LANES), bf16), keys=((seq, LANES), bf16), key_t=((HD, seq), bf16),
+        query=((seq, LANES), bf16), query_t=((LANES, seq), bf16), value=((seq, LANES), bf16),
+        value_t=((HD, seq), bf16), acc=((HD, QB), f32), heads_t=((HD, seq), f32), lse=((8, seq), f32),
+        ostage=((n_b, tb // 2, LANES), bf16), parts=((n_b, tb // 2, LANES), bf16),
+        mix=((seqs, tb, heads * HD), bf16), branch=(block, bf16), landed_b=((n_u,) + own, bf16),
+        sums=((8, width), f32), hidden=(own, f32), nf_own=(own, bf16), nf=(block, bf16),
+        act=((seqs, tb, ff), bf16), dgu=((seqs, tb, 2 * ff), bf16), d_low=(block, bf16),
+        landed_d=((n_u,) + own, bf16), ghid=(own, f32), gb_own=(own, bf16), gb=(block, bf16),
+        f_low=(block, bf16), landed_f=((n_u,) + own, bf16),
+        wd_buf=((n_z, 2, ff_pad, width), bf16), wd_pair=((n_z, ff_pad, width), bf16),
+        wd_sum=((n_z, ff_pad, width), bf16), wd_land=((n_z, ff_pad, width), bf16),
+        wg_buf=((n_z, 2, n_u, rows, 2 * ff), bf16), wg_pair=((n_z, n_u, rows, 2 * ff), bf16),
+        wg_sum=((n_z, n_u, rows, 2 * ff), bf16), wg_land=((n_z, n_u, rows, 2 * ff), bf16),
+        wg_low=((n_u, rows, 2 * ff), bf16),
+        ostage2=((n_b, tb // 2, LANES), bf16), grads=((n_b, tb // 2, LANES), bf16),
+        wo_buf=((n_z, 2, rows, width), bf16), wo_pair=((n_z, rows, width), bf16),
+        wo_sum=((n_z, rows, width), bf16), wo_land=((n_z, rows, width), bf16),
+        grad=((seq, LANES), bf16), grad_t=((LANES, seq), bf16), row_dot=((8, seq), f32),
+        dq_t=((HD, seq), f32), dk=((KB, LANES), f32), dv=((KB, LANES), f32),
+        returned=((n_b, tb + tb // 2, LANES), bf16), raw=((seqs, tb, columns), bf16),
+        gin_low=(block, bf16), landed_g=((n_u,) + own, bf16), gv=((n_u, seqs, td, heads * HD), bf16),
+        wq_buf=((n_z, 2, n_u, rows, columns), bf16), wq_pair=((n_z, n_u, rows, columns), bf16),
+        wq_sum=((n_z, n_u, rows, columns), bf16), wq_land=((n_z, n_u, rows, columns), bf16),
+        wq_low=((n_u, rows, columns), bf16), sums_u=((n_u, 8, width), f32), sums_b=((n_b, 8, width), f32),
+    )
+    names = [*inputs_of, *outs, *scratch, "send_sems", "recv_sems"]
+    vmem = pl.BlockSpec(memory_space=pltpu.VMEM)
+    results = pl.pallas_call(
+        functools.partial(layer_kernel, dims, names),
+        out_shape=[jax.ShapeDtypeStruct(shape, dtype) for shape, dtype in outs.values()],
+        in_specs=[vmem] * len(inputs_of),
+        out_specs=[vmem] * len(outs),
+        scratch_shapes=[pltpu.VMEM(shape, dtype) for shape, dtype in scratch.values()]
+        + [pltpu.SemaphoreType.DMA((SEMAPHORES,))] * 2,
+        compiler_params=pltpu.CompilerParams(
+            collective_id=1, has_side_effects=True, vmem_limit_bytes=VMEM_BYTES
+        ),
+        name="layer",
+    )(*inputs_of.values())
+    got = dict(zip(outs, results))
+    dwq = jnp.moveaxis(got["dwq"].astype(f32), 0, 1)
+    dqk = dwq[:, :, : heads * 2 * HD].reshape(rows, n_u, heads, 2, HD)
+    grad_w_query = dqk[:, :, :, 0].reshape(rows, width)
+    grad_w_key = dqk[:, :, :, 1].reshape(rows, width)
+    grad_w_value = dwq[:, :, heads * 2 * HD :].reshape(rows, width)
+    dwgu = jnp.moveaxis(got["dwgu"].astype(f32), 0, 1).reshape(rows, n_u, 2, n_b, ff_pad)[..., :ff_own]
+    grad_w_gate = dwgu[:, :, 0].reshape(rows, w_gate.shape[1])
+    grad_w_up = dwgu[:, :, 1].reshape(rows, w_gate.shape[1])
+    grad_w_down = got["dwd"][:ff_own]
+    gain_at = (u * n_b + b) * rows
+    sums = got["totals"]
+    grad_gain_attn = lax.dynamic_slice_in_dim(sums[3], gain_at, rows, 0)
+    grad_gain_ffn = lax.dynamic_slice_in_dim(sums[4], gain_at, rows, 0)
+    statistics = jnp.sqrt(jnp.sum(sums[:3], axis=1) / (seqs * seq * width))
+    return (
+        got["out"], got["gin"], got["gvf"], grad_w_query, grad_w_key, grad_w_value, got["dwo"],
+        grad_w_gate, grad_w_up, grad_w_down, grad_gain_attn, grad_gain_ffn, statistics,
+    )
+
+
+SEMAPHORES = 192
+
+
+def fits_units(mesh):
+    return mesh.shape["ulysses"] == 4 and mesh.shape["blk"] == 8
+
+
 def solution(mesh):
     in_specs = (
         P(None, ("blk", "ulysses"), None),
@@ -454,4 +1187,5 @@
         P(("ulysses", "blk")),
         P(),
     )
-    return jax.shard_map(local, mesh=mesh, in_specs=in_specs, out_specs=out_specs, check_vma=False)
+    path = local_units if fits_units(mesh) else local
+    return jax.shard_map(path, mesh=mesh, in_specs=in_specs, out_specs=out_specs, check_vma=False)

time: 1460 us -> 247 us (0.17)
  waiting for transfers between devices: 1070 us -> 0 us
  Pallas kernels: 0 us -> 218 us
  local copies, waits for them, and re-layouts: 120 us -> 21.1 us
  blocking collectives: 98.9 us -> 0 us
  matrix products: 77.9 us -> 0 us
  starting transfers between devices: 22.7 us -> 0 us
  other arithmetic: 25.1 us -> 6.41 us
  loops' own time: 15 us -> 0 us
    reduce_scatter x4 -> x0, waiting for transfers between devices: 688 us -> none  [the longest x1 375 us: local(): lax.psum_scatter(jnp.concatenate([weight_grad(normed, grad_query_raw), we...]
    all_gather x9 -> x0, waiting for transfers between devices: 361 us -> none  [the longest x1 66.4 us: local(): lax.all_gather(w_up, ('ulysses', 'blk'), axis=0, tiled=True)]
    pallas_call x0 -> x1, Pallas kernels: none -> 218 us  [local_units(): pl.pallas_call(functools.partial(layer_kernel, dims, names), out_shape=[j...]
    dot_general x28 -> x0, matrix products: 77.9 us -> none  [the longest x7 29.2 us: weight_grad(): jnp.einsum('std,ste->de', activations, gradient, preferred_element_type=j...]
    concatenate x1 -> x0, local copies, waits for them, and re-layouts: 42.7 us -> none  [local(): jnp.concatenate([weight_grad(normed, grad_query_raw), weight_grad(normed,...]
    unnamed x1 -> x0, blocking collectives: 42.1 us -> none
    psum x1 -> x0, blocking collectives: 39.3 us -> none  [local(): lax.psum((jnp.sum(residual * residual), jnp.sum(attn_branch * attn_branch...]
    dynamic_slice x20 -> x3, local copies, waits for them, and re-layouts: 23.7 us -> 1.18 us  [the longest x1 0.59 us: local_units(): grad_gain_attn = lax.dynamic_slice_in_dim(sums[3], gain_at, rows, 0)]
  transfers between devices with their start and end apart: 19 -> 0, of which waited for: 17 -> 0; matrix products, arithmetic and copies ran while one was open for 7% -> 0% of each run, Pallas kernels for 0% -> 0%
where the time goes in v2:
time: 247 us; the launch traced here: 246 us
  Pallas kernels  218 us (88%)
  local copies, waits for them, and re-layouts  21.1 us (9%)
  other arithmetic  6.41 us (3%)
    pallas_call x1, Pallas kernels, local_units(): pl.pallas_call(functools.partial(layer_kernel, dims, names), out_shape=[j...  218 us
    unnamed x39, local copies, waits for them, and re-layouts  7.75 us

profile of v2, /device:TPU:0, one launch (start us, length us, event | category | flops | bytes accessed | tf_op | source)
XLA Modules:
  0.0 246.4 jit_solution(6646834089734221732)
XLA Ops:
  0.7 0.7 copy-done.13
  1.4 0.1 subtract_reduce_fusion
  1.6 0.6 broadcast_in_dim.41.refs_10_
  2.2 0.6 copy-done.15
  3.0 0.6 pad.18.refs_7_
  3.6 1.0 fusion
  4.6 1.3 pad_maximum_fusion.1
  5.9 0.6 reshape.105
  6.6 0.2 reshape.106
  6.9 0.7 copy-done.7
  7.6 0.6 reshape.107
  8.3 0.2 reshape.108
  8.5 0.8 maximum_bitcast_fusion.refs_4_
  9.3 0.1 stack_reshape.6
  9.5 0.2 copy.35
  9.7 0.6 copy-done.11
  10.3 0.1 stack_reshape.7
  10.5 0.2 copy.36
  10.7 0.7 pad_maximum_fusion
  11.4 0.2 reshape.103
  11.6 0.6 copy-done.12
  12.2 0.7 maximum_bitcast_fusion.1.refs_3_
  12.9 0.3 copy-done.1
  13.3 0.7 copy.50
  14.0 0.3 copy-done.8
  14.3 0.7 pad.17.refs_6_
  15.0 217.9 %layer.1 = (bf16[2,64,1024]{2,1,0:T(8,128)(2,1)}, bf16[2,64,1024]{2,1,0:T(8,128)(2,1)}, bf16[2,64,1024]{2,1,0:T(8,128)(2,1)}, bf16[4,32,768]{2,1,0:T(8,128)(2,1)...) custom-call(bf16[2,64,1024]{2,1,0:T(8,128)(2,1)} %refs_0_.1, ...), custom_call_target="tpu_custom_call" | custom-call | tf_op jit(solution)/shard_map/layer/pallas_call | solution.py:1118
  232.9 1.1 convert_bitcast_fusion
  234.0 0.3 reshape.114
  234.5 1.0 reshape_squeeze.14
  235.6 1.0 reshape_squeeze.15
  236.7 0.4 reshape.109
  237.1 0.4 fusion.6
  237.5 0.9 reshape_squeeze.12
  238.5 0.9 reshape_squeeze.13
  239.4 0.7 copy.47
  240.1 0.8 slice.39
  240.9 0.6 fusion.3
  241.4 0.6 fusion.4
  242.0 0.1 slice_reduce_fusion
  242.1 0.5 multiply_sqrt_fusion
  242.7 0.7 copy.56
  243.4 0.3 copy-done.3
  243.7 0.7 copy.57
  244.4 0.3 copy-done.2
  244.8 0.7 copy.58
  245.5 0.3 copy-done.9
  245.8 0.7 copy.59
  (47 shorter events, 0.9 us)
Async XLA Ops:
  0.6 0.7 copy-start.13
  2.2 0.7 copy-start.15
  2.2 0.7 copy-start.16
  4.6 1.3 copy-start.6
  6.6 0.9 copy-start.7
  8.5 0.8 copy-start.10
  9.5 0.8 copy-start.11
  11.4 0.8 copy-start.12
  12.2 1.0 copy-start.1
  13.3 1.0 copy-start.8
  235.6 1.1 copy-start.5
  238.5 1.6 copy-start
  240.1 0.8 copy-start.14
  240.1 2.6 %copy-start.4 = (bf16[2,64,1024]{2,1,0:T(8,128)(2,1)S(1)}, bf16[2,64,1024]{2,1,0:T(8,128)(2,1)}, u32[]{:S(2)}) copy-start(bf16[2,64,1024]{2,1,0:T(8,128)(2,1)} %get-tuple-element.53) | copy-start | bytes 786436
  242.7 1.0 copy-start.3
  243.7 1.0 copy-start.2
  244.8 1.0 copy-start.9

commit v3 on v2

--- a/solution.py
+++ b/solution.py
@@ -3,6 +3,7 @@
 
 import jax
 import jax.numpy as jnp
+import numpy as np
 from jax import lax
 from jax.experimental import pallas as pl
 from jax.experimental.pallas import tpu as pltpu
@@ -543,6 +544,36 @@
     return jnp.concatenate([packed, swap_halves(packed)], axis=0)
 
 
+class Exchange:
+    def __init__(self, net, staged, landed, u, b, n_b):
+        self.net, self.staged, self.landed, self.u, self.b, self.n_b = net, staged, landed, u, b, n_b
+        self.at = net.count
+        net.count += n_b
+
+    def copy(self, to, slot_from):
+        return pltpu.make_async_remote_copy(
+            src_ref=self.staged.at[to],
+            dst_ref=self.landed.at[slot_from],
+            send_sem=self.net.send_sems.at[self.at + to],
+            recv_sem=self.net.recv_sems.at[self.at + slot_from],
+            device_id=(self.u, to),
+            device_id_type=MESH,
+        )
+
+    def give(self, to):
+        @pl.when(to != self.b)
+        def _():
+            self.copy(to, self.b).start()
+
+    def take(self):
+        for off in range(1, self.n_b):
+            self.copy(self.b ^ off, self.b ^ off).wait_recv()
+
+    def sent(self):
+        for off in range(1, self.n_b):
+            self.copy(self.b ^ off, self.b).wait_send()
+
+
 class Gather:
     def __init__(self, net, slot, u, b):
         self.net, self.slot, self.u, self.b = net, slot, u, b
@@ -634,10 +665,31 @@
     lax.fori_loop(0, units.shape[0], one, 0)
 
 
-def allowed_block(first_key, first_query, low_row):
-    key_place = first_key + lax.broadcasted_iota(jnp.int32, (KB, QB), 0)
-    query_place = first_query + lax.broadcasted_iota(jnp.int32, (KB, QB), 1)
+def allowed_block(first_key, first_query, low_row, keys=KB, queries=QB):
+    key_place = first_key + lax.broadcasted_iota(jnp.int32, (keys, queries), 0)
+    query_place = first_query + lax.broadcasted_iota(jnp.int32, (keys, queries), 1)
     return (key_place <= query_place) & (key_place >= low_row)
+
+
+def widen(rows, size, padded):
+    zeros = jnp.zeros((rows.shape[0], padded - size), rows.dtype)
+    pieces = []
+    for at in range(0, rows.shape[1], size):
+        pieces += [rows[:, at : at + size], zeros]
+    return jnp.concatenate(pieces, axis=1)
+
+
+def rope_rows(base, cut, count):
+    place = base + lax.broadcasted_iota(jnp.int32, (count, LANES), 0)
+    place = place.astype(f32)
+    local_place = jnp.where(place >= cut, place - cut, place)
+    pair = lane_of((count, LANES)) % (HD // 2)
+    inverse = jnp.zeros((1, LANES), f32)
+    for i in range(HD // 2):
+        inverse = jnp.where(pair[0:1] == i, float(np.float32(rope_base ** (-2.0 * i / HD))), inverse)
+    angles = local_place * inverse
+    sign = jnp.where(lane_of((count, LANES)) % HD < HD // 2, -1.0, 1.0)
+    return jnp.cos(angles), sign * jnp.sin(angles)
 
 
 def layer_kernel(dims, names, *refs):
@@ -659,22 +711,40 @@
     def part(v):
         return at_block(v, td)
 
+    share = heads * HD
+    thirds = (r.wq_in, r.wk_in, r.wv_in)
+    r.gains[...] = jnp.zeros_like(r.gains)
+    for row, gain in enumerate((r.ga, r.gf)):
+        r.gains[row : row + 1, 0:rows] = gain[...].astype(f32).reshape(1, rows)
+    lane_place = (b % (LANES // rows)) * rows
+    r.gains[...] = pltpu.roll(r.gains[...], lane_place, 1)
     greet(u, b, n_u, n_b)
-    got_w = [net.push(r.wqkv.at[v], r.wq.at[u, mine], v, b) for v in others]
+    got_w = [
+        net.push(w.at[:, at_block(v, share)], r.wq.at[u, mine, pl.ds(i * share, share)], v, b)
+        for i, w in enumerate(thirds)
+        for v in others
+    ]
     got_g = [net.push(r.gains, r.gbuf.at[b, u], v, b) for v in others]
     r.wo[mine] = r.wout[...]
     g_out = Gather(net, lambda c: r.wo.at[at_block(c, rows)], u, b)
     got_x = [net.push(r.x, r.xg.at[:, slab], v, b) for v in others]
-    r.wq[u, mine] = r.wqkv[u]
+    for i, w in enumerate(thirds):
+        r.wq[u, mine, i * share : (i + 1) * share] = w[:, at_block(u, share)]
     r.gbuf[b, u] = r.gains[...]
     r.xg[:, slab] = r.x[...]
-    r.vfg[:, slab] = r.vf[u]
+    r.vfg[:, slab] = r.vf[:, :, at_block(u, share)]
     r.gog[:, slab] = r.go[...]
     arrive(got_w)
-    g_qkv = Gather(net, lambda c: r.wq.at[:, at_block(c, rows)], u, b)
+    g_qk = Gather(net, lambda c: r.wq.at[:, at_block(c, rows), pl.ds(0, 2 * share)], u, b)
+    g_v = Gather(net, lambda c: r.wq.at[:, at_block(c, rows), pl.ds(2 * share, share)], u, b)
     arrive(got_g)
     got_g = [net.push(r.gbuf.at[b], r.gbuf.at[b], u, b ^ off) for off in range(1, n_b)]
-    got_v = [net.push(r.vf.at[v], r.vfg.at[:, slab], v, b) for v in others]
+    got_v = [net.push(r.vf.at[:, :, at_block(v, share)], r.vfg.at[:, slab], v, b) for v in others]
+    ff_own = r.wd.shape[0]
+    for i, w in enumerate((r.wg_in, r.wu_in)):
+        wide_rows = widen(w[...], ff_own, ff_rows)
+        for v in range(n_u):
+            r.wgu[v, :, i * ff : (i + 1) * ff] = wide_rows[:, v * ff : (v + 1) * ff]
     r.wg[u, mine] = r.wgu[u]
     got_o = [net.push(r.wgu.at[v], r.wg.at[u, mine], v, b) for v in others]
     arrive(got_g)
@@ -685,33 +755,57 @@
             term = r.gbuf[index % n_b, index // n_b]
             total = term if total is None else total + term
         r.gain[:, tile * LANES : (tile + 1) * LANES] = total
+    seq_of_unit = b // heads
+    for s in range(seqs):
+        cut = jnp.sum((1 - r.segments[s : s + 1, :]).astype(f32), axis=1, keepdims=True)
+        r.cosr[s], r.sinr[s] = rope_rows(b * tb, cut, tb)
+
+        @pl.when(seq_of_unit == s)
+        def _():
+            key_place = lane_of((8, seq)).astype(f32)
+            r.low[...] = jnp.where(key_place >= cut, cut, 0.0).astype(jnp.int32)
+
     arrive(got_x)
 
     def norm(step, carry):
         s, place = step // 2, at_block(step % 2, tb // 2)
         values = r.xg[s, place].astype(f32)
         factor = lax.rsqrt(jnp.mean(values * values, axis=-1, keepdims=True) + epsilon)
-        r.normed[s, place] = (values * factor * r.gain[0:1, :]).astype(bf16)
+        hat = values * factor
+        r.hat[s, place] = hat.astype(bf16)
+        r.normed[s, place] = (hat * r.gain[0:1, :]).astype(bf16)
         return carry
 
     lax.fori_loop(0, 2 * seqs, norm, 0)
     got_go = [net.push(r.go, r.gog.at[:, slab], v, b) for v in others]
-    g_out.forward()
-    g_qkv.forward()
-    arrive(got_v)
-    g_qkv.relay()
-    g_qkv.finish()
-
+    g_qk.forward()
+    g_qk.relay()
+    g_v.forward()
+    g_qk.finish()
+
+    x_qk = Exchange(net, r.stage.at[:, pl.ds(0, tb)], r.units.at[:, pl.ds(0, tb)], u, b, n_b)
+    x_v = Exchange(net, r.stage.at[:, pl.ds(tb, tb // 2)], r.units.at[:, pl.ds(tb, tb // 2)], u, b, n_b)
     for s in range(seqs):
         left = r.normed[s]
-        for n in range(heads // 2):
-            found = dot(left, r.wq[:, :, n * 256 : (n + 1) * 256].reshape(width, 256))
+        for n in range(heads // 4):
+            spans = [slice(i * share + n * 256, i * share + (n + 1) * 256) for i in range(2)]
+            pair_of = [dot(left, r.wq[:, :, span].reshape(width, 256)) for span in spans]
             for i in range(2):
-                tile = found[:, i * LANES : (i + 1) * LANES]
-                turned = tile * r.cosr[s] + partner(tile) * r.sinr[s]
-                r.stage[s * heads + 2 * n + i, 0:tb] = turned.astype(bf16)
+                lanes = slice(i * LANES, (i + 1) * LANES)
+                query, key = [f[:, lanes] * r.cosr[s] + partner(f[:, lanes]) * r.sinr[s] for f in pair_of]
+                low_lane = lane_of(query.shape) < HD
+                unit = s * heads + 4 * n + 2 * i
+                r.stage[unit, 0:tb] = jnp.where(low_lane, query, swap_halves(key)).astype(bf16)
+                r.stage[unit + 1, 0:tb] = jnp.where(low_lane, swap_halves(query), key).astype(bf16)
+        for unit in range(s * heads, (s + 1) * heads):
+            x_qk.give(unit)
+    arrive(got_v)
+    g_v.relay()
+    g_v.finish()
+    for s in range(seqs):
+        left = r.normed[s]
         for n in range(heads // 4):
-            first_lane = heads * LANES + n * 256
+            first_lane = 2 * share + n * 256
             found = dot(left, r.wq[:, :, first_lane : first_lane + 256].reshape(width, 256))
             for i in range(2):
                 first = r.vfg[s, :, n * 256 + i * LANES : n * 256 + (i + 1) * LANES].astype(f32)
@@ -719,14 +813,20 @@
                 unit = s * heads + 4 * n + 2 * i
                 r.stage[unit, tb:] = pack_rows(value).astype(bf16)
                 r.stage[unit + 1, tb:] = pack_rows(swap_halves(value)).astype(bf16)
-    got_q = [net.push(r.stage.at[b ^ off], r.units.at[b], u, b ^ off) for off in range(n_b - 1, 0, -1)]
+        for unit in range(s * heads, (s + 1) * heads):
+            x_v.give(unit)
     r.units[b] = r.stage[b]
-    r.wdg[at_block(b, ff_rows)] = r.wd[...]
+    for slot in range(n_b):
+        r.wdg[slot * ff_rows + ff_own : (slot + 1) * ff_rows] = jnp.zeros((ff_rows - ff_own, width), bf16)
+    r.wdg[pl.ds(pl.multiple_of(b * ff_rows, ff_rows), ff_own)] = r.wd[...]
+    g_out.forward()
     g_out.relay()
-    arrive(got_q)
+    x_qk.take()
+    x_v.take()
     g_out.finish()
 
-    g_down = Gather(net, lambda c: r.wdg.at[at_block(c, ff_rows)], u, b)
+    g_down = Gather(net, lambda c: r.wdg.at[pl.ds(pl.multiple_of(c * ff_rows, ff_rows), ff_own)], u, b)
+    x_out = Exchange(net, r.ostage, r.parts, u, b, n_b)
 
     def store(block, query, key, value):
         place = at_block(block, tb)
@@ -739,7 +839,8 @@
 
     fill_units(r.units, tb, store)
 
-    def attend(qb, carry):
+    def attend(step, carry):
+        qb = seq // QB - 1 - step
         q_at = at_block(qb, QB)
         query = r.query_t[:, q_at]
         low_row = r.low[0:1, q_at]
@@ -764,17 +865,20 @@
         r.lse[:, q_at] = jnp.broadcast_to(best + jnp.log(total), (8, QB))
         turned = jnp.transpose(jnp.concatenate([out, jnp.zeros_like(out)], axis=0))
         for i in range(QB // tb):
-            r.ostage[qb * (QB // tb) + i] = pack_rows(turned[i * tb : (i + 1) * tb]).astype(bf16)
+            to = qb * (QB // tb) + i
+            r.ostage[to] = pack_rows(turned[i * tb : (i + 1) * tb]).astype(bf16)
+            x_out.give(to)
         return carry
 
     lax.fori_loop(0, seq // QB, attend, 0)
-    got = [net.push(r.ostage.at[b ^ off], r.parts.at[b], u, b ^ off) for off in range(n_b - 1, 0, -1)]
     r.parts[b] = r.ostage[b]
     g_down.forward()
-    arrive(got)
     arrive(got_o)
+    x_out.take()
     g_gate = Gather(net, lambda c: r.wg.at[:, at_block(c, rows)], u, b)
+
     half = tb // 2
+    got_s = []
     for s in range(seqs):
         for pair in range(heads // 2):
             one = r.parts[s * heads + 2 * pair].astype(f32)
@@ -783,41 +887,36 @@
             lanes = slice(pair * LANES, (pair + 1) * LANES)
             r.mix[s, :half, lanes] = jnp.where(low_lane, one, swap_halves(two)).astype(bf16)
             r.mix[s, half:, lanes] = jnp.where(low_lane, swap_halves(one), two).astype(bf16)
-
-    def project_out(s, carry):
         r.branch[s] = dot(r.mix[s], r.wo[...]).astype(bf16)
-        return carry
-
-    lax.fori_loop(0, seqs, project_out, 0)
-    got = [net.push(r.branch.at[:, part(v)], r.landed_b.at[u], v, b) for v in others]
-    r.landed_b[u] = r.branch[:, slab]
+        got_s.append([net.push(r.branch.at[s, part(v)], r.landed.at[u, s], v, b) for v in others])
+        r.landed[u, s] = r.branch[s, slab]
     g_down.relay()
-    arrive(got)
     r.sums[...] = jnp.zeros_like(r.sums)
+    got_n = []
     for s in range(seqs):
-        total = sum(r.landed_b[v, s].astype(f32) for v in range(n_u))
+        arrive(got_s[s])
+        total = sum(r.landed[v, s].astype(f32) for v in range(n_u))
         own = r.x[s].astype(f32)
         hid = own + total
         r.hidden[s] = hid
         factor = lax.rsqrt(jnp.mean(hid * hid, axis=-1, keepdims=True) + epsilon)
         r.nf_own[s] = (hid * factor * r.gain[1:2, :]).astype(bf16)
+        got_n.append([net.push(r.nf_own.at[s], r.nf.at[s, slab], v, b) for v in others])
+        r.nf[s, slab] = r.nf_own[s]
         r.sums[0:1] = r.sums[0:1] + jnp.sum(own * own, axis=0, keepdims=True)
         r.sums[1:2] = r.sums[1:2] + jnp.sum(total * total, axis=0, keepdims=True)
-    got = [net.push(r.nf_own, r.nf.at[:, slab], v, b) for v in others]
-    r.nf[:, slab] = r.nf_own[...]
     arrive(got_go)
     g_down.finish()
     g_gate.forward()
     g_gate.relay()
-    arrive(got)
     g_gate.finish()
 
-    def hidden_units(s, carry):
+    def hidden_units(s):
         left = r.nf[s]
         grad = r.gog[s]
-        for n in range(ff // 256):
-            span = slice(n * 256, (n + 1) * 256)
-            up_span = slice(ff + n * 256, ff + (n + 1) * 256)
+
+        def some(n, carry):
+            span, up_span = at_block(n, 256), at_block(n + ff // 256, 256)
             gate = dot(left, r.wg[:, :, span].reshape(width, 256))
             up = dot(left, r.wg[:, :, up_span].reshape(width, 256))
             grad_act = dot_nt(grad, r.wdg[span])
@@ -826,39 +925,38 @@
             r.act[s, :, span] = (silu * up).astype(bf16)
             r.dgu[s, :, span] = (grad_act * up * sig * (1.0 + gate * (1.0 - sig))).astype(bf16)
             r.dgu[s, :, up_span] = (grad_act * silu).astype(bf16)
-        return carry
-
-    lax.fori_loop(0, seqs, hidden_units, 0)
-
-    def back_units(s, carry):
+            return carry
+
+        lax.fori_loop(0, ff // 256, some, 0)
+
+    got_d = []
+    for s in range(seqs):
+        arrive(got_n[s])
+        hidden_units(s)
         left = r.dgu[s]
         for v in range(n_u):
             r.d_low[s, :, v * 256 : (v + 1) * 256] = dot_nt(left, r.wg[v]).astype(bf16)
-        return carry
-
-    lax.fori_loop(0, seqs, back_units, 0)
-    got_d = [net.push(r.d_low.at[:, part(v)], r.landed_d.at[u], v, b) for v in others]
-    r.landed_d[u] = r.d_low[:, slab]
-
-    half_units = ff // 2
-    for n in range(2):
+        got_d.append([net.push(r.d_low.at[s, part(v)], r.landed.at[u, s], v, b) for v in others])
+        r.landed[u, s] = r.d_low[s, slab]
+
+    def grad_down(n):
+        half_units = ff // 2
         span = slice(n * half_units, (n + 1) * half_units)
         found = dot_tn(r.act[:, :, span].reshape(tokens, half_units), r.gog[...].reshape(tokens, width))
         r.wd_buf[n * (n_z // 2) : (n + 1) * (n_z // 2)] = found.astype(bf16).reshape(
             n_z // 2, 2, ff_rows, width
         )
-    s_down = Scatter(net, u, b, lambda z, c: r.wd_buf.at[z, c], r.wd_pair, r.wd_sum, r.wd_land)
-    for v in range(n_u):
+
+    def grad_gate(v):
         left = r.nf[:, :, v * 256 : (v + 1) * 256].reshape(tokens, 256)
         found = dot_tn(left, r.dgu[...].reshape(tokens, 2 * ff))
         r.wg_buf[:, :, v] = found.astype(bf16).reshape(n_z, 2, rows, 2 * ff)
-        if v == 1:
-            s_down.middle()
-    s_gate = Scatter(net, u, b, lambda z, c: r.wg_buf.at[z, c], r.wg_pair, r.wg_sum, r.wg_land)
-
-    arrive(got_d)
-    for s in range(seqs):
-        grad_normed = sum(r.landed_d[v, s].astype(f32) for v in range(n_u))
+
+    got_b = []
+
+    def norm_back(s):
+        arrive(got_d[s])
+        grad_normed = sum(r.landed[v, s].astype(f32) for v in range(n_u))
         hid = r.hidden[s]
         factor = lax.rsqrt(jnp.mean(hid * hid, axis=-1, keepdims=True) + epsilon)
         hat = hid * factor
@@ -867,30 +965,48 @@
         total = r.go[s].astype(f32) + factor * (scaled - hat * inner)
         r.ghid[s] = total
         r.gb_own[s] = total.astype(bf16)
+        got_b.append([net.push(r.gb_own.at[s], r.xg.at[s, slab], v, b) for v in others])
+        r.xg[s, slab] = r.gb_own[s]
         r.sums[4:5] = r.sums[4:5] + jnp.sum(grad_normed * hat, axis=0, keepdims=True)
-    got_b = [net.push(r.gb_own, r.gb.at[:, slab], v, b) for v in others]
-    r.gb[:, slab] = r.gb_own[...]
+
+    for n in range(2):
+        grad_down(n)
+    ff_cut = pl.ds(0, ff_own)
+    s_down = Scatter(
+        net, u, b, lambda z, c: r.wd_buf.at[z, c, ff_cut], r.wd_pair.at[:, ff_cut],
+        r.wd_sum.at[:, ff_cut], r.wd_land.at[:, ff_cut],
+    )
+    norm_back(0)
+    grad_gate(0)
+    s_down.middle()
+    norm_back(1)
+    for v in range(1, n_u):
+        grad_gate(v)
     s_down.merge()
+    s_gate = Scatter(net, u, b, lambda z, c: r.wg_buf.at[z, c], r.wg_pair, r.wg_sum, r.wg_land)
+    x_grad = Exchange(net, r.ostage2, r.grads, u, b, n_b)
+    for s in range(seqs):
+        arrive(got_b[s])
+        for pair in range(heads // 2):
+            found = dot_nt(r.xg[s], r.wo[pair * LANES : (pair + 1) * LANES])
+            unit = s * heads + 2 * pair
+            r.ostage2[unit] = pack_rows(found).astype(bf16)
+            r.ostage2[unit + 1] = pack_rows(swap_halves(found)).astype(bf16)
+            x_grad.give(unit)
+            x_grad.give(unit + 1)
+    r.grads[b] = r.ostage2[b]
 
     def forward(s, carry):
         r.f_low[s] = dot(r.act[s], r.wdg[...]).astype(bf16)
         return carry
 
     lax.fori_loop(0, seqs, forward, 0)
-    arrive(got_b)
-    for s in range(seqs):
-        for pair in range(heads // 2):
-            found = dot_nt(r.gb[s], r.wo[pair * LANES : (pair + 1) * LANES])
-            r.ostage2[s * heads + 2 * pair] = pack_rows(found).astype(bf16)
-            r.ostage2[s * heads + 2 * pair + 1] = pack_rows(swap_halves(found)).astype(bf16)
-    got_u = [net.push(r.ostage2.at[b ^ off], r.grads.at[b], u, b ^ off) for off in range(n_b - 1, 0, -1)]
-    r.grads[b] = r.ostage2[b]
     got_f = [net.push(r.f_low.at[:, part(v)], r.landed_f.at[u], v, b) for v in others]
     r.landed_f[u] = r.f_low[:, slab]
-    found = dot_tn(r.mix[...].reshape(tokens, heads * HD), r.gb[...].reshape(tokens, width))
+    found = dot_tn(r.mix[...].reshape(tokens, share), r.xg[...].reshape(tokens, width))
     r.wo_buf[...] = found.astype(bf16).reshape(n_z, 2, rows, width)
     s_out = Scatter(net, u, b, lambda z, c: r.wo_buf.at[z, c], r.wo_pair, r.wo_sum, r.wo_land)
-    arrive(got_u)
+    x_grad.take()
     s_gate.middle()
 
     def more(block, carry):
@@ -905,43 +1021,61 @@
         return carry
 
     lax.fori_loop(0, n_b, more, 0)
-    r.dq_t[...] = jnp.zeros_like(r.dq_t)
-    net.sent(got_q)
-
-    def outer(kb, carry):
-        k_at = at_block(kb, KB)
-        r.dk[...] = jnp.zeros_like(r.dk)
-        r.dv[...] = jnp.zeros_like(r.dv)
-
-        def inner(qb, carry):
-            q_at = at_block(qb, QB)
-            scores = dot(r.keys[k_at], r.query_t[:, q_at])
-            seen = allowed_block(kb * KB, qb * QB, r.low[0:1, q_at])
-            probs = jnp.where(seen, jnp.exp(scores - r.lse[0:1, q_at]), 0.0)
-            prob_grad = dot(r.value[k_at], r.grad_t[:, q_at])
-            score_grad = (probs * (prob_grad - r.row_dot[0:1, q_at])).astype(bf16)
-            r.dv[...] += dot(probs.astype(bf16), r.grad[q_at])
-            r.dk[...] += dot(score_grad, r.query[q_at])
-            r.dq_t[:, q_at] += dot(r.key_t[:, k_at], score_grad)
-            return carry
-
-        lax.fori_loop(kb // (QB // KB), seq // QB, inner, 0)
-        low_lane = lane_of((KB, LANES)) < HD
-        r.stage[kb, 0:tb] = jnp.where(low_lane, 0.0, swap_halves(r.dk[...])).astype(bf16)
-        r.stage[kb, tb:] = pack_rows(r.dv[...]).astype(bf16)
-        return carry
-
-    lax.fori_loop(0, seq // KB, outer, 0)
-
-    def turn_query(block, carry):
-        columns = r.dq_t[:, at_block(block, tb)] * HD ** (-0.5)
+    x_qk.sent()
+    x_v.sent()
+    x_back = Exchange(net, r.stage, r.returned, u, b, n_b)
+
+    def backward(keys_at, first_key, queries_at, first_query):
+        seen = allowed_block(first_key, first_query, r.low[0:1, queries_at], keys_at.size, queries_at.size)
+        scores = dot(r.keys[keys_at], r.query_t[:, queries_at])
+        probs = jnp.where(seen, jnp.exp(scores - r.lse[0:1, queries_at]), 0.0)
+        prob_grad = dot(r.value[keys_at], r.grad_t[:, queries_at])
+        score_grad = (probs * (prob_grad - r.row_dot[0:1, queries_at])).astype(bf16)
+        r.dv[keys_at] += dot(probs.astype(bf16), r.grad[queries_at])
+        r.dk[keys_at] += dot(score_grad, r.query[queries_at])
+        r.dq_t[:, queries_at] += dot(r.key_t[:, keys_at], score_grad)
+
+    def finished(block):
+        place = at_block(block, tb)
+        columns = r.dq_t[:, place] * HD ** (-0.5)
         turned = jnp.transpose(jnp.concatenate([columns, jnp.zeros_like(columns)], axis=0))
         low_lane = lane_of(turned.shape) < HD
-        r.stage[block, 0:tb] = jnp.where(low_lane, turned, r.stage[block, 0:tb].astype(f32)).astype(bf16)
-        return carry
-
-    lax.fori_loop(0, n_b, turn_query, 0)
-    got = [net.push(r.stage.at[b ^ off], r.returned.at[b], u, b ^ off) for off in range(n_b - 1, 0, -1)]
+        r.stage[block, 0:tb] = jnp.where(low_lane, turned, swap_halves(r.dk[place])).astype(bf16)
+        r.stage[block, tb:] = pack_rows(r.dv[place]).astype(bf16)
+        x_back.give(block)
+
+    for buffer in (r.dq_t, r.dk, r.dv):
+        buffer[...] = jnp.zeros_like(buffer)
+    ratio = QB // KB
+
+    @pl.when(b >= n_b // 2)
+    def _():
+        def outer(kb, carry):
+            def inner(qb, carry):
+                backward(at_block(kb, KB), kb * KB, at_block(qb, QB), qb * QB)
+                return carry
+
+            lax.fori_loop(kb // ratio, seq // QB, inner, 0)
+            finished(kb)
+            return carry
+
+        lax.fori_loop(0, n_b, outer, 0)
+
+    @pl.when(b < n_b // 2)
+    def _():
+        def outer(step, carry):
+            qb = n_b - 1 - step
+
+            def inner(kb, carry):
+                backward(at_block(kb, QB), kb * QB, at_block(qb, KB), qb * KB)
+                return carry
+
+            lax.fori_loop(0, qb // ratio + 1, inner, 0)
+            finished(qb)
+            return carry
+
+        lax.fori_loop(0, n_b, outer, 0)
+
     r.returned[b] = r.stage[b]
     s_gate.merge()
     s_out.middle()
@@ -950,20 +1084,27 @@
         total = r.hidden[s] + sum(r.landed_f[v, s].astype(f32) for v in range(n_u))
         r.out[s] = total.astype(bf16)
         r.sums[2:3] = r.sums[2:3] + jnp.sum(total * total, axis=0, keepdims=True)
-    s_down.finish(r.dwd)
-    arrive(got)
-
-    wide = heads * LANES
+    s_down.finish(r.gwd)
+    x_back.take()
+
     for s in range(seqs):
-        for head in range(heads):
-            tile = r.returned[s * heads + head, 0:tb].astype(f32)
-            turned = tile * r.cosr[s] - partner(tile) * r.sinr[s]
-            r.raw[s, :, head * LANES : (head + 1) * LANES] = turned.astype(bf16)
         for pair in range(heads // 2):
-            one = unpack_rows(r.returned[s * heads + 2 * pair, tb:].astype(f32))
-            two = unpack_rows(r.returned[s * heads + 2 * pair + 1, tb:].astype(f32))
-            both = 0.5 * jnp.where(lane_of(one.shape) < HD, one, swap_halves(two))
-            r.raw[s, :, wide + pair * LANES : wide + (pair + 1) * LANES] = both.astype(bf16)
+            unit = s * heads + 2 * pair
+            one, two = r.returned[unit, 0:tb].astype(f32), r.returned[unit + 1, 0:tb].astype(f32)
+            low_lane = lane_of(one.shape) < HD
+            grads = (
+                jnp.where(low_lane, one, swap_halves(two)),
+                jnp.where(low_lane, swap_halves(one), two),
+            )
+            for i, tile in enumerate(grads):
+                turned = tile * r.cosr[s] - partner(tile) * r.sinr[s]
+                at = i * share + pair * LANES
+                r.raw[s, :, at : at + LANES] = turned.astype(bf16)
+            one = unpack_rows(r.returned[unit, tb:].astype(f32))
+            two = unpack_rows(r.returned[unit + 1, tb:].astype(f32))
+            both = 0.5 * jnp.where(low_lane, one, swap_halves(two))
+            at = 2 * share + pair * LANES
+            r.raw[s, :, at : at + LANES] = both.astype(bf16)
     columns = r.raw.shape[2]
     for v in range(n_u):
         left = r.normed[:, :, v * 256 : (v + 1) * 256].reshape(tokens, 256)
@@ -972,55 +1113,77 @@
     s_qkv = Scatter(net, u, b, lambda z, c: r.wq_buf.at[z, c], r.wq_pair, r.wq_sum, r.wq_land)
     s_out.merge()
 
-    def back_inputs(s, carry):
+    got_g = []
+    for s in range(seqs):
         left = r.raw[s]
         for v in range(n_u):
-            r.gin_low[s, :, v * 256 : (v + 1) * 256] = dot_nt(left, r.wq[v]).astype(bf16)
-        return carry
-
-    lax.fori_loop(0, seqs, back_inputs, 0)
-    got_g = [net.push(r.gin_low.at[:, part(v)], r.landed_g.at[u], v, b) for v in others]
-    r.landed_g[u] = r.gin_low[:, slab]
+            lanes = slice(v * 256, (v + 1) * 256)
+            found = dot_nt(left, r.wq[v])
+            r.gin_low[s, :, lanes] = found.astype(bf16)
+            term = jnp.sum(found * r.hat[s, :, lanes].astype(f32), axis=0, keepdims=True)
+            r.sums[3:4, lanes] = r.sums[3:4, lanes] + term
+        got_g.append([net.push(r.gin_low.at[s, part(v)], r.landed.at[u, s], v, b) for v in others])
+        r.landed[u, s] = r.gin_low[s, slab]
+    got_s = [net.push(r.sums, r.sums_u.at[u], v, b) for v in others]
+    r.sums_u[u] = r.sums[...]
     s_qkv.middle()
-    got_v = [net.push(r.raw.at[:, part(v), pl.ds(wide, heads * HD)], r.gv.at[u], v, b) for v in others]
-    r.gv[u] = r.raw[:, slab, wide:]
+    got_v = [net.push(r.raw.at[:, part(v), pl.ds(2 * share, share)], r.gv.at[u], v, b) for v in others]
+    r.gv[u] = r.raw[:, slab, 2 * share :]
     s_gate.finish(r.wg_low)
     got_c = [net.push(r.wg_low.at[v], r.dwgu.at[u], v, b) for v in others]
     r.dwgu[u] = r.wg_low[u]
     s_qkv.merge()
-    s_out.finish(r.dwo)
-    arrive(got_g)
+    s_out.finish(r.gwo)
+    arrive(got_s)
+    r.sums_b[b] = sum(r.sums_u[v] for v in range(n_u))
+    got_s = [net.push(r.sums_b.at[b], r.sums_b.at[b], u, b ^ off) for off in range(1, n_b)]
     for s in range(seqs):
-        grad_normed = sum(r.landed_g[v, s].astype(f32) for v in range(n_u))
+        arrive(got_g[s])
+        grad_normed = sum(r.landed[v, s].astype(f32) for v in range(n_u))
         own = r.x[s].astype(f32)
         factor = lax.rsqrt(jnp.mean(own * own, axis=-1, keepdims=True) + epsilon)
         hat = own * factor
         scaled = grad_normed * r.gain[0:1, :]
         inner = jnp.mean(scaled * hat, axis=-1, keepdims=True)
         r.gin[s] = (r.ghid[s] + factor * (scaled - hat * inner)).astype(bf16)
-        r.sums[3:4] = r.sums[3:4] + jnp.sum(grad_normed * hat, axis=0, keepdims=True)
-    got_s = [net.push(r.sums, r.sums_u.at[u], v, b) for v in others]
-    r.sums_u[u] = r.sums[...]
-    arrive(got_s)
-    r.sums_b[b] = sum(r.sums_u[v] for v in range(n_u))
-    got_s = [net.push(r.sums_b.at[b], r.sums_b.at[b], u, b ^ off) for off in range(1, n_b)]
     arrive(got_v)
     for v in range(n_u):
         r.gvf[:, :, v * 256 : (v + 1) * 256] = r.gv[v]
     arrive(got_s)
-    r.totals[...] = sum(r.sums_b[c] for c in range(n_b))
+    totals = sum(r.sums_b[c] for c in range(n_b))
+    squares = jnp.sum(totals, axis=1, keepdims=True) / (seqs * seq * width)
+    r.totals[...] = totals
+    roots = jnp.sqrt(squares)
+    lane = lane_of((1, LANES))
+    r.stats[...] = jnp.where(lane == 0, roots[0:1], jnp.where(lane == 1, roots[1:2], roots[2:3]))[0, 0:3]
+    per = LANES // rows
+    tile = r.totals[:, at_block(u * (n_b // per) + b // per, LANES)]
+    tile = pltpu.roll(tile, (LANES - lane_place) % LANES, 1)
+    r.gga[...] = tile[3, 0:rows]
+    r.ggf[...] = tile[4, 0:rows]
     s_qkv.finish(r.wq_low)
     got = [net.push(r.wq_low.at[v], r.dwq.at[u], v, b) for v in others]
     r.dwq[u] = r.wq_low[u]
     arrive(got_c)
+    for i, to in enumerate((r.gwg, r.gwu)):
+        pieces = [
+            r.dwgu[v, :, i * ff + j * ff_rows : i * ff + j * ff_rows + ff_own].astype(f32)
+            for v in range(n_u)
+            for j in range(n_b)
+        ]
+        to[...] = jnp.concatenate(pieces, axis=1)
     arrive(got)
+    for i, to in enumerate((r.gwq, r.gwk, r.gwv)):
+        for v in range(n_u):
+            to[:, v * share : (v + 1) * share] = r.dwq[v, :, i * share : (i + 1) * share].astype(f32)
+    for exchange in (x_out, x_grad, x_back):
+        exchange.sent()
     net.drain()
 
 
-def pad_to(values, axis, size):
-    widths = [(0, 0)] * values.ndim
-    widths[axis] = (0, size - values.shape[axis])
-    return jnp.pad(values, widths)
+def hand_out_kernel(count, *refs):
+    for given, taken in zip(refs[:count], refs[count:]):
+        taken[...] = given[...]
 
 
 def local_units(
@@ -1028,7 +1191,6 @@
     w_query, w_key, w_value, w_out, w_gate, w_up, w_down, gain_attn, gain_ffn,
 ):
     n_u, n_b = lax.axis_size("ulysses"), lax.axis_size("blk")
-    u, b = here()
     seqs, td, width = inputs.shape
     rows = w_query.shape[0]
     heads = HEADS // n_u
@@ -1039,51 +1201,22 @@
     ff = ff_pad * n_b
     dims = (n_u, n_b, seqs, td, rows, heads)
 
-    place = jnp.arange(seq, dtype=jnp.int32)
-    cut = jnp.sum(1 - segments, axis=1, keepdims=True)
-    first = jnp.where(segments == 1, cut, 0)
-    low = lax.dynamic_slice_in_dim(first, b // heads, 1, 0)
-    low = jnp.broadcast_to(low, (8, seq))
-    local_place = (place[None, :] - first).astype(f32)
-    angle_rows = lax.dynamic_slice_in_dim(local_place, b * tb, tb, 1)
-    inverse = rope_base ** (-2.0 * jnp.arange(HD // 2, dtype=f32) / HD)
-    angles = angle_rows[:, :, None] * inverse
-    cosine, sine = jnp.cos(angles), jnp.sin(angles)
-    cosr = jnp.concatenate([cosine] * 4, axis=-1)
-    sinr = jnp.concatenate([-sine, sine] * 2, axis=-1)
-
-    qk = jnp.stack([w_query.reshape(rows, n_u, heads, HD), w_key.reshape(rows, n_u, heads, HD)], axis=3)
-    wqkv = jnp.concatenate(
-        [qk.reshape(rows, n_u, heads * 2 * HD), w_value.reshape(rows, n_u, heads * HD)], axis=2
-    )
-    wqkv = jnp.moveaxis(wqkv, 1, 0)
-
-    def hidden_columns(weight):
-        parted = pad_to(weight.reshape(rows, n_u, n_b, ff_own), 3, ff_pad)
-        return parted.reshape(rows, n_u, ff)
-
-    wgu = jnp.moveaxis(
-        jnp.concatenate([hidden_columns(w_gate), hidden_columns(w_up)], axis=2), 1, 0
-    )
-    wd = pad_to(w_down, 0, ff_pad)
-    vf = jnp.moveaxis(v_first.reshape(seqs, td, n_u, heads * HD), 2, 0)
-    pair = jnp.stack([gain_attn, gain_ffn]).astype(f32)
-    lane = (jnp.arange(LANES) // rows) == (u * n_b + b) % (LANES // rows)
-    gains = pad_to(jnp.where(lane[None, :], jnp.tile(pair, (1, LANES // rows)), 0.0), 0, 8)
-
     columns = 3 * heads * HD
     n_z = n_b // 2
     own, block = (seqs, td, width), (seqs, tb, width)
     inputs_of = dict(
-        x=inputs, vf=vf, go=grad_out, wqkv=wqkv, wgu=wgu, wout=w_out, wd=wd, gains=gains,
-        cosr=cosr, sinr=sinr, low=low,
+        x=inputs, vf=v_first, go=grad_out, segments=segments, wq_in=w_query, wk_in=w_key, wv_in=w_value,
+        wout=w_out, wg_in=w_gate, wu_in=w_up, wd=w_down, ga=gain_attn, gf=gain_ffn,
     )
     outs = dict(
-        out=(own, bf16), gin=(own, bf16), gvf=(own, bf16), dwq=((n_u, rows, columns), bf16),
-        dwo=((rows, width), f32), dwd=((ff_pad, width), f32), dwgu=((n_u, rows, 2 * ff), bf16),
-        totals=((8, width), f32),
+        out=(own, bf16), gin=(own, bf16), gvf=(own, bf16), gwq=((rows, width), f32), gwk=((rows, width), f32),
+        gwv=((rows, width), f32), gwo=((rows, width), f32), gwg=(w_gate.shape, f32), gwu=(w_gate.shape, f32),
+        gwd=((ff_own, width), f32), gga=((rows,), f32), ggf=((rows,), f32), stats=((3,), f32),
     )
     scratch = dict(
+        gains=((8, LANES), f32), wgu=((n_u, rows, 2 * ff), bf16), cosr=((seqs, tb, LANES), f32),
+        sinr=((seqs, tb, LANES), f32), low=((8, seq), jnp.int32),
+        dwq=((n_u, rows, columns), bf16), dwgu=((n_u, rows, 2 * ff), bf16),
         xg=(block, bf16), vfg=((seqs, tb, heads * HD), bf16), gbuf=((n_b, n_u, 8, LANES), f32),
         gain=((8, width), f32), normed=(block, bf16), wq=((n_u, n_b * rows, columns), bf16),
         gog=(block, bf16), wg=((n_u, n_b * rows, 2 * ff), bf16), wdg=((ff, width), bf16),
@@ -1092,10 +1225,10 @@
         query=((seq, LANES), bf16), query_t=((LANES, seq), bf16), value=((seq, LANES), bf16),
         value_t=((HD, seq), bf16), acc=((HD, QB), f32), heads_t=((HD, seq), f32), lse=((8, seq), f32),
         ostage=((n_b, tb // 2, LANES), bf16), parts=((n_b, tb // 2, LANES), bf16),
-        mix=((seqs, tb, heads * HD), bf16), branch=(block, bf16), landed_b=((n_u,) + own, bf16),
-        sums=((8, width), f32), hidden=(own, f32), nf_own=(own, bf16), nf=(block, bf16),
+        mix=((seqs, tb, heads * HD), bf16), branch=(block, bf16), landed=((n_u,) + own, bf16),
+        sums=((8, width), f32), totals=((8, width), f32), hat=(block, bf16), hidden=(own, f32), nf_own=(own, bf16), nf=(block, bf16),
         act=((seqs, tb, ff), bf16), dgu=((seqs, tb, 2 * ff), bf16), d_low=(block, bf16),
-        landed_d=((n_u,) + own, bf16), ghid=(own, f32), gb_own=(own, bf16), gb=(block, bf16),
+        ghid=(own, f32), gb_own=(own, bf16),
         f_low=(block, bf16), landed_f=((n_u,) + own, bf16),
         wd_buf=((n_z, 2, ff_pad, width), bf16), wd_pair=((n_z, ff_pad, width), bf16),
         wd_sum=((n_z, ff_pad, width), bf16), wd_land=((n_z, ff_pad, width), bf16),
@@ -1106,9 +1239,9 @@
         wo_buf=((n_z, 2, rows, width), bf16), wo_pair=((n_z, rows, width), bf16),
         wo_sum=((n_z, rows, width), bf16), wo_land=((n_z, rows, width), bf16),
         grad=((seq, LANES), bf16), grad_t=((LANES, seq), bf16), row_dot=((8, seq), f32),
-        dq_t=((HD, seq), f32), dk=((KB, LANES), f32), dv=((KB, LANES), f32),
+        dq_t=((HD, seq), f32), dk=((seq, LANES), f32), dv=((seq, LANES), f32),
         returned=((n_b, tb + tb // 2, LANES), bf16), raw=((seqs, tb, columns), bf16),
-        gin_low=(block, bf16), landed_g=((n_u,) + own, bf16), gv=((n_u, seqs, td, heads * HD), bf16),
+        gin_low=(block, bf16), gv=((n_u, seqs, td, heads * HD), bf16),
         wq_buf=((n_z, 2, n_u, rows, columns), bf16), wq_pair=((n_z, n_u, rows, columns), bf16),
         wq_sum=((n_z, n_u, rows, columns), bf16), wq_land=((n_z, n_u, rows, columns), bf16),
         wq_low=((n_u, rows, columns), bf16), sums_u=((n_u, 8, width), f32), sums_b=((n_b, 8, width), f32),
@@ -1127,28 +1260,16 @@
         ),
         name="layer",
     )(*inputs_of.values())
-    got = dict(zip(outs, results))
-    dwq = jnp.moveaxis(got["dwq"].astype(f32), 0, 1)
-    dqk = dwq[:, :, : heads * 2 * HD].reshape(rows, n_u, heads, 2, HD)
-    grad_w_query = dqk[:, :, :, 0].reshape(rows, width)
-    grad_w_key = dqk[:, :, :, 1].reshape(rows, width)
-    grad_w_value = dwq[:, :, heads * 2 * HD :].reshape(rows, width)
-    dwgu = jnp.moveaxis(got["dwgu"].astype(f32), 0, 1).reshape(rows, n_u, 2, n_b, ff_pad)[..., :ff_own]
-    grad_w_gate = dwgu[:, :, 0].reshape(rows, w_gate.shape[1])
-    grad_w_up = dwgu[:, :, 1].reshape(rows, w_gate.shape[1])
-    grad_w_down = got["dwd"][:ff_own]
-    gain_at = (u * n_b + b) * rows
-    sums = got["totals"]
-    grad_gain_attn = lax.dynamic_slice_in_dim(sums[3], gain_at, rows, 0)
-    grad_gain_ffn = lax.dynamic_slice_in_dim(sums[4], gain_at, rows, 0)
-    statistics = jnp.sqrt(jnp.sum(sums[:3], axis=1) / (seqs * seq * width))
-    return (
-        got["out"], got["gin"], got["gvf"], grad_w_query, grad_w_key, grad_w_value, got["dwo"],
-        grad_w_gate, grad_w_up, grad_w_down, grad_gain_attn, grad_gain_ffn, statistics,
-    )
-
-
-SEMAPHORES = 192
+    return pl.pallas_call(
+        functools.partial(hand_out_kernel, len(outs)),
+        out_shape=[jax.ShapeDtypeStruct(shape, dtype) for shape, dtype in outs.values()],
+        in_specs=[vmem] * len(outs),
+        out_specs=[vmem] * len(outs),
+        name="hand_out",
+    )(*results)
+
+
+SEMAPHORES = 224
 
 
 def fits_units(mesh):

time: 247 us -> 213 us (0.86)
  local copies, waits for them, and re-layouts: 21.1 us -> 0 us
  other arithmetic: 6.41 us -> 0 us
  Pallas kernels: 218 us -> 212 us
    pallas_call x1, Pallas kernels: 218 us -> 209 us  [local_units(): pl.pallas_call(functools.partial(layer_kernel, dims, names), out_shape=[j...]
    unnamed x39 -> x0, local copies, waits for them, and re-layouts: 7.75 us -> none
    another operation x10 -> x0, local copies, waits for them, and re-layouts: 4.67 us -> none  [the longest x1 1.04 us: local_units(): grad_w_gate = dwgu[:, :, 0].reshape(rows, w_gate.shape[1])]
    reshape x12 -> x0, local copies, waits for them, and re-layouts: 4.02 us -> none  [the longest x4 1.28 us: hidden_columns(): parted = pad_to(weight.reshape(rows, n_u, n_b, ff_own), 3, ff_pad)]
    pallas_call x0 -> x1, Pallas kernels: none -> 3.11 us  [local_units(): pl.pallas_call(functools.partial(hand_out_kernel, len(outs)), out_shape=[...]
where the time goes in v3:
time: 213 us
  Pallas kernels  212 us (100%)
    pallas_call x1, Pallas kernels, local_units(): pl.pallas_call(functools.partial(layer_kernel, dims, names), out_shape=[j...  209 us

profile of v3, /device:TPU:0, one launch (start us, length us, event | category | flops | bytes accessed | tf_op | source)
XLA Modules:
  0.0 212.6 jit_solution(12575470060518414859)
XLA Ops:
  0.6 208.7 %layer.1 = (bf16[2,64,1024]{2,1,0:T(8,128)(2,1)}, bf16[2,64,1024]{2,1,0:T(8,128)(2,1)}, bf16[2,64,1024]{2,1,0:T(8,128)(2,1)}, f32[32,1024]{1,0:T(8,128)}, f32[32...) custom-call(bf16[2,64,1024]{2,1,0:T(8,128)(2,1)} %refs_0_.1, ...), custom_call_target="tpu_custom_call" | custom-call | tf_op jit(solution)/shard_map/layer/pallas_call | solution.py:1251
  209.4 3.1 %hand_out.1 = (bf16[2,64,1024]{2,1,0:T(8,128)(2,1)}, bf16[2,64,1024]{2,1,0:T(8,128)(2,1)}, bf16[2,64,1024]{2,1,0:T(8,128)(2,1)}, f32[32,1024]{1,0:T(8,128)}, f32...) custom-call(bf16[2,64,1024]{2,1,0:T(8,128)(2,1)} %get-tuple-element., ...), custom_call_target="tpu_custom_call" | custom-call | tf_op jit(solution)/shard_map/hand_out/pallas_call | solution.py:1263

commit v4 on v3

--- a/solution.py
+++ b/solution.py
@@ -707,11 +707,13 @@
     mine = at_block(b, rows)
     ff = r.wdg.shape[0]
     ff_rows = ff // n_b
+    chunks = ff // 256
 
     def part(v):
         return at_block(v, td)
 
     share = heads * HD
+    ff_own = r.wd.shape[0]
     thirds = (r.wq_in, r.wk_in, r.wv_in)
     r.gains[...] = jnp.zeros_like(r.gains)
     for row, gain in enumerate((r.ga, r.gf)):
@@ -719,34 +721,37 @@
     lane_place = (b % (LANES // rows)) * rows
     r.gains[...] = pltpu.roll(r.gains[...], lane_place, 1)
     greet(u, b, n_u, n_b)
+    got_g = [net.push(r.gains, r.gbuf.at[b, u], v, b) for v in others]
     got_w = [
         net.push(w.at[:, at_block(v, share)], r.wq.at[u, mine, pl.ds(i * share, share)], v, b)
         for i, w in enumerate(thirds)
         for v in others
     ]
-    got_g = [net.push(r.gains, r.gbuf.at[b, u], v, b) for v in others]
     r.wo[mine] = r.wout[...]
     g_out = Gather(net, lambda c: r.wo.at[at_block(c, rows)], u, b)
-    got_x = [net.push(r.x, r.xg.at[:, slab], v, b) for v in others]
+    got_x = [[net.push(r.x.at[s], r.xg.at[s, slab], v, b) for v in others] for s in range(seqs)]
     for i, w in enumerate(thirds):
         r.wq[u, mine, i * share : (i + 1) * share] = w[:, at_block(u, share)]
-    r.gbuf[b, u] = r.gains[...]
     r.xg[:, slab] = r.x[...]
     r.vfg[:, slab] = r.vf[:, :, at_block(u, share)]
     r.gog[:, slab] = r.go[...]
+    r.gbuf[b, u] = r.gains[...]
+    arrive(got_g)
+    got_g = [net.push(r.gbuf.at[b], r.gbuf.at[b], u, b ^ off) for off in range(1, n_b)]
     arrive(got_w)
     g_qk = Gather(net, lambda c: r.wq.at[:, at_block(c, rows), pl.ds(0, 2 * share)], u, b)
     g_v = Gather(net, lambda c: r.wq.at[:, at_block(c, rows), pl.ds(2 * share, share)], u, b)
-    arrive(got_g)
-    got_g = [net.push(r.gbuf.at[b], r.gbuf.at[b], u, b ^ off) for off in range(1, n_b)]
     got_v = [net.push(r.vf.at[:, :, at_block(v, share)], r.vfg.at[:, slab], v, b) for v in others]
-    ff_own = r.wd.shape[0]
-    for i, w in enumerate((r.wg_in, r.wu_in)):
-        wide_rows = widen(w[...], ff_own, ff_rows)
-        for v in range(n_u):
-            r.wgu[v, :, i * ff : (i + 1) * ff] = wide_rows[:, v * ff : (v + 1) * ff]
-    r.wg[u, mine] = r.wgu[u]
-    got_o = [net.push(r.wgu.at[v], r.wg.at[u, mine], v, b) for v in others]
+    seq_of_unit = b // heads
+    for s in range(seqs):
+        cut = jnp.sum((1 - r.segments[s : s + 1, :]).astype(f32), axis=1, keepdims=True)
+        r.cosr[s], r.sinr[s] = rope_rows(b * tb, cut, tb)
+
+        @pl.when(seq_of_unit == s)
+        def _():
+            key_place = lane_of((8, seq)).astype(f32)
+            r.low[...] = jnp.where(key_place >= cut, cut, 0.0).astype(jnp.int32)
+
     arrive(got_g)
     per_tile = LANES // rows
     for tile in range(n_u * n_b // per_tile):
@@ -755,28 +760,19 @@
             term = r.gbuf[index % n_b, index // n_b]
             total = term if total is None else total + term
         r.gain[:, tile * LANES : (tile + 1) * LANES] = total
-    seq_of_unit = b // heads
     for s in range(seqs):
-        cut = jnp.sum((1 - r.segments[s : s + 1, :]).astype(f32), axis=1, keepdims=True)
-        r.cosr[s], r.sinr[s] = rope_rows(b * tb, cut, tb)
-
-        @pl.when(seq_of_unit == s)
-        def _():
-            key_place = lane_of((8, seq)).astype(f32)
-            r.low[...] = jnp.where(key_place >= cut, cut, 0.0).astype(jnp.int32)
-
-    arrive(got_x)
-
-    def norm(step, carry):
-        s, place = step // 2, at_block(step % 2, tb // 2)
-        values = r.xg[s, place].astype(f32)
-        factor = lax.rsqrt(jnp.mean(values * values, axis=-1, keepdims=True) + epsilon)
-        hat = values * factor
-        r.hat[s, place] = hat.astype(bf16)
-        r.normed[s, place] = (hat * r.gain[0:1, :]).astype(bf16)
-        return carry
-
-    lax.fori_loop(0, 2 * seqs, norm, 0)
+        arrive(got_x[s])
+
+        def norm(step, carry, s=s):
+            place = at_block(step, tb // 2)
+            values = r.xg[s, place].astype(f32)
+            factor = lax.rsqrt(jnp.mean(values * values, axis=-1, keepdims=True) + epsilon)
+            hat = values * factor
+            r.hat[s, place] = hat.astype(bf16)
+            r.normed[s, place] = (hat * r.gain[0:1, :]).astype(bf16)
+            return carry
+
+        lax.fori_loop(0, 2, norm, 0)
     got_go = [net.push(r.go, r.gog.at[:, slab], v, b) for v in others]
     g_qk.forward()
     g_qk.relay()
@@ -815,6 +811,14 @@
                 r.stage[unit + 1, tb:] = pack_rows(swap_halves(value)).astype(bf16)
         for unit in range(s * heads, (s + 1) * heads):
             x_v.give(unit)
+    for i, w in enumerate((r.wg_in, r.wu_in)):
+        wide_rows = widen(w[...], ff_own, ff_rows)
+        for v in range(n_u):
+            for n in range(chunks):
+                at = (2 * n + i) * 256
+                r.wgu[v, :, at : at + 256] = wide_rows[:, v * ff + n * 256 : v * ff + (n + 1) * 256]
+    r.wg[u, mine] = r.wgu[u]
+    got_o = [net.push(r.wgu.at[v], r.wg.at[u, mine], v, b) for v in others]
     r.units[b] = r.stage[b]
     for slot in range(n_b):
         r.wdg[slot * ff_rows + ff_own : (slot + 1) * ff_rows] = jnp.zeros((ff_rows - ff_own, width), bf16)
@@ -875,7 +879,10 @@
     g_down.forward()
     arrive(got_o)
     x_out.take()
-    g_gate = Gather(net, lambda c: r.wg.at[:, at_block(c, rows)], u, b)
+    def gate_slot(n):
+        return lambda c: r.wg.at[:, at_block(c, rows), pl.ds(n * 512, 512)]
+
+    g_gate = [Gather(net, gate_slot(n), u, b) for n in range(chunks)]
 
     half = tb // 2
     got_s = []
@@ -907,37 +914,34 @@
         r.sums[1:2] = r.sums[1:2] + jnp.sum(total * total, axis=0, keepdims=True)
     arrive(got_go)
     g_down.finish()
-    g_gate.forward()
-    g_gate.relay()
-    g_gate.finish()
-
-    def hidden_units(s):
-        left = r.nf[s]
-        grad = r.gog[s]
-
-        def some(n, carry):
-            span, up_span = at_block(n, 256), at_block(n + ff // 256, 256)
-            gate = dot(left, r.wg[:, :, span].reshape(width, 256))
-            up = dot(left, r.wg[:, :, up_span].reshape(width, 256))
-            grad_act = dot_nt(grad, r.wdg[span])
-            sig = 1.0 / (1.0 + jnp.exp(-gate))
-            silu = gate * sig
-            r.act[s, :, span] = (silu * up).astype(bf16)
-            r.dgu[s, :, span] = (grad_act * up * sig * (1.0 + gate * (1.0 - sig))).astype(bf16)
-            r.dgu[s, :, up_span] = (grad_act * silu).astype(bf16)
+    for n in range(2):
+        g_gate[n].forward()
+        g_gate[n].relay()
+
+    def hidden_units(n, s):
+        span, at = slice(n * 256, (n + 1) * 256), n * 512
+        gate = dot(r.nf[s], r.wg[:, :, at : at + 256].reshape(width, 256))
+        up = dot(r.nf[s], r.wg[:, :, at + 256 : at + 512].reshape(width, 256))
+        grad_act = dot_nt(r.gog[s], r.wdg[span])
+        sig = 1.0 / (1.0 + jnp.exp(-gate))
+        silu = gate * sig
+        r.act[s, :, span] = (silu * up).astype(bf16)
+        r.dgu[s, :, at : at + 256] = (grad_act * up * sig * (1.0 + gate * (1.0 - sig))).astype(bf16)
+        r.dgu[s, :, at + 256 : at + 512] = (grad_act * silu).astype(bf16)
+
+    def grad_gate(n):
+        right = r.dgu[:, :, n * 512 : (n + 1) * 512].reshape(tokens, 512)
+
+        def some(v, carry):
+            found = dot(r.nft[at_block(v, 256)], right)
+            r.wg_buf[n, :, :, v] = found.astype(bf16).reshape(n_z, 2, rows, 512)
             return carry
 
-        lax.fori_loop(0, ff // 256, some, 0)
-
-    got_d = []
-    for s in range(seqs):
-        arrive(got_n[s])
-        hidden_units(s)
-        left = r.dgu[s]
-        for v in range(n_u):
-            r.d_low[s, :, v * 256 : (v + 1) * 256] = dot_nt(left, r.wg[v]).astype(bf16)
-        got_d.append([net.push(r.d_low.at[s, part(v)], r.landed.at[u, s], v, b) for v in others])
-        r.landed[u, s] = r.d_low[s, slab]
+        lax.fori_loop(0, n_u, some, 0)
+        parts = r.wg_buf.at[n]
+        return Scatter(
+            net, u, b, lambda z, c: parts.at[z, c], r.wg_pair.at[n], r.wg_sum.at[n], r.wg_land.at[n]
+        )
 
     def grad_down(n):
         half_units = ff // 2
@@ -947,10 +951,29 @@
             n_z // 2, 2, ff_rows, width
         )
 
-    def grad_gate(v):
-        left = r.nf[:, :, v * 256 : (v + 1) * 256].reshape(tokens, 256)
-        found = dot_tn(left, r.dgu[...].reshape(tokens, 2 * ff))
-        r.wg_buf[:, :, v] = found.astype(bf16).reshape(n_z, 2, rows, 2 * ff)
+    got_d, s_gate = [], []
+    for n in range(chunks):
+        g_gate[n].finish()
+        for s in range(seqs):
+            if n == 0:
+                arrive(got_n[s])
+            hidden_units(n, s)
+            if n == 0:
+                r.nft[:, s * tb : (s + 1) * tb] = jnp.transpose(r.nf[s])
+        if n + 2 < chunks:
+            g_gate[n + 2].forward()
+            g_gate[n + 2].relay()
+        if n > 0:
+            s_gate[n - 1].middle()
+        if n + 1 < chunks:
+            s_gate.append(grad_gate(n))
+    for s in range(seqs):
+        left = r.dgu[s]
+        for v in range(n_u):
+            r.d_low[s, :, v * 256 : (v + 1) * 256] = dot_nt(left, r.wg[v]).astype(bf16)
+        got_d.append([net.push(r.d_low.at[s, part(v)], r.landed.at[u, s], v, b) for v in others])
+        r.landed[u, s] = r.d_low[s, slab]
+    s_gate.append(grad_gate(chunks - 1))
 
     got_b = []
 
@@ -969,21 +992,18 @@
         r.xg[s, slab] = r.gb_own[s]
         r.sums[4:5] = r.sums[4:5] + jnp.sum(grad_normed * hat, axis=0, keepdims=True)
 
-    for n in range(2):
-        grad_down(n)
+    norm_back(0)
+    grad_down(0)
+    norm_back(1)
+    grad_down(1)
+    s_gate[0].merge()
+    s_gate[chunks - 1].middle()
     ff_cut = pl.ds(0, ff_own)
     s_down = Scatter(
         net, u, b, lambda z, c: r.wd_buf.at[z, c, ff_cut], r.wd_pair.at[:, ff_cut],
         r.wd_sum.at[:, ff_cut], r.wd_land.at[:, ff_cut],
     )
-    norm_back(0)
-    grad_gate(0)
-    s_down.middle()
-    norm_back(1)
-    for v in range(1, n_u):
-        grad_gate(v)
-    s_down.merge()
-    s_gate = Scatter(net, u, b, lambda z, c: r.wg_buf.at[z, c], r.wg_pair, r.wg_sum, r.wg_land)
+    s_gate[1].merge()
     x_grad = Exchange(net, r.ostage2, r.grads, u, b, n_b)
     for s in range(seqs):
         arrive(got_b[s])
@@ -996,18 +1016,22 @@
             x_grad.give(unit + 1)
     r.grads[b] = r.ostage2[b]
 
+    for copies in got_s:
+        net.sent(copies)
+
     def forward(s, carry):
-        r.f_low[s] = dot(r.act[s], r.wdg[...]).astype(bf16)
+        r.branch[s] = dot(r.act[s], r.wdg[...]).astype(bf16)
         return carry
 
     lax.fori_loop(0, seqs, forward, 0)
-    got_f = [net.push(r.f_low.at[:, part(v)], r.landed_f.at[u], v, b) for v in others]
-    r.landed_f[u] = r.f_low[:, slab]
+    got_f = [net.push(r.branch.at[:, part(v)], r.landed_f.at[u], v, b) for v in others]
+    r.landed_f[u] = r.branch[:, slab]
     found = dot_tn(r.mix[...].reshape(tokens, share), r.xg[...].reshape(tokens, width))
     r.wo_buf[...] = found.astype(bf16).reshape(n_z, 2, rows, width)
     s_out = Scatter(net, u, b, lambda z, c: r.wo_buf.at[z, c], r.wo_pair, r.wo_sum, r.wo_land)
     x_grad.take()
-    s_gate.middle()
+    s_gate[2].merge()
+    s_out.middle()
 
     def more(block, carry):
         place = at_block(block, tb)
@@ -1044,6 +1068,7 @@
         r.stage[block, tb:] = pack_rows(r.dv[place]).astype(bf16)
         x_back.give(block)
 
+    s_out.merge()
     for buffer in (r.dq_t, r.dk, r.dv):
         buffer[...] = jnp.zeros_like(buffer)
     ratio = QB // KB
@@ -1076,15 +1101,13 @@
 
         lax.fori_loop(0, n_b, outer, 0)
 
+    s_down.middle()
     r.returned[b] = r.stage[b]
-    s_gate.merge()
-    s_out.middle()
     arrive(got_f)
     for s in range(seqs):
         total = r.hidden[s] + sum(r.landed_f[v, s].astype(f32) for v in range(n_u))
         r.out[s] = total.astype(bf16)
         r.sums[2:3] = r.sums[2:3] + jnp.sum(total * total, axis=0, keepdims=True)
-    s_down.finish(r.gwd)
     x_back.take()
 
     for s in range(seqs):
@@ -1111,29 +1134,34 @@
         found = dot_tn(left, r.raw[...].reshape(tokens, columns))
         r.wq_buf[:, :, v] = found.astype(bf16).reshape(n_z, 2, rows, columns)
     s_qkv = Scatter(net, u, b, lambda z, c: r.wq_buf.at[z, c], r.wq_pair, r.wq_sum, r.wq_land)
-    s_out.merge()
-
+    s_down.merge()
+
+    for copies in got_d:
+        net.sent(copies)
     got_g = []
     for s in range(seqs):
         left = r.raw[s]
         for v in range(n_u):
             lanes = slice(v * 256, (v + 1) * 256)
             found = dot_nt(left, r.wq[v])
-            r.gin_low[s, :, lanes] = found.astype(bf16)
+            r.d_low[s, :, lanes] = found.astype(bf16)
             term = jnp.sum(found * r.hat[s, :, lanes].astype(f32), axis=0, keepdims=True)
             r.sums[3:4, lanes] = r.sums[3:4, lanes] + term
-        got_g.append([net.push(r.gin_low.at[s, part(v)], r.landed.at[u, s], v, b) for v in others])
-        r.landed[u, s] = r.gin_low[s, slab]
+        got_g.append([net.push(r.d_low.at[s, part(v)], r.landed.at[u, s], v, b) for v in others])
+        r.landed[u, s] = r.d_low[s, slab]
     got_s = [net.push(r.sums, r.sums_u.at[u], v, b) for v in others]
     r.sums_u[u] = r.sums[...]
     s_qkv.middle()
     got_v = [net.push(r.raw.at[:, part(v), pl.ds(2 * share, share)], r.gv.at[u], v, b) for v in others]
     r.gv[u] = r.raw[:, slab, 2 * share :]
-    s_gate.finish(r.wg_low)
-    got_c = [net.push(r.wg_low.at[v], r.dwgu.at[u], v, b) for v in others]
-    r.dwgu[u] = r.wg_low[u]
+    got_c = []
+    for n in range(chunks):
+        s_gate[n].finish(r.wg_low.at[n])
+        got_c += [net.push(r.wg_low.at[n, v], r.dwgu.at[n, u], v, b) for v in others]
+        r.dwgu[n, u] = r.wg_low[n, u]
     s_qkv.merge()
     s_out.finish(r.gwo)
+    s_down.finish(r.gwd)
     arrive(got_s)
     r.sums_b[b] = sum(r.sums_u[v] for v in range(n_u))
     got_s = [net.push(r.sums_b.at[b], r.sums_b.at[b], u, b ^ off) for off in range(1, n_b)]
@@ -1166,11 +1194,12 @@
     r.dwq[u] = r.wq_low[u]
     arrive(got_c)
     for i, to in enumerate((r.gwg, r.gwu)):
-        pieces = [
-            r.dwgu[v, :, i * ff + j * ff_rows : i * ff + j * ff_rows + ff_own].astype(f32)
-            for v in range(n_u)
-            for j in range(n_b)
-        ]
+        pieces = []
+        for v in range(n_u):
+            row = jnp.concatenate(
+                [r.dwgu[n, v, :, i * 256 : (i + 1) * 256] for n in range(chunks)], axis=1
+            ).astype(f32)
+            pieces += [row[:, j * ff_rows : j * ff_rows + ff_own] for j in range(n_b)]
         to[...] = jnp.concatenate(pieces, axis=1)
     arrive(got)
     for i, to in enumerate((r.gwq, r.gwk, r.gwv)):
@@ -1199,6 +1228,7 @@
     ff_own = w_down.shape[0]
     ff_pad = -(-ff_own // 32) * 32
     ff = ff_pad * n_b
+    chunks = ff // 256
     dims = (n_u, n_b, seqs, td, rows, heads)
 
     columns = 3 * heads * HD
@@ -1216,7 +1246,7 @@
     scratch = dict(
         gains=((8, LANES), f32), wgu=((n_u, rows, 2 * ff), bf16), cosr=((seqs, tb, LANES), f32),
         sinr=((seqs, tb, LANES), f32), low=((8, seq), jnp.int32),
-        dwq=((n_u, rows, columns), bf16), dwgu=((n_u, rows, 2 * ff), bf16),
+        dwq=((n_u, rows, columns), bf16), dwgu=((chunks, n_u, rows, 512), bf16), nft=((width, seqs * tb), bf16),
         xg=(block, bf16), vfg=((seqs, tb, heads * HD), bf16), gbuf=((n_b, n_u, 8, LANES), f32),
         gain=((8, width), f32), normed=(block, bf16), wq=((n_u, n_b * rows, columns), bf16),
         gog=(block, bf16), wg=((n_u, n_b * rows, 2 * ff), bf16), wdg=((ff, width), bf16),
@@ -1229,19 +1259,19 @@
         sums=((8, width), f32), totals=((8, width), f32), hat=(block, bf16), hidden=(own, f32), nf_own=(own, bf16), nf=(block, bf16),
         act=((seqs, tb, ff), bf16), dgu=((seqs, tb, 2 * ff), bf16), d_low=(block, bf16),
         ghid=(own, f32), gb_own=(own, bf16),
-        f_low=(block, bf16), landed_f=((n_u,) + own, bf16),
+        landed_f=((n_u,) + own, bf16),
         wd_buf=((n_z, 2, ff_pad, width), bf16), wd_pair=((n_z, ff_pad, width), bf16),
         wd_sum=((n_z, ff_pad, width), bf16), wd_land=((n_z, ff_pad, width), bf16),
-        wg_buf=((n_z, 2, n_u, rows, 2 * ff), bf16), wg_pair=((n_z, n_u, rows, 2 * ff), bf16),
-        wg_sum=((n_z, n_u, rows, 2 * ff), bf16), wg_land=((n_z, n_u, rows, 2 * ff), bf16),
-        wg_low=((n_u, rows, 2 * ff), bf16),
+        wg_buf=((chunks, n_z, 2, n_u, rows, 512), bf16), wg_pair=((chunks, n_z, n_u, rows, 512), bf16),
+        wg_sum=((chunks, n_z, n_u, rows, 512), bf16), wg_land=((chunks, n_z, n_u, rows, 512), bf16),
+        wg_low=((chunks, n_u, rows, 512), bf16),
         ostage2=((n_b, tb // 2, LANES), bf16), grads=((n_b, tb // 2, LANES), bf16),
         wo_buf=((n_z, 2, rows, width), bf16), wo_pair=((n_z, rows, width), bf16),
         wo_sum=((n_z, rows, width), bf16), wo_land=((n_z, rows, width), bf16),
         grad=((seq, LANES), bf16), grad_t=((LANES, seq), bf16), row_dot=((8, seq), f32),
         dq_t=((HD, seq), f32), dk=((seq, LANES), f32), dv=((seq, LANES), f32),
         returned=((n_b, tb + tb // 2, LANES), bf16), raw=((seqs, tb, columns), bf16),
-        gin_low=(block, bf16), gv=((n_u, seqs, td, heads * HD), bf16),
+        gv=((n_u, seqs, td, heads * HD), bf16),
         wq_buf=((n_z, 2, n_u, rows, columns), bf16), wq_pair=((n_z, n_u, rows, columns), bf16),
         wq_sum=((n_z, n_u, rows, columns), bf16), wq_land=((n_z, n_u, rows, columns), bf16),
         wq_low=((n_u, rows, columns), bf16), sums_u=((n_u, 8, width), f32), sums_b=((n_b, 8, width), f32),
@@ -1269,7 +1299,7 @@
     )(*results)
 
 
-SEMAPHORES = 224
+SEMAPHORES = 288
 
 
 def fits_units(mesh):

time: 213 us -> 203 us (0.953)
  Pallas kernels: 212 us -> 202 us
    pallas_call x1, Pallas kernels: 209 us -> 199 us  [local_units(): pl.pallas_call(functools.partial(layer_kernel, dims, names), out_shape=[j...]
where the time goes in v4:
time: 203 us
  Pallas kernels  202 us (100%)
    pallas_call x1, Pallas kernels, local_units(): pl.pallas_call(functools.partial(layer_kernel, dims, names), out_shape=[j...  199 us

profile of v4, /device:TPU:0, one launch (start us, length us, event | category | flops | bytes accessed | tf_op | source)
XLA Modules:
  0.0 202.6 jit_solution(5717477535853245556)
XLA Ops:
  0.6 198.6 %layer.1 = (bf16[2,64,1024]{2,1,0:T(8,128)(2,1)}, bf16[2,64,1024]{2,1,0:T(8,128)(2,1)}, bf16[2,64,1024]{2,1,0:T(8,128)(2,1)}, f32[32,1024]{1,0:T(8,128)}, f32[32...) custom-call(bf16[2,64,1024]{2,1,0:T(8,128)(2,1)} %refs_0_.1, ...), custom_call_target="tpu_custom_call" | custom-call | tf_op jit(solution)/shard_map/layer/pallas_call | solution.py:1281
  199.3 3.1 %hand_out.1 = (bf16[2,64,1024]{2,1,0:T(8,128)(2,1)}, bf16[2,64,1024]{2,1,0:T(8,128)(2,1)}, bf16[2,64,1024]{2,1,0:T(8,128)(2,1)}, f32[32,1024]{1,0:T(8,128)}, f32...) custom-call(bf16[2,64,1024]{2,1,0:T(8,128)(2,1)} %get-tuple-element., ...), custom_call_target="tpu_custom_call" | custom-call | tf_op jit(solution)/shard_map/hand_out/pallas_call | solution.py:1293

commit v5 on v4

--- a/solution.py
+++ b/solution.py
@@ -652,19 +652,6 @@
             total[...] = (total[...].astype(f32) + self.landed[2].astype(f32)).astype(total.dtype)
 
 
-def fill_units(units, tb, store):
-    def one(block, carry):
-        low = lane_of((tb, LANES)) < HD
-        tile = units[block, 0:tb].astype(f32)
-        query = jnp.where(low, tile * HD ** (-0.5), 0.0)
-        key = jnp.where(low, swap_halves(tile), 0.0)
-        value = jnp.where(low, unpack_rows(units[block, tb:].astype(f32)), 0.0)
-        store(block, query, key, value)
-        return carry
-
-    lax.fori_loop(0, units.shape[0], one, 0)
-
-
 def allowed_block(first_key, first_query, low_row, keys=KB, queries=QB):
     key_place = first_key + lax.broadcasted_iota(jnp.int32, (keys, queries), 0)
     query_place = first_query + lax.broadcasted_iota(jnp.int32, (keys, queries), 1)
@@ -702,7 +689,7 @@
     width = r.x.shape[2]
     u, b = here()
     net = Net(r.send_sems, r.recv_sems)
-    others = [u ^ off for off in range(1, n_u)]
+    others = [u ^ off for off in range(n_u - 1, 0, -1)]
     slab = at_block(u, td)
     mine = at_block(b, rows)
     ff = r.wdg.shape[0]
@@ -826,22 +813,39 @@
     g_out.forward()
     g_out.relay()
     x_qk.take()
-    x_v.take()
     g_out.finish()
 
-    g_down = Gather(net, lambda c: r.wdg.at[pl.ds(pl.multiple_of(c * ff_rows, ff_rows), ff_own)], u, b)
-    x_out = Exchange(net, r.ostage, r.parts, u, b, n_b)
-
-    def store(block, query, key, value):
+
+    def fill_keys(block, carry):
         place = at_block(block, tb)
+        low = lane_of((tb, LANES)) < HD
+        tile = r.units[block, 0:tb].astype(f32)
+        query = jnp.where(low, tile * HD ** (-0.5), 0.0)
+        key = jnp.where(low, swap_halves(tile), 0.0)
         r.keys[place] = key.astype(bf16)
         r.key_t[:, place] = jnp.transpose(key)[:HD].astype(bf16)
         r.query[place] = query.astype(bf16)
         r.query_t[:, place] = jnp.transpose(query).astype(bf16)
+        return carry
+
+    def fill_values(block, carry):
+        place = at_block(block, tb)
+        low = lane_of((tb, LANES)) < HD
+        value = jnp.where(low, unpack_rows(r.units[block, tb:].astype(f32)), 0.0)
         r.value[place] = value.astype(bf16)
         r.value_t[:, place] = jnp.transpose(value)[:HD].astype(bf16)
-
-    fill_units(r.units, tb, store)
+        return carry
+
+    lax.fori_loop(0, n_b, fill_keys, 0)
+    x_v.take()
+    arrive(got_o)
+
+    def gate_slot(n):
+        return lambda c: r.wg.at[:, at_block(c, rows), pl.ds(n * 512, 512)]
+
+    g_gate = [Gather(net, gate_slot(0), u, b)]
+    x_out = Exchange(net, r.ostage, r.parts, u, b, n_b)
+    lax.fori_loop(0, n_b, fill_values, 0)
 
     def attend(step, carry):
         qb = seq // QB - 1 - step
@@ -852,9 +856,9 @@
 
         def inner(kb, state):
             best, total = state
-            k_at = at_block(kb, KB)
+            k_at = at_block(kb, QB)
             scores = dot(r.keys[k_at], query)
-            scores = jnp.where(allowed_block(kb * KB, qb * QB, low_row), scores, neg_big)
+            scores = jnp.where(allowed_block(kb * QB, qb * QB, low_row, QB, QB), scores, neg_big)
             new_best = jnp.maximum(best, jnp.max(scores, axis=0, keepdims=True))
             weights = jnp.exp(scores - new_best)
             rescale = jnp.exp(best - new_best)
@@ -863,7 +867,7 @@
             return new_best, total
 
         start = (jnp.full((1, QB), neg_big, f32), jnp.zeros((1, QB), f32))
-        best, total = lax.fori_loop(0, (qb + 1) * (QB // KB), inner, start)
+        best, total = lax.fori_loop(0, qb + 1, inner, start)
         out = r.acc[...] / total
         r.heads_t[:, q_at] = out
         r.lse[:, q_at] = jnp.broadcast_to(best + jnp.log(total), (8, QB))
@@ -876,13 +880,10 @@
 
     lax.fori_loop(0, seq // QB, attend, 0)
     r.parts[b] = r.ostage[b]
-    g_down.forward()
-    arrive(got_o)
+    g_gate[0].forward()
     x_out.take()
-    def gate_slot(n):
-        return lambda c: r.wg.at[:, at_block(c, rows), pl.ds(n * 512, 512)]
-
-    g_gate = [Gather(net, gate_slot(n), u, b) for n in range(chunks)]
+    g_down = Gather(net, lambda c: r.wdg.at[pl.ds(pl.multiple_of(c * ff_rows, ff_rows), ff_own)], u, b)
+    g_gate += [Gather(net, gate_slot(n), u, b) for n in range(1, chunks)]
 
     half = tb // 2
     got_s = []
@@ -897,7 +898,8 @@
         r.branch[s] = dot(r.mix[s], r.wo[...]).astype(bf16)
         got_s.append([net.push(r.branch.at[s, part(v)], r.landed.at[u, s], v, b) for v in others])
         r.landed[u, s] = r.branch[s, slab]
-    g_down.relay()
+    g_gate[0].relay()
+    g_down.forward()
     r.sums[...] = jnp.zeros_like(r.sums)
     got_n = []
     for s in range(seqs):
@@ -913,10 +915,9 @@
         r.sums[0:1] = r.sums[0:1] + jnp.sum(own * own, axis=0, keepdims=True)
         r.sums[1:2] = r.sums[1:2] + jnp.sum(total * total, axis=0, keepdims=True)
     arrive(got_go)
+    g_down.relay()
     g_down.finish()
-    for n in range(2):
-        g_gate[n].forward()
-        g_gate[n].relay()
+    g_gate[1].forward()
 
     def hidden_units(n, s):
         span, at = slice(n * 256, (n + 1) * 256), n * 512
@@ -960,9 +961,10 @@
             hidden_units(n, s)
             if n == 0:
                 r.nft[:, s * tb : (s + 1) * tb] = jnp.transpose(r.nf[s])
+            if s == 0 and n + 1 < chunks:
+                g_gate[n + 1].relay()
         if n + 2 < chunks:
             g_gate[n + 2].forward()
-            g_gate[n + 2].relay()
         if n > 0:
             s_gate[n - 1].middle()
         if n + 1 < chunks:

time: 203 us -> 200 us (0.985)
  Pallas kernels: 202 us -> 199 us
    pallas_call x1, Pallas kernels: 199 us -> 196 us  [local_units(): pl.pallas_call(functools.partial(layer_kernel, dims, names), out_shape=[j...]
where the time goes in v5:
time: 200 us
  Pallas kernels  199 us (100%)
    pallas_call x1, Pallas kernels, local_units(): pl.pallas_call(functools.partial(layer_kernel, dims, names), out_shape=[j...  196 us

profile of v5, /device:TPU:0, one launch (start us, length us, event | category | flops | bytes accessed | tf_op | source)
XLA Modules:
  0.0 199.6 jit_solution(3224198104040992154)
XLA Ops:
  0.6 195.7 %layer.1 = (bf16[2,64,1024]{2,1,0:T(8,128)(2,1)}, bf16[2,64,1024]{2,1,0:T(8,128)(2,1)}, bf16[2,64,1024]{2,1,0:T(8,128)(2,1)}, f32[32,1024]{1,0:T(8,128)}, f32[32...) custom-call(bf16[2,64,1024]{2,1,0:T(8,128)(2,1)} %refs_0_.1, ...), custom_call_target="tpu_custom_call" | custom-call | tf_op jit(solution)/shard_map/layer/pallas_call | solution.py:1283
  196.4 3.1 %hand_out.1 = (bf16[2,64,1024]{2,1,0:T(8,128)(2,1)}, bf16[2,64,1024]{2,1,0:T(8,128)(2,1)}, bf16[2,64,1024]{2,1,0:T(8,128)(2,1)}, f32[32,1024]{1,0:T(8,128)}, f32...) custom-call(bf16[2,64,1024]{2,1,0:T(8,128)(2,1)} %get-tuple-element., ...), custom_call_target="tpu_custom_call" | custom-call | tf_op jit(solution)/shard_map/hand_out/pallas_call | solution.py:1295

commit v6 on v5

--- a/solution.py
+++ b/solution.py
@@ -917,7 +917,6 @@
     arrive(got_go)
     g_down.relay()
     g_down.finish()
-    g_gate[1].forward()
 
     def hidden_units(n, s):
         span, at = slice(n * 256, (n + 1) * 256), n * 512
@@ -962,9 +961,9 @@
             if n == 0:
                 r.nft[:, s * tb : (s + 1) * tb] = jnp.transpose(r.nf[s])
             if s == 0 and n + 1 < chunks:
-                g_gate[n + 1].relay()
-        if n + 2 < chunks:
-            g_gate[n + 2].forward()
+                g_gate[n + 1].forward()
+        if n + 1 < chunks:
+            g_gate[n + 1].relay()
         if n > 0:
             s_gate[n - 1].middle()
         if n + 1 < chunks:

time: 200 us -> 199 us (level)
  no operation moved by 1% of the time
where the time goes in v6:
time: 199 us
  Pallas kernels  198 us (99%)
    pallas_call x1, Pallas kernels, local_units(): pl.pallas_call(functools.partial(layer_kernel, dims, names), out_shape=[j...  195 us

profile of v6, /device:TPU:0, one launch (start us, length us, event | category | flops | bytes accessed | tf_op | source)
XLA Modules:
  0.0 198.8 jit_solution(11723457833109803507)
XLA Ops:
  0.6 194.9 %layer.1 = (bf16[2,64,1024]{2,1,0:T(8,128)(2,1)}, bf16[2,64,1024]{2,1,0:T(8,128)(2,1)}, bf16[2,64,1024]{2,1,0:T(8,128)(2,1)}, f32[32,1024]{1,0:T(8,128)}, f32[32...) custom-call(bf16[2,64,1024]{2,1,0:T(8,128)(2,1)} %refs_0_.1, ...), custom_call_target="tpu_custom_call" | custom-call | tf_op jit(solution)/shard_map/layer/pallas_call | solution.py:1282
  195.6 3.1 %hand_out.1 = (bf16[2,64,1024]{2,1,0:T(8,128)(2,1)}, bf16[2,64,1024]{2,1,0:T(8,128)(2,1)}, bf16[2,64,1024]{2,1,0:T(8,128)(2,1)}, f32[32,1024]{1,0:T(8,128)}, f32...) custom-call(bf16[2,64,1024]{2,1,0:T(8,128)(2,1)} %get-tuple-element., ...), custom_call_target="tpu_custom_call" | custom-call | tf_op jit(solution)/shard_map/hand_out/pallas_call | solution.py:1294
